TPU v7x, 128 devices: a whole 4x4x4 slice. The times are simulated.
128 devices in a mesh: run: 2 (over core), row: 8 (over z_lo, x), col: 8 (over y, z_hi).
Axes of the slice: x: 4, y: 4, z: 4 (z_hi: 2, z_lo: 2; z = z_hi * 2 + z_lo), core: 2. Of those that a mesh axis runs over, the one named last changes fastest.
Arguments:
- init_field: float32 [96, 512, 1024], P('run', 'row', 'col'), may hold values from -6 to 6
- conduct: float32 [512, 1024], P('row', 'col'), may hold values from 0.5 to 2
- nonlin: float32 [96], P('run'), may hold values from 0.1 to 1
- counts: int32 [96], P('run'), may hold values from 1 to 8
- descriptors: bfloat16 [96, 256], replicated, may hold values from -6 to 6
- time_code: bfloat16 [8, 256], replicated, may hold values from -6 to 6
- w_in: bfloat16 [256, 512], replicated, may hold values from -0.375 to 0.375
- bias_in: float32 [512], replicated, may hold values from -6 to 6
- w_out: bfloat16 [512, 512], replicated, may hold values from -0.25 to 0.25
- decoder: bfloat16 [512, 512, 1024], P(None, ('row', 'col')), may hold values from -0.22 to 0.22
Outputs:
- final_field: float32 [96, 512, 1024], P('run', 'row', 'col')
- new_w_in: float32 [256, 512], replicated
- new_bias: float32 [512], replicated
- new_w_out: float32 [512, 512], replicated
- mean_loss: float32 [], replicated
All inputs are finite; a program needn't handle non-finite values.
Results may differ from a plain program's by a relative error of at most 0.0017.
Values may be sent and summed in bfloat16 or wider, within the bound.
A program may use at most 128 MiB of HBM per device.

v0:
```python
import jax
import jax.numpy as jnp
from jax import lax
from jax.sharding import PartitionSpec as P

HALO = 4


time_step = 0.12
learn_rate = 0.5


def extended(block, sides, width):
    for axis, dim in sides:
        count = lax.axis_size(axis)
        forward = [(i, i + 1) for i in range(count - 1)]
        backward = [(target, source) for source, target in forward]
        low = lax.ppermute(
            lax.slice_in_dim(block, block.shape[dim] - width, None, axis=dim), axis, forward
        )
        high = lax.ppermute(lax.slice_in_dim(block, 0, width, axis=dim), axis, backward)
        block = jnp.concatenate([low, block, high], axis=dim)
    return block


def split_up(array, dim, peers):
    dims = array.shape
    blocks = array.reshape(*dims[:dim], peers, dims[dim] // peers, *dims[dim + 1 :])
    return jnp.moveaxis(blocks, dim, 0)


def sum_at_owner(array, axis, dim):
    blocks = split_up(array, dim, lax.axis_size(axis))
    arrived = lax.all_to_all(blocks, axis, split_axis=0, concat_axis=0, tiled=True)
    return arrived.sum(axis=0)


def filled_up(lines, peers):
    spare = -lines.shape[0] % peers
    if not spare:
        return lines
    return jnp.concatenate([lines, jnp.zeros((spare, *lines.shape[1:]), lines.dtype)])


def joined_along(blocks, dim):
    dims = list(blocks.shape[1:])
    dims[dim] *= blocks.shape[0]
    return jnp.moveaxis(blocks, 0, dim).reshape(dims)


def from_everyone(array, axis):
    copies = jnp.broadcast_to(array, (lax.axis_size(axis), *array.shape))
    return lax.all_to_all(copies, axis, split_axis=0, concat_axis=0, tiled=True)


def gather_directly(array, axis, dim):
    return joined_along(from_everyone(array, axis), dim)


def nested_sum(array, axes):
    own = sum_at_owner(filled_up(array, lax.axis_size(axes)), axes, 0)
    whole = gather_directly(own, axes, 0)
    return whole[: len(array)].reshape(array.shape)


def together(arrays, axis):
    ends = [0]
    for a in arrays:
        ends.append(ends[-1] + a.size)
    subtotal = nested_sum(jnp.concatenate([a.ravel() for a in arrays]), axis)
    return tuple((subtotal[b:e].reshape(a.shape) for a, b, e in zip(arrays, ends, ends[1:])))


def over_copies(array, axis):
    everything = from_everyone(array, axis)
    return jnp.sum(everything, axis=0)


def in_one(arrays, axis):
    ravelled, at, gathered = (jnp.concatenate([a.reshape(-1) for a in arrays]), 0, [])
    subtotal = over_copies(ravelled, axis)
    for a in arrays:
        gathered.append(subtotal[at : at + a.size].reshape(a.shape))
        at += a.size
    return tuple(gathered)


def advance(padded, cond_pad, nonlin, active, inside):
    kappa = cond_pad[None] / (1.0 + nonlin[:, None, None] * padded * padded)
    centre = padded[:, 1:-1, 1:-1]
    middle = kappa[:, 1:-1, 1:-1]
    flux = jnp.zeros_like(centre)
    places = (
        (slice(2, None), slice(1, -1)),
        (slice(0, -2), slice(1, -1)),
        (slice(1, -1), slice(2, None)),
        (slice(1, -1), slice(0, -2)),
    )
    for rows_at, cols_at in places:
        flux = flux + 0.5 * (middle + kappa[:, rows_at, cols_at]) * (
            padded[:, rows_at, cols_at] - centre
        )
    moved = jnp.where(inside[None, 1:-1, 1:-1], centre + time_step * flux, jnp.zeros_like(centre))
    return jnp.where(active[:, None, None], moved, centre)


def trim(array, margin):
    return array[..., margin : array.shape[-2] - margin, margin : array.shape[-1] - margin]


def trunk(rows_in, w_in, bias_in, w_out):
    pre = jnp.dot(rows_in, w_in, preferred_element_type=jnp.float32) + bias_in
    act = jax.nn.gelu(pre).astype(jnp.bfloat16)
    hidden = jnp.dot(act, w_out, preferred_element_type=jnp.float32).astype(jnp.bfloat16)
    return (pre, act, hidden)


def trunk_grads(rows_in, pre, act, w_out, dhidden):
    grad_b = dhidden.astype(jnp.bfloat16)
    grad_out = lax.dot_general(
        act, grad_b, (((0,), (0,)), ((), ())), preferred_element_type=jnp.float32
    )
    back = lax.dot_general(
        grad_b, w_out, (((1,), (1,)), ((), ())), preferred_element_type=jnp.float32
    )
    _, pull = jax.vjp(jax.nn.gelu, pre)
    grad_pre = pull(back)[0]
    grad_in = lax.dot_general(
        rows_in,
        grad_pre.astype(jnp.bfloat16),
        (((0,), (0,)), ((), ())),
        preferred_element_type=jnp.float32,
    )
    return (grad_in, jnp.sum(grad_pre, axis=0), grad_out)


def per_device(
    init_field, conduct, nonlin, counts, descriptors, time_code, w_in, bias_in, w_out, decoder
):
    run_dev, rows_dev, cols_dev = init_field.shape
    steps = time_code.shape[0]
    width = w_out.shape[0]
    run_size = lax.axis_size("run")
    row_size = lax.axis_size("row")
    column_size = lax.axis_size("col")
    cond_pad = extended(conduct.astype(jnp.bfloat16), (("row", 0), ("col", 1)), HALO).astype(
        conduct.dtype
    )
    row_ids = lax.axis_index("row") * rows_dev + jnp.arange(rows_dev + 2 * HALO) - HALO
    col_ids = lax.axis_index("col") * cols_dev + jnp.arange(cols_dev + 2 * HALO) - HALO
    row_ok = (row_ids >= 0) & (row_ids < rows_dev * row_size)
    col_ok = (col_ids >= 0) & (col_ids < cols_dev * column_size)
    inside = row_ok[:, None] & col_ok[None, :]
    field = init_field
    shots = []
    for outer in range(steps // HALO):
        padded = extended(field, (("row", 1), ("col", 2)), HALO)
        for inner in range(HALO):
            step = outer * HALO + inner
            padded = advance(
                padded, trim(cond_pad, inner), nonlin, step < counts, trim(inside, inner)
            )
            shots.append(trim(padded, HALO - 1 - inner).astype(jnp.bfloat16))
        field = padded
    snapshots = jnp.stack(shots, axis=1)
    runs_total = run_dev * run_size
    scale = 1.0 / (runs_total * steps)
    desc_wide = descriptors.astype(jnp.float32)
    codes_wide = time_code.astype(jnp.float32)
    sectioned = decoder.reshape(width, 1, decoder.shape[1], column_size, cols_dev)
    moved = lax.all_to_all(sectioned, "col", split_axis=3, concat_axis=1, tiled=True)
    weights = moved.reshape(width, rows_dev * cols_dev)
    targets = snapshots.reshape(run_dev * steps, rows_dev * cols_dev)
    mine = lax.dynamic_slice_in_dim(desc_wide, lax.axis_index("run") * run_dev, run_dev, 0)
    rows_in = (
        (mine[:, None, :] + codes_wide[None])
        .astype(jnp.bfloat16)
        .reshape(run_dev * steps, desc_wide.shape[1])
    )
    pre, act, hidden = trunk(rows_in, w_in, bias_in, w_out)
    pred = jnp.dot(hidden, weights, preferred_element_type=jnp.float32)
    err = pred - targets.astype(jnp.float32)
    grad_pred = (err * scale).astype(jnp.bfloat16)
    partial_value = lax.dot_general(
        grad_pred, weights, (((1,), (1,)), ((), ())), preferred_element_type=jnp.float32
    )
    loss_part = jnp.sum(err * err)
    dhidden, loss_grid = together((partial_value, loss_part), ("row", "col"))
    grad_in, grad_bias, grad_out = trunk_grads(rows_in, pre, act, w_out, dhidden)
    grad_in, grad_bias, grad_out, loss_total = in_one(
        (grad_in, grad_bias, grad_out, loss_grid), "run"
    )
    new_w_in = w_in.astype(jnp.float32) - learn_rate * grad_in
    new_bias = bias_in - learn_rate * grad_bias
    new_w_out = w_out.astype(jnp.float32) - learn_rate * grad_out
    cells_total = rows_dev * row_size * cols_dev * column_size
    mean_loss = loss_total / (runs_total * steps * cells_total)
    return (field, new_w_in, new_bias, new_w_out, mean_loss)


def solution(mesh):
    in_specs = (
        P("run", "row", "col"),
        P("row", "col"),
        P("run"),
        P("run"),
        P(),
        P(),
        P(),
        P(),
        P(),
        P(None, ("row", "col"), None),
    )
    out_specs = (P("run", "row", "col"), P(), P(), P(), P())
    return jax.shard_map(
        per_device, mesh=mesh, in_specs=in_specs, out_specs=out_specs, check_vma=False
    )
```

profile of v0, /device:TPU:1, one launch (start us, length us, event | category | flops | bytes accessed | tf_op | source)
XLA Modules:
  0.0 418.5 jit_solution(3283372075120051438)
XLA Ops:
  2.7 4.6 %collective-permute-start.4 = (bf16[4,128]{1,0:T(4,128)(2,1)S(1)}, bf16[4,128]{1,0:T(4,128)(2,1)S(1)}, u32[]{:S(2)}, u32[]{:S(2)}) collective-permute-start(bf16[4,128]{1,0:T(4,128)(2,1)S(1)} %get-tuple-element.62), channel_id=1, source_target_pairs={{0,8},{8,16},{16,24},{24,32},{32,40},{40,48},{48,56},{1,9},{9,17},... | collective-permute-start | bytes 3080 | tf_op jit(solution)/shard_map/ppermute | solution.py:18
  9.7 4.0 collective-permute-start
  13.7 12.7 %copy.109 = bf16[512,8,1024]{0,2,1:T(8,128)(2,1)} copy(bf16[512,8,1024]{2,1,0:T(8,128)(2,1)} %param.19) | data formatting | bytes 16777216 | tf_op args[9]
  26.4 12.9 %copy.110 = bf16[512,1,8,8,128]{4,2,0,1,3:T(8,128)(2,1)} copy(bf16[512,1,8,8,128]{0,4,3,2,1:T(8,128)(2,1)} %bitcast.78) | data formatting | bytes 16777216 | tf_op jit(solution)/shard_map/reshape | solution.py:170
  39.3 7.9 %all-to-all-start = ((bf16[512,1,8,8,128]{4,2,0,1,3:T(8,128)(2,1)}), bf16[512,1,8,8,128]{4,2,0,1,3:T(8,128)(2,1)}, u32[]{:S(2)}, u32[]{:S(2)}) async-start(bf16[512,1,8,8,128]{4,2,0,1,3:T(8,128)(2,1)} %copy.110), calls=%async_computation | async-start | bytes 16777216 | tf_op jit(solution)/shard_map/all_to_all | solution.py:171
  51.5 6.1 %collective-permute-start.6 = (bf16[72,4]{1,0:T(8,128)(2,1)S(1)}, bf16[72,4]{1,0:T(8,128)(2,1)}, u32[]{:S(2)}, u32[]{:S(2)}) collective-permute-start(bf16[72,4]{1,0:T(8,128)(2,1)S(1)} %get-tuple-element.60), channel_id=1, source_target_pairs={{0,1},{1,2},{2,3},{3,4},{4,5},{5,6},{6,7},{8,9},{9,10},{10,11},{11... | collective-permute-start | bytes 1736 | tf_op jit(solution)/shard_map/ppermute | solution.py:18
  65.6 6.6 %collective-permute-start.2 = (f32[48,72,4]{1,0,2:T(8,128)}, f32[48,72,4]{1,0,2:T(8,128)}, u32[]{:S(2)}, u32[]{:S(2)}) collective-permute-start(f32[48,72,4]{1,0,2:T(8,128)} %copy.97), channel_id=1, source_target_pairs={{0,1},{1,2},{2,3},{3,4},{4,5},{5,6},{6,7},{8,9},{9,10},{10,11},{11... | collective-permute-start | bytes 165896 | tf_op jit(solution)/shard_map/ppermute | solution.py:18
  72.2 22.3 %collective-permute-done.7 = bf16[72,4]{1,0:T(8,128)(2,1)S(1)} collective-permute-done((bf16[72,4]{1,0:T(8,128)(2,1)S(1)}, bf16[72,4]{1,0:T(8,128)(2,1)S(1)}, u32[]{:S(2)}, u32[]{:S(2)}) %collective-permute-start.7) | collective-permute-done | bytes 608 | tf_op jit(solution)/shard_map/ppermute | solution.py:21
  95.1 19.3 %collective-permute-done.6 = bf16[72,4]{1,0:T(8,128)(2,1)} collective-permute-done((bf16[72,4]{1,0:T(8,128)(2,1)S(1)}, bf16[72,4]{1,0:T(8,128)(2,1)}, u32[]{:S(2)}, u32[]{:S(2)}) %collective-permute-start.6) | collective-permute-done | bytes 608 | tf_op jit(solution)/shard_map/ppermute | solution.py:18
  118.9 2.7 copy.99
  121.7 3.8 fusion.3
  125.5 7.8 %fusion.5 = (f32[48,70,134]{2,1,0:T(8,128)S(1)}, f32[48,70,134]{2,1,0:T(8,128)S(1)}) fusion(f32[48]{0:T(128)S(1)} %copy-done.20, f32[70,134]{1,0:T(8,128)S(1)} %copy-done.11, f32[48,72,136]{2,1,0:T(8,128)S(1)} %get-tuple-element.51, f32[48,72,136]{2,1,0:T(8,128)S(1)} %get-tuple-element.50, pred[70,134]{1,0:T(8,128)(4,1)S(1)} %copy-done.14, ...), kind=kLoop, calls=%fused_computation.17 | loop fusion | flops 12156480 | bytes 21658660 | tf_op jit(solution)/shard_map/div | solution.py:89
  134.8 7.8 %fusion.7 = (f32[48,68,132]{2,1,0:T(8,128)S(1)}, f32[48,68,132]{2,1,0:T(8,128)S(1)}) fusion(f32[48]{0:T(128)S(1)} %copy-done.20, f32[68,132]{1,0:T(8,128)S(1)} %copy-done.9, f32[48,70,134]{2,1,0:T(8,128)S(1)} %get-tuple-element.49, f32[48,70,134]{2,1,0:T(8,128)S(1)} %get-tuple-element.48, pred[68,132]{1,0:T(8,128)(4,1)S(1)} %slice.464, ...), kind=kLoop, calls=%fused_computation.19 | loop fusion | flops 11632896 | bytes 20725824 | tf_op jit(solution)/shard_map/div | solution.py:89
  144.0 7.8 %fusion.9 = (f32[48,66,130]{2,1,0:T(8,128)S(1)}, f32[48,66,130]{2,1,0:T(8,128)S(1)}) fusion(f32[48]{0:T(128)S(1)} %copy-done.20, f32[66,130]{1,0:T(8,128)S(1)} %copy-done.7, f32[48,68,132]{2,1,0:T(8,128)S(1)} %get-tuple-element.47, f32[48,68,132]{2,1,0:T(8,128)S(1)} %get-tuple-element.46, pred[66,130]{1,0:T(8,128)(4,1)S(1)} %slice.463, ...), kind=kLoop, calls=%fused_computation.21 | loop fusion | flops 11119680 | bytes 19811460 | tf_op jit(solution)/shard_map/div | solution.py:89
  153.3 4.2 %bitcast_dynamic-update-slice_fusion = (bf16[48,8,64,128]{3,2,1,0:T(8,128)(2,1)}, f32[48,64,128]{2,1,0:T(8,128)S(1)}) fusion(bf16[48,8,64,128]{3,2,1,0:T(8,128)(2,1)} %fusion.146, f32[48,66,130]{2,1,0:T(8,128)S(1)} %get-tuple-element.45, f32[48,66,130]{2,1,0:T(8,128)S(1)} %get-tuple-element.44, pred[64,128]{1,0:T(8,128)(4,1)S(1)} %copy-done.17, ...), kind=kLoop, calls=%fused_computation.253 | loop fusion | flops 9437184 | bytes 18096176
  158.9 4.0 collective-permute-start.8
  172.4 52.7 %collective-permute-start.10 = (f32[48,72,4]{1,0,2:T(8,128)}, f32[48,72,4]{1,0,2:T(8,128)}, u32[]{:S(2)}, u32[]{:S(2)}) collective-permute-start(f32[48,72,4]{1,0,2:T(8,128)} %copy.105), channel_id=1, source_target_pairs={{0,1},{1,2},{2,3},{3,4},{4,5},{5,6},{6,7},{8,9},{9,10},{10,11},{11... | collective-permute-start | bytes 165896 | tf_op jit(solution)/shard_map/ppermute | solution.py:18
  228.8 2.7 copy.107
  231.5 4.1 fusion.11
  235.7 7.8 %fusion.13 = (f32[48,70,134]{2,1,0:T(8,128)S(1)}, f32[48,70,134]{2,1,0:T(8,128)S(1)}) fusion(f32[48]{0:T(128)S(1)} %copy-done.21, f32[70,134]{1,0:T(8,128)S(1)} %copy-done.12, f32[48,72,136]{2,1,0:T(8,128)S(1)} %get-tuple-element.43, f32[48,72,136]{2,1,0:T(8,128)S(1)} %get-tuple-element.42, pred[70,134]{1,0:T(8,128)(4,1)S(1)} %copy-done.15, ...), kind=kLoop, calls=%fused_computation.25 | loop fusion | flops 12156480 | bytes 21658660 | tf_op jit(solution)/shard_map/div | solution.py:89
  244.9 7.8 %fusion.15 = (f32[48,68,132]{2,1,0:T(8,128)S(1)}, f32[48,68,132]{2,1,0:T(8,128)S(1)}) fusion(f32[48]{0:T(128)S(1)} %copy-done.21, f32[68,132]{1,0:T(8,128)S(1)} %copy-done.10, f32[48,70,134]{2,1,0:T(8,128)S(1)} %get-tuple-element.41, f32[48,70,134]{2,1,0:T(8,128)S(1)} %get-tuple-element.40, pred[68,132]{1,0:T(8,128)(4,1)S(1)} %slice.464, ...), kind=kLoop, calls=%fused_computation.27 | loop fusion | flops 11632896 | bytes 20725824 | tf_op jit(solution)/shard_map/div | solution.py:89
  254.2 7.8 %fusion.17 = (f32[48,66,130]{2,1,0:T(8,128)S(1)}, f32[48,66,130]{2,1,0:T(8,128)S(1)}) fusion(f32[48]{0:T(128)S(1)} %copy-done.21, f32[66,130]{1,0:T(8,128)S(1)} %copy-done.8, f32[48,68,132]{2,1,0:T(8,128)S(1)} %get-tuple-element.39, f32[48,68,132]{2,1,0:T(8,128)S(1)} %get-tuple-element.38, pred[66,130]{1,0:T(8,128)(4,1)S(1)} %slice.463, ...), kind=kLoop, calls=%fused_computation.29 | loop fusion | flops 11119680 | bytes 19811460 | tf_op jit(solution)/shard_map/div | solution.py:89
  263.4 4.5 %bitcast_dynamic-update-slice_fusion.1 = (bf16[48,8,64,128]{3,2,1,0:T(8,128)(2,1)}, f32[48,64,128]{2,1,0:T(8,128)}) fusion(bf16[48,8,64,128]{3,2,1,0:T(8,128)(2,1)} %fusion.148, f32[48,66,130]{2,1,0:T(8,128)S(1)} %get-tuple-element.37, f32[48,66,130]{2,1,0:T(8,128)S(1)} %get-tuple-element.36, pred[64,128]{1,0:T(8,128)(4,1)S(1)} %copy-done.18, ...), kind=kLoop, calls=%fused_computation.254 | loop fusion | flops 9437184 | bytes 18096176 | tf_op jit(solution)/shard_map/stack | solution.py:165
  267.9 8.9 %convert_bitcast_fusion = f32[48,8,64,128]{3,2,1,0:T(8,128)} fusion(bf16[48,8,64,128]{3,2,1,0:T(8,128)(2,1)} %get-tuple-element.32), kind=kLoop, calls=%fused_computation.1 | loop fusion | flops 3145728 | bytes 18874368
  276.9 12.8 %copy.111 = bf16[512,1,8,8,128]{0,4,2,3,1:T(8,128)(2,1)} copy(bf16[512,1,8,8,128]{4,2,0,1,3:T(8,128)(2,1)} %all-to-all-done) | data formatting | bytes 16777216 | tf_op jit(solution)/shard_map/all_to_all | solution.py:171
  289.7 20.8 %multiply_reduce_fusion = (f32[]{:T(128)}, f32[384,8192]{1,0:T(8,128)}) fusion(f32[48,8,64,128]{3,2,1,0:T(8,128)} %convert_bitcast_fusion, bf16[512,8192]{0,1:T(8,128)(2,1)} %bitcast.76, bf16[512,512]{1,0:T(8,128)(2,1)S(1)} %copy-done, f32[384,512]{1,0:T(8,128)S(1)} %copy-done.3), kind=kOutput, calls=%fused_computation.2 | convolution fusion | flops 3433955328 | bytes 34865156 | tf_op jit(solution)/shard_map/dot_general | solution.py:181
  310.5 8.8 %fusion.138 = f32[48,4,8,128]{3,2,1,0:T(8,128)S(1)} fusion(bf16[512,8192]{0,1:T(8,128)(2,1)} %bitcast.77, f32[384,8192]{1,0:T(8,128)} %get-tuple-element.73), kind=kOutput, calls=%fused_computation.226 | convolution fusion | flops 3227516928 | bytes 21757952 | tf_op jit(solution)/shard_map/dot_general | solution.py:184
  321.7 26.9 %all_to_all.36 = f32[64,1,3073]{2,1,0:T(1,128)S(1)} all-to-all(f32[64,1,3073]{2,1,0:T(1,128)S(1)} %all_to_all.28), channel_id=1, replica_groups=mesh['run'=2,'row'=8,'col'=8] {'row','col'}, dimensions={0} | all-to-all | bytes 1573376 | tf_op jit(solution)/shard_map/all_to_all | solution.py:34
  349.4 16.8 %all_to_all.37 = f32[64,1,3073]{2,1,0:T(1,128)S(1)} all-to-all(f32[64,1,3073]{2,1,0:T(1,128)S(1)} %broadcast_in_dim.155), channel_id=1, replica_groups=mesh['run'=2,'row'=8,'col'=8] {'row','col'}, dimensions={0} | all-to-all | bytes 1573376 | tf_op jit(solution)/shard_map/all_to_all | solution.py:53
  372.2 7.4 %broadcast_in_dim.156 = f32[2,1,393729]{2,1,0:T(1,128)S(1)} broadcast(f32[393729]{0:T(1024)S(1)} %pad_maximum_fusion.4), dimensions={2} | broadcast | bytes 4724748 | tf_op jit(solution)/shard_map/broadcast_in_dim | solution.py:52
  379.6 15.8 %all_to_all.38 = f32[2,1,393729]{2,1,0:T(1,128)S(1)} all-to-all(f32[2,1,393729]{2,1,0:T(1,128)S(1)} %broadcast_in_dim.156), channel_id=1, replica_groups=mesh['run'=2,'row'=8,'col'=8] {'run'}, dimensions={0} | all-to-all | bytes 6299664 | tf_op jit(solution)/shard_map/all_to_all | solution.py:53
  395.5 13.8 %reduce_sum.39 = f32[393729]{0:T(1024)} reduce(f32[2,1,393729]{2,1,0:T(1,128)S(1)} %all_to_all.38, f32[]{:T(128)} %constant.47.clone.1), dimensions={0,1}, to_apply=%region_3.4 | reduce | flops 393729 | bytes 4724752 | tf_op jit(solution)/shard_map/reduce_sum | solution.py:76
  (161 shorter events, 61.0 us)
Async XLA Ops:
  1.4 48.7 %copy-start.16 = (bf16[64,128]{1,0:T(8,128)(2,1)}, bf16[64,128]{1,0:T(8,128)(2,1)S(1)}, u32[]{:S(2)}) copy-start(bf16[64,128]{1,0:T(8,128)(2,1)S(1)} %convert_element_type.67) | copy-start | bytes 49156
  1.4 48.7 %collective-permute-start.5 = (bf16[4,128]{1,0:T(4,128)(2,1)S(1)}, bf16[4,128]{1,0:T(4,128)(2,1)S(1)}, u32[]{:S(2)}, u32[]{:S(2)}) collective-permute-start(bf16[4,128]{1,0:T(4,128)(2,1)S(1)} %get-tuple-element.63), channel_id=1, source_target_pairs={{8,0},{16,8},{24,16},{32,24},{40,32},{48,40},{56,48},{9,1},{17,9},... | collective-permute-start | bytes 3080 | tf_op jit(solution)/shard_map/ppermute | solution.py:21
  2.7 47.4 %collective-permute-start.4 = (bf16[4,128]{1,0:T(4,128)(2,1)S(1)}, bf16[4,128]{1,0:T(4,128)(2,1)S(1)}, u32[]{:S(2)}, u32[]{:S(2)}) collective-permute-start(bf16[4,128]{1,0:T(4,128)(2,1)S(1)} %get-tuple-element.62), channel_id=1, source_target_pairs={{0,8},{8,16},{16,24},{24,32},{32,40},{40,48},{48,56},{1,9},{9,17},... | collective-permute-start | bytes 3080 | tf_op jit(solution)/shard_map/ppermute | solution.py:18
  8.4 49.3 %collective-permute-start.1 = (f32[48,4,128]{2,0,1:T(8,128)S(1)}, f32[48,4,128]{2,0,1:T(8,128)S(1)}, u32[]{:S(2)}, u32[]{:S(2)}) collective-permute-start(f32[48,4,128]{2,0,1:T(8,128)S(1)} %copy.124), channel_id=1, source_target_pairs={{8,0},{16,8},{24,16},{32,24},{40,32},{48,40},{56,48},{9,1},{17,9},... | collective-permute-start | bytes 294920 | tf_op jit(solution)/shard_map/ppermute | solution.py:21
  9.7 48.0 %collective-permute-start = (f32[48,4,128]{2,0,1:T(8,128)S(1)}, f32[48,4,128]{2,0,1:T(8,128)S(1)}, u32[]{:S(2)}, u32[]{:S(2)}) collective-permute-start(f32[48,4,128]{2,0,1:T(8,128)S(1)} %copy.123), channel_id=1, source_target_pairs={{0,8},{8,16},{16,24},{24,32},{32,40},{40,48},{48,56},{1,9},{9,17},... | collective-permute-start | bytes 294920 | tf_op jit(solution)/shard_map/ppermute | solution.py:18
  39.3 10.2 %copy-start.27 = (bf16[8,256]{1,0:T(8,128)(2,1)S(1)}, bf16[8,256]{1,0:T(8,128)(2,1)}, u32[]{:S(2)}) copy-start(bf16[8,256]{1,0:T(8,128)(2,1)} %param.15) | copy-start | bytes 12292
  39.3 19.1 %copy-start.2 = (f32[48,64,128]{2,1,0:T(8,128)S(1)}, f32[48,64,128]{2,1,0:T(8,128)}, u32[]{:S(2)}) copy-start(f32[48,64,128]{2,1,0:T(8,128)} %param.10) | copy-start | bytes 4718596
  39.3 237.6 %all-to-all-start = ((bf16[512,1,8,8,128]{4,2,0,1,3:T(8,128)(2,1)}), bf16[512,1,8,8,128]{4,2,0,1,3:T(8,128)(2,1)}, u32[]{:S(2)}, u32[]{:S(2)}) async-start(bf16[512,1,8,8,128]{4,2,0,1,3:T(8,128)(2,1)} %copy.110), calls=%async_computation | async-start | bytes 16777216 | tf_op jit(solution)/shard_map/all_to_all | solution.py:171
  50.2 44.3 %collective-permute-start.7 = (bf16[72,4]{1,0:T(8,128)(2,1)S(1)}, bf16[72,4]{1,0:T(8,128)(2,1)S(1)}, u32[]{:S(2)}, u32[]{:S(2)}) collective-permute-start(bf16[72,4]{1,0:T(8,128)(2,1)S(1)} %get-tuple-element.61), channel_id=1, source_target_pairs={{1,0},{2,1},{3,2},{4,3},{5,4},{6,5},{7,6},{9,8},{10,9},{11,10},{12... | collective-permute-start | bytes 1736 | tf_op jit(solution)/shard_map/ppermute | solution.py:21
  51.5 62.9 %collective-permute-start.6 = (bf16[72,4]{1,0:T(8,128)(2,1)S(1)}, bf16[72,4]{1,0:T(8,128)(2,1)}, u32[]{:S(2)}, u32[]{:S(2)}) collective-permute-start(bf16[72,4]{1,0:T(8,128)(2,1)S(1)} %get-tuple-element.60), channel_id=1, source_target_pairs={{0,1},{1,2},{2,3},{3,4},{4,5},{5,6},{6,7},{8,9},{9,10},{10,11},{11... | collective-permute-start | bytes 1736 | tf_op jit(solution)/shard_map/ppermute | solution.py:18
  63.1 54.3 %collective-permute-start.3 = (f32[48,72,4]{1,0,2:T(8,128)}, f32[48,72,4]{1,0,2:T(8,128)}, u32[]{:S(2)}, u32[]{:S(2)}) collective-permute-start(f32[48,72,4]{1,0,2:T(8,128)} %copy.98), channel_id=1, source_target_pairs={{1,0},{2,1},{3,2},{4,3},{5,4},{6,5},{7,6},{9,8},{10,9},{11,10},{12... | collective-permute-start | bytes 165896 | tf_op jit(solution)/shard_map/ppermute | solution.py:21
  65.6 53.3 %collective-permute-start.2 = (f32[48,72,4]{1,0,2:T(8,128)}, f32[48,72,4]{1,0,2:T(8,128)}, u32[]{:S(2)}, u32[]{:S(2)}) collective-permute-start(f32[48,72,4]{1,0,2:T(8,128)} %copy.97), channel_id=1, source_target_pairs={{0,1},{1,2},{2,3},{3,4},{4,5},{5,6},{6,7},{8,9},{9,10},{10,11},{11... | collective-permute-start | bytes 165896 | tf_op jit(solution)/shard_map/ppermute | solution.py:18
  125.5 9.3 %copy-start.9 = (f32[68,132]{1,0:T(8,128)S(1)}, f32[68,132]{1,0:T(8,128)}, u32[]{:S(2)}) copy-start(f32[68,132]{1,0:T(8,128)} %slice.494) | copy-start | bytes 107716
  125.5 9.2 %copy-start.34 = (pred[48]{0:T(512)(128)(4,1)S(1)}, pred[48]{0:T(512)(128)(4,1)}, u32[]{:S(2)}) copy-start(pred[48]{0:T(512)(128)(4,1)} %get-tuple-element.71) | copy-start | bytes 148
  134.8 9.3 %copy-start.7 = (f32[66,130]{1,0:T(8,128)S(1)}, f32[66,130]{1,0:T(8,128)}, u32[]{:S(2)}) copy-start(f32[66,130]{1,0:T(8,128)} %slice.505) | copy-start | bytes 102964
  134.8 9.3 %copy-start.33 = (pred[48]{0:T(512)(128)(4,1)S(1)}, pred[48]{0:T(512)(128)(4,1)}, u32[]{:S(2)}) copy-start(pred[48]{0:T(512)(128)(4,1)} %get-tuple-element.65) | copy-start | bytes 148
  144.0 9.2 %copy-start.29 = (pred[48]{0:T(512)(128)(4,1)S(1)}, pred[48]{0:T(512)(128)(4,1)}, u32[]{:S(2)}) copy-start(pred[48]{0:T(512)(128)(4,1)} %get-tuple-element.66) | copy-start | bytes 148
  153.3 9.6 %copy-start.23 = (bf16[96,256]{1,0:T(8,128)(2,1)S(1)}, bf16[96,256]{1,0:T(8,128)(2,1)}, u32[]{:S(2)}) copy-start(bf16[96,256]{1,0:T(8,128)(2,1)} %param.14) | copy-start | bytes 147460
  157.6 6.0 %collective-permute-start.9 = (f32[48,4,128]{2,0,1:T(8,128)S(1)}, f32[48,4,128]{2,0,1:T(8,128)S(1)}, u32[]{:S(2)}, u32[]{:S(2)}) collective-permute-start(f32[48,4,128]{2,0,1:T(8,128)S(1)} %copy.102), channel_id=1, source_target_pairs={{8,0},{16,8},{24,16},{32,24},{40,32},{48,40},{56,48},{9,1},{17,9},... | collective-permute-start | bytes 294920 | tf_op jit(solution)/shard_map/ppermute | solution.py:21
  158.9 5.6 %collective-permute-start.8 = (f32[48,4,128]{2,0,1:T(8,128)S(1)}, f32[48,4,128]{2,0,1:T(8,128)S(1)}, u32[]{:S(2)}, u32[]{:S(2)}) collective-permute-start(f32[48,4,128]{2,0,1:T(8,128)S(1)} %copy.101), channel_id=1, source_target_pairs={{0,8},{8,16},{16,24},{24,32},{32,40},{40,48},{48,56},{1,9},{9,17},... | collective-permute-start | bytes 294920 | tf_op jit(solution)/shard_map/ppermute | solution.py:18
  169.9 57.4 %collective-permute-start.11 = (f32[48,72,4]{1,0,2:T(8,128)}, f32[48,72,4]{1,0,2:T(8,128)}, u32[]{:S(2)}, u32[]{:S(2)}) collective-permute-start(f32[48,72,4]{1,0,2:T(8,128)} %copy.106), channel_id=1, source_target_pairs={{1,0},{2,1},{3,2},{4,3},{5,4},{6,5},{7,6},{9,8},{10,9},{11,10},{12... | collective-permute-start | bytes 165896 | tf_op jit(solution)/shard_map/ppermute | solution.py:21
  172.4 56.3 %collective-permute-start.10 = (f32[48,72,4]{1,0,2:T(8,128)}, f32[48,72,4]{1,0,2:T(8,128)}, u32[]{:S(2)}, u32[]{:S(2)}) collective-permute-start(f32[48,72,4]{1,0,2:T(8,128)} %copy.105), channel_id=1, source_target_pairs={{0,1},{1,2},{2,3},{3,4},{4,5},{5,6},{6,7},{8,9},{9,10},{10,11},{11... | collective-permute-start | bytes 165896 | tf_op jit(solution)/shard_map/ppermute | solution.py:18
  235.7 9.2 %copy-start.10 = (f32[68,132]{1,0:T(8,128)S(1)}, f32[68,132]{1,0:T(8,128)}, u32[]{:S(2)}) copy-start(f32[68,132]{1,0:T(8,128)} %slice.494) | copy-start | bytes 107716
  235.7 9.2 %copy-start.31 = (pred[48]{0:T(512)(128)(4,1)S(1)}, pred[48]{0:T(512)(128)(4,1)}, u32[]{:S(2)}) copy-start(pred[48]{0:T(512)(128)(4,1)} %get-tuple-element.68) | copy-start | bytes 148
  244.9 9.3 %copy-start.8 = (f32[66,130]{1,0:T(8,128)S(1)}, f32[66,130]{1,0:T(8,128)}, u32[]{:S(2)}) copy-start(f32[66,130]{1,0:T(8,128)} %slice.505) | copy-start | bytes 102964
  244.9 9.3 %copy-start.30 = (pred[48]{0:T(512)(128)(4,1)S(1)}, pred[48]{0:T(512)(128)(4,1)}, u32[]{:S(2)}) copy-start(pred[48]{0:T(512)(128)(4,1)} %get-tuple-element.69) | copy-start | bytes 148
  254.2 9.3 %copy-start.18 = (pred[64,128]{1,0:T(8,128)(4,1)S(1)}, pred[64,128]{1,0:T(8,128)(4,1)}, u32[]{:S(2)}) copy-start(pred[64,128]{1,0:T(8,128)(4,1)} %slice.462) | copy-start | bytes 24580
  254.2 9.3 %copy-start.28 = (pred[48]{0:T(512)(128)(4,1)S(1)}, pred[48]{0:T(512)(128)(4,1)}, u32[]{:S(2)}) copy-start(pred[48]{0:T(512)(128)(4,1)} %get-tuple-element.64) | copy-start | bytes 148
  276.9 12.8 %copy-start = (bf16[512,512]{1,0:T(8,128)(2,1)S(1)}, bf16[512,512]{1,0:T(8,128)(2,1)}, u32[]{:S(2)}) copy-start(bf16[512,512]{1,0:T(8,128)(2,1)} %param.18) | copy-start | bytes 1572868
  276.9 12.8 %copy-start.3 = (f32[384,512]{1,0:T(8,128)S(1)}, f32[384,512]{1,0:T(8,128)}, u32[]{:S(2)}) copy-start(f32[384,512]{1,0:T(8,128)} %convolution_add_fusion) | copy-start | bytes 2359300
  395.5 14.9 %copy-start.24 = (f32[512]{0:T(512)S(1)}, f32[512]{0:T(512)}, u32[]{:S(2)}) copy-start(f32[512]{0:T(512)} %param.17) | copy-start | bytes 6148
  395.5 18.8 %copy-start.4 = (bf16[256,512]{1,0:T(8,128)(2,1)S(1)}, bf16[256,512]{1,0:T(8,128)(2,1)}, u32[]{:S(2)}) copy-start(bf16[256,512]{1,0:T(8,128)(2,1)} %param.16) | copy-start | bytes 786436
  (18 other events, 73.4 us)
where the time goes:
time: 424 us; the launch traced here: 418 us
  other arithmetic  99.3 us (23%)
  starting transfers between devices  93.6 us (22%)
  local copies, waits for them, and re-layouts  86.9 us (20%)
  blocking collectives  59.5 us (14%)
  waiting for transfers between devices  42.6 us (10%)
  matrix products  33.4 us (8%)
    ppermute x6, starting transfers between devices, extended(): lax.ppermute(lax.slice_in_dim(block, block.shape[dim] - width, None, axis...  78 us
    div x8, other arithmetic, advance(): kappa = cond_pad[None] / (1.0 + nonlin[:, None, None] * padded * padded)  54.8 us
    all_to_all x2, blocking collectives, from_everyone(): return lax.all_to_all(copies, axis, split_axis=0, concat_axis=0, tiled=True)  32.6 us
    all_to_all x1, blocking collectives, sum_at_owner(): lax.all_to_all(blocks, axis, split_axis=0, concat_axis=0, tiled=True)  26.9 us
    unnamed x86, local copies, waits for them, and re-layouts  23.8 us
    ppermute x6, waiting for transfers between devices, extended(): lax.ppermute(lax.slice_in_dim(block, 0, width, axis=dim), axis, backward)  22.3 us
    dot_general x1, matrix products, per_device(): pred = jnp.dot(hidden, weights, preferred_element_type=jnp.float32)  20.8 us
    ppermute x6, waiting for transfers between devices, extended(): lax.ppermute(lax.slice_in_dim(block, block.shape[dim] - width, None, axis...  20.2 us
  transfers between devices with their start and end apart: 13, of which 3 were waited for; matrix products, arithmetic and copies ran while one was open for 33% of the time, Pallas kernels for 0%

commit v1 on v0

v1 whole, which is shorter than its diff:
```python
import jax
import jax.numpy as jnp
from jax import lax
from jax.experimental import pallas as pl
from jax.experimental.pallas import tpu as pltpu
from jax.sharding import PartitionSpec as P

MESH = pl.DeviceIdType.MESH
f32, bf16 = jnp.float32, jnp.bfloat16
STEP, RATE = 0.12, 0.5
ROWS = 96
GROUPS = ROWS // 4
OFFSETS = ((2, 1), (1, 1), (3, 1), (2, 0), (0, 1), (1, 0), (3, 0))
VMEM_ALL = 64 << 20


def signal_all(peers):
    barrier = pltpu.get_barrier_semaphore()
    for peer in peers:
        pl.semaphore_signal(barrier, inc=1, device_id=peer, device_id_type=MESH)
    pl.semaphore_wait(barrier, len(peers))


def remote(src, dst, send, recv, peer):
    return pltpu.make_async_remote_copy(
        src_ref=src, dst_ref=dst, send_sem=send, recv_sem=recv, device_id=peer, device_id_type=MESH
    )


def main_kernel(
    field, conduct, nl, cnt, decoder, hid,
    final, part, loss,
    fs, cd, u, cb, xs, xr, fx, snap, tr, dl, raw, tf, gram, acc,
    loc_sem, raw_sem, row_send, row_recv, col_send, col_recv, dec_send, dec_recv, own_sem, fwd_send, fwd_recv,
):
    core, row, col = (lax.axis_index(n) for n in ("run", "row", "col"))
    y, zh = col // 2, col % 2
    sibling = (1 - core, row, col)
    down, up = (core, (row + 1) % 8, col), (core, (row + 7) % 8, col)
    right, left = (core, row, (col + 1) % 8), (core, row, (col + 7) % 8)
    targets = [((y + dy) % 4) * 2 + (zh + dz) % 2 for dy, dz in OFFSETS]
    signal_all([(core, row, t) for t in targets] + [up, down, sibling])

    fs3 = fs.reshape(48, 80, 128)
    row_copies = [
        remote(field.at[:, pl.ds(56, 8), :], fs3.at[:, pl.ds(0, 8), :], row_send.at[0], row_recv.at[0], down),
        remote(field.at[:, pl.ds(0, 8), :], fs3.at[:, pl.ds(72, 8), :], row_send.at[1], row_recv.at[1], up),
        remote(conduct.at[pl.ds(56, 8), :], cd.at[pl.ds(0, 8), :], row_send.at[2], row_recv.at[2], down),
        remote(conduct.at[pl.ds(0, 8), :], cd.at[pl.ds(72, 8), :], row_send.at[3], row_recv.at[3], up),
    ]
    loc_copies = [
        pltpu.make_async_copy(field, fs3.at[:, pl.ds(8, 64), :], loc_sem.at[0]),
        pltpu.make_async_copy(conduct, cd.at[pl.ds(8, 64), :], loc_sem.at[1]),
    ]

    def raw_copy(part_at, slot):
        start = pl.multiple_of(part_at * 1024, 1024)
        return pltpu.make_async_copy(decoder.at[pl.ds(start, 1024), :], raw.at[slot], raw_sem.at[slot])

    mine, other = 2 * core, 2 * (1 - core)

    def turn(quarter, slot):
        def piece(hb, carry):
            at = pl.multiple_of(hb * 256, 256)
            to = pl.multiple_of(quarter * 128 + hb * 32, 32)
            for t in range(8):
                tf[t] = raw[slot, pl.ds(at, 256), t * 128 : (t + 1) * 128].astype(f32)
            for t in range(8):
                for i in range(8):
                    tr[t, i, pl.ds(to, 32), :] = tf[t, pl.ds(i, 32, stride=8), :].astype(bf16)
            return carry

        lax.fori_loop(0, 4, piece, 0)

    def dec_copies(hh, kk):
        h0 = pl.multiple_of((mine + hh) * 128, 128)
        rnd = hh * 4 + kk
        out = []
        for j, t in enumerate(targets):
            out.append(
                remote(
                    tr.at[t, pl.ds(2 * kk, 2), pl.ds(h0, 128), :],
                    dl.at[kk, pl.ds(2 * col, 2), pl.ds(h0, 128), :],
                    dec_send.at[rnd, j], dec_recv.at[rnd, j], (core, row, t),
                )
            )
        return out

    def own_copy(hh, kk):
        h0 = pl.multiple_of((mine + hh) * 128, 128)
        return pltpu.make_async_copy(
            tr.at[col, pl.ds(2 * kk, 2), pl.ds(h0, 128), :],
            dl.at[kk, pl.ds(2 * col, 2), pl.ds(h0, 128), :],
            own_sem.at[hh * 4 + kk],
        )

    def fwd_copy(hh, kk):
        h0 = pl.multiple_of((mine + hh) * 128, 128)
        block = dl.at[kk, :, pl.ds(h0, 128), :]
        return remote(block, block, fwd_send.at[hh * 4 + kk], fwd_recv.at[hh * 4 + kk], sibling)

    def send_round(hh, kk):
        for c in dec_copies(hh, kk):
            c.start()
        own_copy(hh, kk).start()

    def pass_round(hh, kk):
        for c in dec_copies(hh, kk):
            c.wait_recv()
        own_copy(hh, kk).wait()
        fwd_copy(hh, kk).start()

    for c in row_copies + loc_copies:
        c.start()
    raw_copy(mine, 0).start()
    raw_copy(mine + 1, 1).start()
    raw_copy(mine, 0).wait()
    turn(mine, 0)
    raw_copy(other, 0).start()
    send_round(0, 0)

    for c in loc_copies:
        c.wait()
    for c in row_copies:
        c.wait_recv()
    for b in range(3):
        u[b, 0:8] = jnp.zeros((8, 2, 8, 128), f32)
        u[b, 88:96] = jnp.zeros((8, 2, 8, 128), f32)

    def fill(i, carry):
        for b in range(3):
            u[b, i + 8] = fs[pl.ds(b * 1280 + i, 16, stride=80), :].reshape(2, 8, 128)
        cb[0, i + 8] = jnp.broadcast_to(cd[pl.ds(i, 1), :] * (0.5 * STEP), (8, 128))
        return carry

    lax.fori_loop(0, 80, fill, 0)
    for s in (0, 1):
        cb[s, 0:8] = jnp.zeros((8, 8, 128), f32)
        cb[s, 88:96] = jnp.zeros((8, 8, 128), f32)

    def clear(b):
        @pl.when(row == 0)
        def _():
            u[b, 8:16] = jnp.zeros((8, 2, 8, 128), f32)

        @pl.when(row == 7)
        def _():
            u[b, 80:88] = jnp.zeros((8, 2, 8, 128), f32)

    for b in range(3):
        clear(b)

    @pl.when(row == 0)
    def _():
        cb[0, 8:16] = jnp.zeros((8, 8, 128), f32)

    @pl.when(row == 7)
    def _():
        cb[0, 80:88] = jnp.zeros((8, 8, 128), f32)

    lane = lax.broadcasted_iota(jnp.int32, (2, 8, 128), 2)
    in32 = lane % 32

    def gather_edges(i):
        out = None
        for b in range(4):
            v = u[b, i] if b < 3 else jnp.broadcast_to(cb[0, i][None], (2, 8, 128))
            ends = pltpu.roll(v, (32 * b + 8) % 128, 2)
            starts = pltpu.roll(v, (32 * b + 24) % 128, 2)
            both = jnp.where(in32 < 8, ends, starts)
            out = both if b == 0 else jnp.where(lane // 32 == b, both, out)
        return out

    def pack(g, carry):
        to_right = to_left = None
        for q in range(4):
            o = gather_edges(4 * g + q)
            u[3, 4 * g + q] = o
            r = pltpu.roll(o, 8 * q, 2) if q else o
            l = pltpu.roll(o, (8 * q + 8) % 32 + 96 if q < 3 else 0, 2) if q < 3 else pltpu.roll(o, 0, 2)
            here = in32 // 8 == q
            to_right = r if q == 0 else jnp.where(here, r, to_right)
            to_left = l if q == 0 else jnp.where(here, l, to_left)
        xs[0, g] = to_right
        xs[1, g] = to_left
        return carry

    lax.fori_loop(2, GROUPS - 2, pack, 0)
    col_copies = [
        remote(xs.at[0], xr.at[0], col_send.at[0], col_recv.at[0], right),
        remote(xs.at[1], xr.at[1], col_send.at[1], col_recv.at[1], left),
    ]
    for c in col_copies:
        c.start()
    for kk in range(1, 4):
        send_round(0, kk)
    raw_copy(mine + 1, 1).wait()
    turn(mine + 1, 1)
    raw_copy(other + 1, 1).start()
    for kk in range(4):
        send_round(1, kk)

    raw_copy(other, 0).wait()
    turn(other, 0)
    for c in col_copies:
        c.wait_recv()

    u[3, 0:8] = jnp.zeros((8, 2, 8, 128), f32)
    u[3, 88:96] = jnp.zeros((8, 2, 8, 128), f32)
    from_left = (in32 >= 16) & (in32 < 24)
    from_right = (in32 >= 8) & (in32 < 16)
    left_ok = (jnp.zeros((2, 8, 128), jnp.int32) + col) > 0
    right_ok = (jnp.zeros((2, 8, 128), jnp.int32) + col) < 7

    def unpack(g, carry):
        gl = xr[0, g]
        gr = xr[1, g]
        for q in range(4):
            o = u[3, 4 * g + q]
            a = pltpu.roll(gl, (16 - 8 * q) % 128, 2)
            c = pltpu.roll(gr, (8 - 8 * q) % 128, 2)
            o = jnp.where(from_left, jnp.where(left_ok, a, 0.0), o)
            o = jnp.where(from_right, jnp.where(right_ok, c, 0.0), o)
            u[3, 4 * g + q] = o
            k = o[0]
            for b in range(3):
                k = jnp.where(lane[0] // 32 == b, pltpu.roll(o[0], 32 * (b + 1), 1), k)
            cb[1, 4 * g + q] = jnp.where(lane[0] < 96, k, 0.0)
        return carry

    lax.fori_loop(2, GROUPS - 2, unpack, 0)
    clear(3)

    @pl.when(row == 0)
    def _():
        cb[1, 8:16] = jnp.zeros((8, 8, 128), f32)

    @pl.when(row == 7)
    def _():
        cb[1, 80:88] = jnp.zeros((8, 8, 128), f32)

    first, last = lane == 0, lane == 127

    def solve(b):
        side = 1 if b == 3 else 0
        coef = nl[b]
        limit = cnt[b]

        def kappa(v, i):
            return cb[side, i][None] / (1.0 + coef * v * v)

        def one_step(s, carry):
            active = jnp.where(limit > s, 1.0, 0.0).astype(f32)
            begin = (9 + s) // 4
            r0 = 4 * begin
            before = u[b, r0 - 1]
            v0 = u[b, r0]
            k0 = kappa(v0, r0)
            flow0 = (k0 + kappa(before, r0 - 1)) * (v0 - before)

            def group(g, state):
                v, k, flow = state
                for q in range(4):
                    i = 4 * g + q
                    vn = u[b, i + 1]
                    kn = kappa(vn, i + 1)
                    flow_n = (k + kn) * (vn - v)
                    vr = pltpu.roll(v, 127, 2)
                    kr = pltpu.roll(k, 127, 2)
                    across = (k + kr) * (vr - v)
                    if b == 3:
                        fx[s, i] = jnp.where(in32 == 8, pltpu.roll(across, 128 - 15, 2), across)
                        came = pltpu.roll(across, 1, 2)
                    else:
                        e = pltpu.roll(fx[s, i], (120 - 32 * b) % 128, 2)
                        across = jnp.where(last, e, across)
                        came = jnp.where(first, e, pltpu.roll(across, 1, 2))
                    new = v + active * ((flow_n - flow) + (across - came))
                    u[b, i] = new
                    if b < 3:
                        snap[2 * (g % 2) + q // 2, 2 * (g // 2) - 2 + q % 2, s, 16 * b : 16 * b + 16, :] = (
                            new.reshape(16, 128).astype(bf16)
                        )
                    v, k, flow = vn, kn, flow_n
                return v, k, flow

            lax.fori_loop(begin, GROUPS - begin, group, (v0, k0, flow0))
            clear(b)
            return carry

        lax.fori_loop(0, 8, one_step, 0)

    solve(3)
    raw_copy(other + 1, 1).wait()
    turn(other + 1, 1)
    pass_round(0, 0)
    solve(0)
    pass_round(0, 1)
    pass_round(0, 2)
    solve(1)
    pass_round(0, 3)
    pass_round(1, 0)
    solve(2)

    def give_back(i, carry):
        for b in range(3):
            fs[pl.ds(b * 1280 + i, 16, stride=80), :] = u[b, i + 8].reshape(16, 128)
        return carry

    lax.fori_loop(8, 72, give_back, 0)
    out_copy = pltpu.make_async_copy(fs3.at[:, pl.ds(8, 64), :], final, loc_sem.at[2])
    out_copy.start()

    gram[...] = jnp.zeros((512, 512), f32)
    nt = (((1,), (1,)), ((), ()))

    def add_gram(t, carry):
        for h in range(2):
            x = jnp.concatenate([tr[t, 4 * h + i] for i in range(4)], axis=1)
            gram[...] += lax.dot_general(x, x, nt, preferred_element_type=f32)
        return carry

    lax.fori_loop(0, 8, add_gram, 0)
    big = gram[...].astype(bf16)
    small = (gram[...] - big.astype(f32)).astype(bf16)
    part[...] = jnp.dot(hid[...], big, preferred_element_type=f32) + jnp.dot(
        hid[...], small, preferred_element_type=f32
    )

    def square(n, total):
        x = snap[n // 16, 2 + n % 16].astype(f32).reshape(48, 8, 128)
        return total + jnp.sum(x * x, axis=0)

    squares = lax.fori_loop(0, 64, square, jnp.zeros((8, 128), f32))

    acc[...] = jnp.zeros((2, 384, 256), f32)
    for hh in range(2):
        for kk in range(4):
            if hh == 0 and kk == 0:
                pass_round(1, 1)
            if hh == 0 and kk == 2:
                pass_round(1, 2)
            if hh == 1 and kk == 0:
                pass_round(1, 3)
            fwd_copy(hh, kk).wait_recv()

            def multiply(n, carry):
                lhs = jnp.concatenate(
                    [snap[kk, 2 + 4 * n + i].reshape(384, 128) for i in range(4)], axis=1
                )
                rhs = jnp.concatenate(
                    [
                        jnp.concatenate(
                            [
                                dl[kk, 4 * n + i, 128 * hh : 128 * hh + 128, :],
                                dl[kk, 4 * n + i, 256 + 128 * hh : 384 + 128 * hh, :],
                            ],
                            axis=0,
                        )
                        for i in range(4)
                    ],
                    axis=1,
                )
                acc[hh] += lax.dot_general(lhs, rhs, nt, preferred_element_type=f32)
                return carry

            lax.fori_loop(0, 4, multiply, 0)

    total = squares
    for hh in range(2):
        for half in range(2):
            at = slice(256 * half + 128 * hh, 256 * half + 128 * hh + 128)
            a = part[:, at]
            c = acc[hh, :, 128 * half : 128 * half + 128]
            part[:, at] = a - c
            total = total + jnp.sum((hid[:, at].astype(f32) * (a - 2.0 * c)).reshape(48, 8, 128), axis=0)
    loss[...] = total

    out_copy.wait()
    for c in row_copies + col_copies:
        c.wait_send()
    for hh in range(2):
        for kk in range(4):
            for c in dec_copies(hh, kk):
                c.wait_send()
            fwd_copy(hh, kk).wait_send()


def reduce_kernel(part, loss_in, grad, loss_out, r1, q1, r2, q2, l1, l2, l3, g_stage, sem_s, sem_r):
    core, row, col = (lax.axis_index(n) for n in ("run", "row", "col"))
    x, zl = row % 4, row // 4
    y, zh = col // 2, col % 2
    spot = y * 4 + zh * 2 + zl

    def at_x(v):
        return (core, zl * 4 + v, col)

    def at_spot(p):
        return (core, (p % 2) * 4 + x, (p // 4) * 2 + (p // 2) % 2)

    xs = [(x + j) % 4 for j in range(1, 4)]
    spots = [(spot + j) % 16 for j in range(1, 16)]
    sibling = (1 - core, row, col)
    signal_all([at_x(v) for v in xs] + [at_spot(p) for p in spots] + [sibling])
    done = []

    def go(copies):
        for c in copies:
            c.start()
        done.extend(copies)

    first = [
        remote(part.at[pl.ds(pl.multiple_of(96 * v, 8), 96), :], r1.at[j], sem_s.at[j], sem_r.at[j], at_x(v))
        for j, v in enumerate(xs)
    ]
    lfirst = [
        remote(loss_in, l1.at[x], sem_s.at[3 + j], sem_r.at[3 + j], at_x(v)) for j, v in enumerate(xs)
    ]
    go(first + lfirst)
    l1[x] = loss_in[...]
    for c in first + lfirst:
        c.wait_recv()
    total = part[pl.ds(pl.multiple_of(96 * x, 8), 96), :]
    for j in range(3):
        total = total + r1[j]
    for b in range(4):
        q1[b] = total[:, 128 * b : 128 * b + 128]
    l2[spot] = (l1[0] + l1[1]) + (l1[2] + l1[3])

    def tile(ref, p):
        return ref.at[p % 4, pl.ds(pl.multiple_of(24 * (p // 4), 8), 24), :]

    second = [
        remote(tile(q1, p), r2.at[j], sem_s.at[6 + j], sem_r.at[6 + j], at_spot(p)) for j, p in enumerate(spots)
    ]
    lsecond = [
        remote(l2.at[spot], l2.at[spot], sem_s.at[21 + j], sem_r.at[21 + j], at_spot(p))
        for j, p in enumerate(spots)
    ]
    go(second + lsecond)
    for c in second + lsecond:
        c.wait_recv()
    mine = q1[spot % 4, pl.ds(pl.multiple_of(24 * (spot // 4), 8), 24), :]
    for j in range(15):
        mine = mine + r2[j]
    q2[spot % 4, pl.ds(pl.multiple_of(24 * (spot // 4), 8), 24), :] = mine * (1.0 / 768.0)
    lsum = l2[0]
    for p in range(1, 16):
        lsum = lsum + l2[p]
    l3[core] = lsum

    third = [
        remote(tile(q2, spot), tile(q2, spot), sem_s.at[36 + j], sem_r.at[36 + j], at_spot(p))
        for j, p in enumerate(spots)
    ]
    lthird = [remote(l3.at[core], l3.at[core], sem_s.at[51], sem_r.at[51], sibling)]
    go(third + lthird)
    for c in third:
        c.wait_recv()
    for b in range(4):
        g_stage[core, x, :, 128 * b : 128 * b + 128] = q2[b].astype(bf16)

    def block(c, v):
        return g_stage.at[c, v]

    fourth = [
        remote(block(core, x), block(core, x), sem_s.at[52 + j], sem_r.at[52 + j], at_x(v)) for j, v in enumerate(xs)
    ]
    cross = [
        remote(block(core, v), block(core, v), sem_s.at[55 + j], sem_r.at[55 + j], sibling)
        for j, v in enumerate([x] + [(x + 4 - j) % 4 for j in range(1, 4)])
    ]
    go(fourth + cross[:1])
    for j in range(3):
        fourth[j].wait_recv()
        go([cross[1 + j]])
    for c in cross + lthird:
        c.wait_recv()
    grad[...] = g_stage[...].reshape(768, 512)
    loss_out[...] = l3[0] + l3[1]
    for c in done:
        c.wait_send()


def spread(values):
    three = values.reshape(3, 16)
    wide = jnp.broadcast_to(three[:, :, None], (3, 16, 128))
    edge = jnp.concatenate(
        [jnp.broadcast_to(three[b][:, None], (16, 32)) for b in range(3)] + [jnp.zeros((16, 32), values.dtype)],
        axis=1,
    )
    return jnp.concatenate([wide, edge[None]], axis=0).reshape(4, 2, 8, 128)


def per_device(
    init_field, conduct, nonlin, counts, descriptors, time_code, w_in, bias_in, w_out, decoder
):
    core = lax.axis_index("run")
    col = lax.axis_index("col")
    wide = descriptors.astype(f32).reshape(2, 1, 48, 256) + time_code.astype(f32).reshape(1, 8, 1, 256)
    rows_in = wide.astype(bf16).reshape(768, 256)
    pre = jnp.dot(rows_in, w_in, preferred_element_type=f32) + bias_in
    act = jax.nn.gelu(pre).astype(bf16)
    hidden = jnp.dot(act, w_out, preferred_element_type=f32).astype(bf16)
    hid = lax.dynamic_slice_in_dim(hidden, core * 384, 384, 0)

    lanes = jnp.arange(128) % 32
    outside = ((lanes >= 16) & (lanes < 24) & (col == 0)) | ((lanes >= 8) & (lanes < 16) & (col == 7))
    cnt = spread(counts)
    cnt = cnt.at[3].set(jnp.where(outside[None, None, :], 0, cnt[3]))
    vmem = pl.BlockSpec(memory_space=pltpu.VMEM)
    hbm = pl.BlockSpec(memory_space=pl.ANY)
    dma = pltpu.SemaphoreType.DMA
    final, part, loss = pl.pallas_call(
        main_kernel,
        name="solve_and_learn",
        out_shape=(
            jax.ShapeDtypeStruct((48, 64, 128), f32),
            jax.ShapeDtypeStruct((384, 512), f32),
            jax.ShapeDtypeStruct((8, 128), f32),
        ),
        in_specs=[hbm, hbm, vmem, vmem, hbm, vmem],
        out_specs=(hbm, vmem, vmem),
        scratch_shapes=[
            pltpu.VMEM((3840, 128), f32),
            pltpu.VMEM((80, 128), f32),
            pltpu.VMEM((4, ROWS, 2, 8, 128), f32),
            pltpu.VMEM((2, ROWS, 8, 128), f32),
            pltpu.VMEM((2, GROUPS, 2, 8, 128), f32),
            pltpu.VMEM((2, GROUPS, 2, 8, 128), f32),
            pltpu.VMEM((8, ROWS, 2, 8, 128), f32),
            pltpu.VMEM((4, 20, 8, 48, 128), bf16),
            pltpu.VMEM((8, 8, 512, 128), bf16),
            pltpu.VMEM((4, 16, 512, 128), bf16),
            pltpu.VMEM((2, 1024, 1024), bf16),
            pltpu.VMEM((8, 256, 128), f32),
            pltpu.VMEM((512, 512), f32),
            pltpu.VMEM((2, 384, 256), f32),
            dma((3,)), dma((2,)), dma((4,)), dma((4,)), dma((2,)), dma((2,)),
            dma((8, 7)), dma((8, 7)), dma((8,)), dma((8,)), dma((8,)),
        ],
        compiler_params=pltpu.CompilerParams(
            collective_id=0, has_side_effects=True, vmem_limit_bytes=VMEM_ALL - (1 << 16)
        ),
    )(init_field, conduct, spread(nonlin), cnt, decoder.reshape(4096, 1024), hid)

    grad, loss_sum = pl.pallas_call(
        reduce_kernel,
        name="reduce_grad",
        out_shape=(jax.ShapeDtypeStruct((768, 512), bf16), jax.ShapeDtypeStruct((8, 128), f32)),
        in_specs=[vmem, vmem],
        out_specs=(vmem, vmem),
        scratch_shapes=[
            pltpu.VMEM((3, 96, 512), f32),
            pltpu.VMEM((4, 96, 128), f32),
            pltpu.VMEM((15, 24, 128), f32),
            pltpu.VMEM((4, 96, 128), f32),
            pltpu.VMEM((4, 8, 128), f32),
            pltpu.VMEM((16, 8, 128), f32),
            pltpu.VMEM((2, 8, 128), f32),
            pltpu.VMEM((2, 4, 96, 512), bf16),
            dma((60,)), dma((60,)),
        ],
        compiler_params=pltpu.CompilerParams(collective_id=1, has_side_effects=True),
    )(part, loss)

    grad_out = lax.dot_general(act, grad, (((0,), (0,)), ((), ())), preferred_element_type=f32)
    back = lax.dot_general(grad, w_out, (((1,), (1,)), ((), ())), preferred_element_type=f32)
    _, pull = jax.vjp(jax.nn.gelu, pre)
    grad_pre = pull(back)[0]
    grad_in = lax.dot_general(
        rows_in, grad_pre.astype(bf16), (((0,), (0,)), ((), ())), preferred_element_type=f32
    )
    new_w_in = w_in.astype(f32) - RATE * grad_in
    new_bias = bias_in - RATE * jnp.sum(grad_pre, axis=0)
    new_w_out = w_out.astype(f32) - RATE * grad_out
    mean_loss = jnp.sum(loss_sum) / (768 * 512 * 1024)
    return final, new_w_in, new_bias, new_w_out, mean_loss


def solution(mesh):
    in_specs = (
        P("run", "row", "col"), P("row", "col"), P("run"), P("run"), P(), P(), P(), P(), P(),
        P(None, ("row", "col"), None),
    )
    out_specs = (P("run", "row", "col"), P(), P(), P(), P())
    return jax.shard_map(
        per_device, mesh=mesh, in_specs=in_specs, out_specs=out_specs, check_vma=False
    )
```

time: 424 us -> 238 us (0.56); the launches traced: 418 us -> 237 us
  Pallas kernels: 0 us -> 215 us
  other arithmetic: 99.3 us -> 3.61 us
  starting transfers between devices: 93.6 us -> 0 us
  local copies, waits for them, and re-layouts: 86.9 us -> 7.73 us
  blocking collectives: 59.5 us -> 0 us
  waiting for transfers between devices: 42.6 us -> 0 us
  matrix products: 33.4 us -> 8.32 us
    pallas_call x0 -> x2, Pallas kernels: none -> 215 us  [the longest x1 175 us: per_device(): pl.pallas_call(main_kernel, name='solve_and_learn', out_shape=(jax.ShapeD...]
    ppermute x12 -> x0, starting transfers between devices: 85.7 us -> none  [the longest x6 78 us: extended(): lax.ppermute(lax.slice_in_dim(block, block.shape[dim] - width, None, axis...]
    all_to_all x3 -> x0, blocking collectives: 59.5 us -> none  [the longest x2 32.6 us: from_everyone(): return lax.all_to_all(copies, axis, split_axis=0, concat_axis=0, tiled=True)]
    div x8 -> x0, other arithmetic: 54.8 us -> none  [advance(): kappa = cond_pad[None] / (1.0 + nonlin[:, None, None] * padded * padded)]
    ppermute x12 -> x0, waiting for transfers between devices: 42.6 us -> none  [the longest x6 22.3 us: extended(): lax.ppermute(lax.slice_in_dim(block, 0, width, axis=dim), axis, backward)]
    dot_general x6 -> x5, matrix products: 33.4 us -> 8.32 us  [the longest x1 3.41 us: per_device(): lax.dot_general(grad, w_out, (((1,), (1,)), ((), ())), preferred_element_...]
    unnamed x86 -> x25, local copies, waits for them, and re-layouts: 23.8 us -> 3.06 us
    slice x22 -> x2, local copies, waits for them, and re-layouts: 18.1 us -> 1.68 us  [spread(): three[b][:, None]]
  transfers between devices with their start and end apart: 13 -> 0, of which waited for: 3 -> 0; matrix products, arithmetic and copies ran while one was open for 33% -> 0% of each run, Pallas kernels for 0% -> 0%
where the time goes in v1:
time: 238 us; the launch traced here: 237 us
  Pallas kernels  215 us (90%)
  matrix products  8.32 us (3%)
  local copies, waits for them, and re-layouts  7.73 us (3%)
  other arithmetic  3.61 us (2%)
  between operations  2.59 us (1%)
    pallas_call x1, Pallas kernels, per_device(): pl.pallas_call(main_kernel, name='solve_and_learn', out_shape=(jax.ShapeD...  175 us
    pallas_call x1, Pallas kernels, per_device(): pl.pallas_call(reduce_kernel, name='reduce_grad', out_shape=(jax.ShapeDty...  40.4 us

profile of v1, /device:TPU:1, one launch (start us, length us, event | category | flops | bytes accessed | tf_op | source)
XLA Modules:
  0.0 237.3 jit_solution(16645535999415661846)
XLA Ops:
  0.6 0.8 fusion.13
  1.5 0.1 broadcast_in_dim.70
  1.5 0.1 broadcast_in_dim.69
  1.6 0.1 broadcast_in_dim.68
  1.7 0.1 pad.13.clone
  1.8 0.1 maximum_bitcast_fusion
  1.8 0.7 broadcast_in_dim.36
  2.6 0.1 broadcast_in_dim.37
  2.7 0.6 pad_maximum_fusion.nl
  3.3 0.8 fusion.12
  4.1 0.1 broadcast_in_dim.76
  4.2 0.1 broadcast_in_dim.75
  4.3 0.1 pad.7.clone
  4.4 0.1 add_bitcast_fusion
  4.5 0.7 broadcast_in_dim.72
  5.2 0.1 broadcast_in_dim.73
  5.3 0.1 select_dynamic-update-slice_fusion.cnt
  5.4 0.7 convert_element_type.26
  6.1 0.8 convert.1
  7.0 0.7 copy-done
  7.7 1.3 convolution_add_fusion
  9.1 1.1 copy-done.2
  10.2 0.7 fusion.9
  10.9 0.8 dynamic-slice_convert_fusion.hid
  11.6 174.6 %solve_and_learn.1 = (f32[48,64,128]{2,1,0:T(8,128)}, f32[384,512]{1,0:T(8,128)}, f32[8,128]{1,0:T(8,128)}) custom-call(f32[48,64,128]{2,1,0:T(8,128)} %field.1, f32[64,128]{1,0:T(8,128)} %conduct.1, f32[4,2,8,128]{3,2,1,0:T(8,128)} %pad_maximum_fusion.nl, s32[4,2,8,128]{3,2,1,0:T(8,128)} %copy-done.6, bf16[4096,1024]{1,0:T(8,128)(2,1)} %bitcast.18, ...), custom_call_target="tpu_custom_call" | custom-call | tf_op jit(solution)/shard_map/solve_and_learn/pallas_call | solution.py:514
  186.3 40.4 %reduce_grad.1 = (bf16[768,512]{1,0:T(8,128)(2,1)}, f32[8,128]{1,0:T(8,128)}) custom-call(f32[384,512]{1,0:T(8,128)} %get-tuple-element.23.part, f32[8,128]{1,0:T(8,128)} %get-tuple-element.24.loss_in), custom_call_target="tpu_custom_call" | custom-call | tf_op jit(solution)/shard_map/reduce_grad/pallas_call | solution.py:547
  226.7 3.4 %fusion.10 = (f32[512]{0:T(512)S(1)}, bf16[768,512]{1,0:T(8,128)(2,1)S(1)}) fusion(f32[768,512]{1,0:T(8,128)} %copy-done.2, bf16[768,512]{1,0:T(8,128)(2,1)} %get-tuple-element.25, bf16[512,512]{1,0:T(8,128)(2,1)} %param.20), kind=kOutput, calls=%fused_computation.26 | convolution fusion | flops 410910208 | bytes 3672064 | tf_op jit(solution)/shard_map/dot_general | solution.py:568
  230.2 1.2 fusion.7
  231.4 0.6 multiply_subtract_fusion
  232.0 1.8 fusion.6
  233.7 0.6 reduce_sum.19
  235.0 1.1 copy.17
  (28 shorter events, 0.2 us)
Async XLA Ops:
  2.7 7.5 %copy-start.10 = (bf16[512,512]{1,0:T(8,128)(2,1)S(1)}, bf16[512,512]{1,0:T(8,128)(2,1)}, u32[]{:S(2)}) copy-start(bf16[512,512]{1,0:T(8,128)(2,1)} %param.20) | copy-start | bytes 1572868
  5.4 1.6 copy-start.6
  7.0 0.7 copy-start
  9.0 1.1 copy-start.2
  226.7 3.5 %copy-start.1 = (bf16[2,8,48,256]{3,2,1,0:T(8,128)(2,1)S(1)}, bf16[2,8,48,256]{3,2,1,0:T(8,128)(2,1)}, u32[]{:S(2)}) copy-start(bf16[2,8,48,256]{3,2,1,0:T(8,128)(2,1)} %copy-done) | copy-start | bytes 1179652
  226.7 3.5 %copy-start.5 = (bf16[256,512]{1,0:T(8,128)(2,1)S(1)}, bf16[256,512]{1,0:T(8,128)(2,1)}, u32[]{:S(2)}) copy-start(bf16[256,512]{1,0:T(8,128)(2,1)} %param.18) | copy-start | bytes 786436
  226.7 5.3 %copy-start.9 = (bf16[768,512]{1,0:T(8,128)(2,1)S(1)}, bf16[768,512]{1,0:T(8,128)(2,1)}, u32[]{:S(2)}) copy-start(bf16[768,512]{1,0:T(8,128)(2,1)} %get-tuple-element.25) | copy-start | bytes 2359300
  226.7 5.2 %copy-start.11 = (bf16[512,512]{1,0:T(8,128)(2,1)S(1)}, bf16[512,512]{1,0:T(8,128)(2,1)}, u32[]{:S(2)}) copy-start(bf16[512,512]{1,0:T(8,128)(2,1)} %param.20) | copy-start | bytes 1572868
  230.1 1.2 copy-start.7
  230.1 1.8 copy-start.3
  232.0 1.8 copy-start.8
  232.0 3.0 %copy-start.4 = (f32[48,64,128]{2,1,0:T(8,128)S(1)}, f32[48,64,128]{2,1,0:T(8,128)}, u32[]{:S(2)}) copy-start(f32[48,64,128]{2,1,0:T(8,128)} %get-tuple-element.42) | copy-start | bytes 4718596

commit v2 on v1

--- a/solution.py
+++ b/solution.py
@@ -30,7 +30,7 @@
 def main_kernel(
     field, conduct, nl, cnt, decoder, hid,
     final, part, loss,
-    fs, cd, u, cb, xs, xr, fx, snap, tr, dl, raw, tf, gram, acc,
+    fs, cd, u, cb, xs, xr, fx, ks, ac, snap, tr, dl, raw, tf, gram, acc,
     loc_sem, raw_sem, row_send, row_recv, col_send, col_recv, dec_send, dec_recv, own_sem, fwd_send, fwd_recv,
 ):
     core, row, col = (lax.axis_index(n) for n in ("run", "row", "col"))
@@ -134,7 +134,7 @@
         return carry
 
     lax.fori_loop(0, 80, fill, 0)
-    for s in (0, 1):
+    for s in range(4):
         cb[s, 0:8] = jnp.zeros((8, 8, 128), f32)
         cb[s, 88:96] = jnp.zeros((8, 8, 128), f32)
 
@@ -225,7 +225,7 @@
             k = o[0]
             for b in range(3):
                 k = jnp.where(lane[0] // 32 == b, pltpu.roll(o[0], 32 * (b + 1), 1), k)
-            cb[1, 4 * g + q] = jnp.where(lane[0] < 96, k, 0.0)
+            cb[2, 4 * g + q] = jnp.where(lane[0] < 96, k, 0.0)
         return carry
 
     lax.fori_loop(2, GROUPS - 2, unpack, 0)
@@ -233,74 +233,119 @@
 
     @pl.when(row == 0)
     def _():
-        cb[1, 8:16] = jnp.zeros((8, 8, 128), f32)
+        cb[2, 8:16] = jnp.zeros((8, 8, 128), f32)
 
     @pl.when(row == 7)
     def _():
-        cb[1, 80:88] = jnp.zeros((8, 8, 128), f32)
-
+        cb[2, 80:88] = jnp.zeros((8, 8, 128), f32)
+
+    def shift_conduct(g, carry):
+        for q in range(4):
+            for side in (0, 2):
+                cb[side + 1, 4 * g + q] = pltpu.roll(cb[side, 4 * g + q], 127, 1)
+        return carry
+
+    lax.fori_loop(2, GROUPS - 2, shift_conduct, 0)
     first, last = lane == 0, lane == 127
 
-    def solve(b):
-        side = 1 if b == 3 else 0
-        coef = nl[b]
-        limit = cnt[b]
-
-        def kappa(v, i):
-            return cb[side, i][None] / (1.0 + coef * v * v)
+    def solve(blocks, size, after_step=None):
+        edge = blocks == (3,)
+        side = 2 if edge else 0
+        per = 8 // size
+        coef = [nl[b] for b in blocks]
+
+        def kappa(v, i, n, shifted=0):
+            return cb[side + shifted, i][None] / (1.0 + coef[n] * v * v)
 
         def one_step(s, carry):
-            active = jnp.where(limit > s, 1.0, 0.0).astype(f32)
-            begin = (9 + s) // 4
-            r0 = 4 * begin
-            before = u[b, r0 - 1]
-            v0 = u[b, r0]
-            k0 = kappa(v0, r0)
-            flow0 = (k0 + kappa(before, r0 - 1)) * (v0 - before)
-
-            def group(g, state):
-                v, k, flow = state
-                for q in range(4):
-                    i = 4 * g + q
-                    vn = u[b, i + 1]
-                    kn = kappa(vn, i + 1)
-                    flow_n = (k + kn) * (vn - v)
+            active = [jnp.where(cnt[b] > s, 1.0, 0.0).astype(f32) for b in blocks]
+            begin = (9 + s) // size
+            r0 = size * begin
+
+            def ahead(i, vs):
+                out = []
+                for n, b in enumerate(blocks):
+                    v = vs[n]
+                    k = kappa(v, i, n)
                     vr = pltpu.roll(v, 127, 2)
-                    kr = pltpu.roll(k, 127, 2)
-                    across = (k + kr) * (vr - v)
-                    if b == 3:
-                        fx[s, i] = jnp.where(in32 == 8, pltpu.roll(across, 128 - 15, 2), across)
-                        came = pltpu.roll(across, 1, 2)
-                    else:
-                        e = pltpu.roll(fx[s, i], (120 - 32 * b) % 128, 2)
-                        across = jnp.where(last, e, across)
-                        came = jnp.where(first, e, pltpu.roll(across, 1, 2))
-                    new = v + active * ((flow_n - flow) + (across - came))
-                    u[b, i] = new
-                    if b < 3:
-                        snap[2 * (g % 2) + q // 2, 2 * (g // 2) - 2 + q % 2, s, 16 * b : 16 * b + 16, :] = (
-                            new.reshape(16, 128).astype(bf16)
-                        )
-                    v, k, flow = vn, kn, flow_n
-                return v, k, flow
-
-            lax.fori_loop(begin, GROUPS - begin, group, (v0, k0, flow0))
-            clear(b)
+                    across = (k + kappa(vr, i, n, 1)) * (vr - v)
+                    if not edge:
+                        across = jnp.where(last, fx[b, s, i], across)
+                    out.append((k, across))
+                return out
+
+            def keep(g, q, made):
+                for n, (k, across) in enumerate(made):
+                    ks[n, (g % 2) * size + q] = k
+                    ac[n, (g % 2) * size + q] = across
+
+            flows = []
+            for q in range(size):
+                vs = [u[b, r0 + q] for b in blocks]
+                made = ahead(r0 + q, vs)
+                keep(begin, q, made)
+                if q == 0:
+                    for n, b in enumerate(blocks):
+                        before = u[b, r0 - 1]
+                        flows.append((made[n][0] + kappa(before, r0 - 1, n)) * (vs[n] - before))
+
+            def group(g, flow):
+                flow = list(flow)
+                base, now = size * g, (g % 2) * size
+                count = range(len(blocks))
+                v = [[u[b, base + q] for b in blocks] for q in range(size)]
+                k = [[ks[n, now + q] for n in count] for q in range(size)]
+                a = [[ac[n, now + q] for n in count] for q in range(size)]
+                v_next = [[u[b, base + size + q] for b in blocks] for q in range(size)]
+                made = [ahead(base + size + q, v_next[q]) for q in range(size)]
+                for q in range(size):
+                    for n, b in enumerate(blocks):
+                        vn = v[q + 1][n] if q + 1 < size else v_next[0][n]
+                        kn = k[q + 1][n] if q + 1 < size else made[0][n][0]
+                        flow_n = (k[q][n] + kn) * (vn - v[q][n])
+                        came = pltpu.roll(a[q][n], 1, 2)
+                        if edge:
+                            f = jnp.where(in32 == 8, pltpu.roll(a[q][n], 113, 2), a[q][n])
+                            for to in range(3):
+                                fx[to, s, base + q] = pltpu.roll(f, 120 - 32 * to, 2)
+                        else:
+                            came = jnp.where(first, fx[b, s, base + q], came)
+                        new = v[q][n] + active[n] * ((flow_n - flow[n]) + (a[q][n] - came))
+                        u[b, base + q] = new
+                        if not edge:
+                            snap[
+                                size * (g % per) // 2 + q // 2, 2 * (g // per) - 2 + q % 2, s, 16 * b : 16 * b + 16, :
+                            ] = new.reshape(16, 128).astype(bf16)
+                        flow[n] = flow_n
+                for q in range(size):
+                    keep(g + 1, q, made[q])
+                return tuple(flow)
+
+            lax.fori_loop(begin, ROWS // size - begin, group, tuple(flows))
+            for b in blocks:
+                clear(b)
+            if after_step is not None:
+                after_step(s)
             return carry
 
         lax.fori_loop(0, 8, one_step, 0)
 
-    solve(3)
+    solve((3,), 8)
     raw_copy(other + 1, 1).wait()
     turn(other + 1, 1)
     pass_round(0, 0)
-    solve(0)
     pass_round(0, 1)
     pass_round(0, 2)
-    solve(1)
-    pass_round(0, 3)
-    pass_round(1, 0)
-    solve(2)
+
+    def pass_at(s):
+        for at, hh, kk in ((2, 0, 3), (4, 1, 0), (6, 1, 1)):
+
+            @pl.when(s == at)
+            def _():
+                pass_round(hh, kk)
+
+    solve((0, 1, 2), 4, pass_at)
+    pass_round(1, 2)
 
     def give_back(i, carry):
         for b in range(3):
@@ -315,12 +360,14 @@
     nt = (((1,), (1,)), ((), ()))
 
     def add_gram(t, carry):
-        for h in range(2):
-            x = jnp.concatenate([tr[t, 4 * h + i] for i in range(4)], axis=1)
-            gram[...] += lax.dot_general(x, x, nt, preferred_element_type=f32)
+        x = jnp.concatenate([tr[t, i] for i in range(8)], axis=1)
+        gram[0:256] += lax.dot_general(x[0:256], x, nt, preferred_element_type=f32)
+        gram[256:512, 256:512] += lax.dot_general(x[256:512], x[256:512], nt, preferred_element_type=f32)
         return carry
 
     lax.fori_loop(0, 8, add_gram, 0)
+    pass_round(1, 3)
+    gram[256:512, 0:256] = gram[0:256, 256:512].T
     big = gram[...].astype(bf16)
     small = (gram[...] - big.astype(f32)).astype(bf16)
     part[...] = jnp.dot(hid[...], big, preferred_element_type=f32) + jnp.dot(
@@ -333,38 +380,26 @@
 
     squares = lax.fori_loop(0, 64, square, jnp.zeros((8, 128), f32))
 
-    acc[...] = jnp.zeros((2, 384, 256), f32)
     for hh in range(2):
         for kk in range(4):
-            if hh == 0 and kk == 0:
-                pass_round(1, 1)
-            if hh == 0 and kk == 2:
-                pass_round(1, 2)
-            if hh == 1 and kk == 0:
-                pass_round(1, 3)
             fwd_copy(hh, kk).wait_recv()
 
-            def multiply(n, carry):
-                lhs = jnp.concatenate(
-                    [snap[kk, 2 + 4 * n + i].reshape(384, 128) for i in range(4)], axis=1
-                )
-                rhs = jnp.concatenate(
-                    [
-                        jnp.concatenate(
-                            [
-                                dl[kk, 4 * n + i, 128 * hh : 128 * hh + 128, :],
-                                dl[kk, 4 * n + i, 256 + 128 * hh : 384 + 128 * hh, :],
-                            ],
-                            axis=0,
-                        )
-                        for i in range(4)
-                    ],
-                    axis=1,
-                )
-                acc[hh] += lax.dot_general(lhs, rhs, nt, preferred_element_type=f32)
-                return carry
-
-            lax.fori_loop(0, 4, multiply, 0)
+            lhs = jnp.concatenate([snap[kk, 2 + i].reshape(384, 128) for i in range(16)], axis=1)
+            rhs = jnp.concatenate(
+                [
+                    jnp.concatenate(
+                        [
+                            dl[kk, i, 128 * hh : 128 * hh + 128, :],
+                            dl[kk, i, 256 + 128 * hh : 384 + 128 * hh, :],
+                        ],
+                        axis=0,
+                    )
+                    for i in range(16)
+                ],
+                axis=1,
+            )
+            got = lax.dot_general(lhs, rhs, nt, preferred_element_type=f32)
+            acc[hh] = got if kk == 0 else acc[hh] + got
 
     total = squares
     for hh in range(2):
@@ -525,10 +560,12 @@
             pltpu.VMEM((3840, 128), f32),
             pltpu.VMEM((80, 128), f32),
             pltpu.VMEM((4, ROWS, 2, 8, 128), f32),
-            pltpu.VMEM((2, ROWS, 8, 128), f32),
+            pltpu.VMEM((4, ROWS, 8, 128), f32),
             pltpu.VMEM((2, GROUPS, 2, 8, 128), f32),
             pltpu.VMEM((2, GROUPS, 2, 8, 128), f32),
-            pltpu.VMEM((8, ROWS, 2, 8, 128), f32),
+            pltpu.VMEM((3, 8, ROWS, 2, 8, 128), f32),
+            pltpu.VMEM((3, 16, 2, 8, 128), f32),
+            pltpu.VMEM((3, 16, 2, 8, 128), f32),
             pltpu.VMEM((4, 20, 8, 48, 128), bf16),
             pltpu.VMEM((8, 8, 512, 128), bf16),
             pltpu.VMEM((4, 16, 512, 128), bf16),

time: 238 us -> 178 us (0.75)
  Pallas kernels: 215 us -> 155 us
    pallas_call x1, Pallas kernels: 175 us -> 114 us  [per_device(): pl.pallas_call(main_kernel, name='solve_and_learn', out_shape=(jax.ShapeD...]
where the time goes in v2:
time: 178 us
  Pallas kernels  155 us (87%)
  matrix products  8.32 us (5%)
  local copies, waits for them, and re-layouts  7.73 us (4%)
  other arithmetic  3.61 us (2%)
  between operations  2.59 us (1%)
    pallas_call x1, Pallas kernels, per_device(): pl.pallas_call(main_kernel, name='solve_and_learn', out_shape=(jax.ShapeD...  114 us
    pallas_call x1, Pallas kernels, per_device(): pl.pallas_call(reduce_kernel, name='reduce_grad', out_shape=(jax.ShapeDty...  40.9 us

profile of v2, /device:TPU:1, one launch (start us, length us, event | category | flops | bytes accessed | tf_op | source)
XLA Modules:
  0.0 177.6 jit_solution(2112108936271407853)
XLA Ops:
  0.6 0.8 fusion.13
  1.5 0.1 broadcast_in_dim.70
  1.5 0.1 broadcast_in_dim.69
  1.6 0.1 broadcast_in_dim.68
  1.7 0.1 pad.13.clone
  1.8 0.1 maximum_bitcast_fusion
  1.8 0.7 broadcast_in_dim.36
  2.6 0.1 broadcast_in_dim.37
  2.7 0.6 pad_maximum_fusion.nl
  3.3 0.8 fusion.12
  4.1 0.1 broadcast_in_dim.76
  4.2 0.1 broadcast_in_dim.75
  4.3 0.1 pad.7.clone
  4.4 0.1 add_bitcast_fusion
  4.5 0.7 broadcast_in_dim.72
  5.2 0.1 broadcast_in_dim.73
  5.3 0.1 select_dynamic-update-slice_fusion.cnt
  5.4 0.7 convert_element_type.26
  6.1 0.8 convert.1
  7.0 0.7 copy-done
  7.7 1.3 convolution_add_fusion
  9.1 1.1 copy-done.2
  10.2 0.7 fusion.9
  10.9 0.8 dynamic-slice_convert_fusion.hid
  11.6 114.4 %solve_and_learn.1 = (f32[48,64,128]{2,1,0:T(8,128)}, f32[384,512]{1,0:T(8,128)}, f32[8,128]{1,0:T(8,128)}) custom-call(f32[48,64,128]{2,1,0:T(8,128)} %field.1, f32[64,128]{1,0:T(8,128)} %conduct.1, f32[4,2,8,128]{3,2,1,0:T(8,128)} %pad_maximum_fusion.nl, s32[4,2,8,128]{3,2,1,0:T(8,128)} %copy-done.6, bf16[4096,1024]{1,0:T(8,128)(2,1)} %bitcast.18, ...), custom_call_target="tpu_custom_call" | custom-call | tf_op jit(solution)/shard_map/solve_and_learn/pallas_call | solution.py:549
  126.0 40.9 %reduce_grad.1 = (bf16[768,512]{1,0:T(8,128)(2,1)}, f32[8,128]{1,0:T(8,128)}) custom-call(f32[384,512]{1,0:T(8,128)} %get-tuple-element.23.part, f32[8,128]{1,0:T(8,128)} %get-tuple-element.24.loss_in), custom_call_target="tpu_custom_call" | custom-call | tf_op jit(solution)/shard_map/reduce_grad/pallas_call | solution.py:584
  167.0 3.4 %fusion.10 = (f32[512]{0:T(512)S(1)}, bf16[768,512]{1,0:T(8,128)(2,1)S(1)}) fusion(f32[768,512]{1,0:T(8,128)} %copy-done.2, bf16[768,512]{1,0:T(8,128)(2,1)} %get-tuple-element.25, bf16[512,512]{1,0:T(8,128)(2,1)} %param.20), kind=kOutput, calls=%fused_computation.26 | convolution fusion | flops 410910208 | bytes 3672064 | tf_op jit(solution)/shard_map/dot_general | solution.py:605
  170.5 1.2 fusion.7
  171.7 0.6 multiply_subtract_fusion
  172.3 1.8 fusion.6
  174.0 0.6 reduce_sum.19
  175.3 1.1 copy.17
  (28 shorter events, 0.2 us)
Async XLA Ops:
  2.7 7.5 %copy-start.10 = (bf16[512,512]{1,0:T(8,128)(2,1)S(1)}, bf16[512,512]{1,0:T(8,128)(2,1)}, u32[]{:S(2)}) copy-start(bf16[512,512]{1,0:T(8,128)(2,1)} %param.20) | copy-start | bytes 1572868
  5.4 1.6 copy-start.6
  7.0 0.7 copy-start
  9.0 1.1 copy-start.2
  167.0 3.5 %copy-start.1 = (bf16[2,8,48,256]{3,2,1,0:T(8,128)(2,1)S(1)}, bf16[2,8,48,256]{3,2,1,0:T(8,128)(2,1)}, u32[]{:S(2)}) copy-start(bf16[2,8,48,256]{3,2,1,0:T(8,128)(2,1)} %copy-done) | copy-start | bytes 1179652
  167.0 3.5 %copy-start.5 = (bf16[256,512]{1,0:T(8,128)(2,1)S(1)}, bf16[256,512]{1,0:T(8,128)(2,1)}, u32[]{:S(2)}) copy-start(bf16[256,512]{1,0:T(8,128)(2,1)} %param.18) | copy-start | bytes 786436
  167.0 5.3 %copy-start.9 = (bf16[768,512]{1,0:T(8,128)(2,1)S(1)}, bf16[768,512]{1,0:T(8,128)(2,1)}, u32[]{:S(2)}) copy-start(bf16[768,512]{1,0:T(8,128)(2,1)} %get-tuple-element.25) | copy-start | bytes 2359300
  167.0 5.2 %copy-start.11 = (bf16[512,512]{1,0:T(8,128)(2,1)S(1)}, bf16[512,512]{1,0:T(8,128)(2,1)}, u32[]{:S(2)}) copy-start(bf16[512,512]{1,0:T(8,128)(2,1)} %param.20) | copy-start | bytes 1572868
  170.4 1.2 copy-start.7
  170.4 1.8 %copy-start.3 = (f32[768,512]{1,0:T(8,128)S(1)}, f32[768,512]{1,0:T(8,128)}, u32[]{:S(2)}) copy-start(f32[768,512]{1,0:T(8,128)} %copy-done.2) | copy-start | bytes 4718596
  172.2 1.8 copy-start.8
  172.2 3.0 %copy-start.4 = (f32[48,64,128]{2,1,0:T(8,128)S(1)}, f32[48,64,128]{2,1,0:T(8,128)}, u32[]{:S(2)}) copy-start(f32[48,64,128]{2,1,0:T(8,128)} %get-tuple-element.42) | copy-start | bytes 4718596

commit v3 on v2

--- a/solution.py
+++ b/solution.py
@@ -30,7 +30,7 @@
 def main_kernel(
     field, conduct, nl, cnt, decoder, hid,
     final, part, loss,
-    fs, cd, u, cb, xs, xr, fx, ks, ac, snap, tr, dl, raw, tf, gram, acc,
+    fs, cd, u, cb, rs, rr, xs, xr, fx, ks, ac, snap, tr, dl, raw, tf, gram, acc,
     loc_sem, raw_sem, row_send, row_recv, col_send, col_recv, dec_send, dec_recv, own_sem, fwd_send, fwd_recv,
 ):
     core, row, col = (lax.axis_index(n) for n in ("run", "row", "col"))
@@ -41,15 +41,17 @@
     targets = [((y + dy) % 4) * 2 + (zh + dz) % 2 for dy, dz in OFFSETS]
     signal_all([(core, row, t) for t in targets] + [up, down, sibling])
 
-    fs3 = fs.reshape(48, 80, 128)
+    fs3 = fs.reshape(48, 64, 128)
     row_copies = [
-        remote(field.at[:, pl.ds(56, 8), :], fs3.at[:, pl.ds(0, 8), :], row_send.at[0], row_recv.at[0], down),
-        remote(field.at[:, pl.ds(0, 8), :], fs3.at[:, pl.ds(72, 8), :], row_send.at[1], row_recv.at[1], up),
+        remote(rs.at[0], rr.at[0], row_send.at[0], row_recv.at[0], down),
+        remote(rs.at[1], rr.at[1], row_send.at[1], row_recv.at[1], up),
+    ]
+    edge_copies = [
         remote(conduct.at[pl.ds(56, 8), :], cd.at[pl.ds(0, 8), :], row_send.at[2], row_recv.at[2], down),
         remote(conduct.at[pl.ds(0, 8), :], cd.at[pl.ds(72, 8), :], row_send.at[3], row_recv.at[3], up),
     ]
     loc_copies = [
-        pltpu.make_async_copy(field, fs3.at[:, pl.ds(8, 64), :], loc_sem.at[0]),
+        pltpu.make_async_copy(field, fs3, loc_sem.at[0]),
         pltpu.make_async_copy(conduct, cd.at[pl.ds(8, 64), :], loc_sem.at[1]),
     ]
 
@@ -110,7 +112,7 @@
         own_copy(hh, kk).wait()
         fwd_copy(hh, kk).start()
 
-    for c in row_copies + loc_copies:
+    for c in loc_copies + edge_copies:
         c.start()
     raw_copy(mine, 0).start()
     raw_copy(mine + 1, 1).start()
@@ -121,19 +123,50 @@
 
     for c in loc_copies:
         c.wait()
-    for c in row_copies:
-        c.wait_recv()
     for b in range(3):
         u[b, 0:8] = jnp.zeros((8, 2, 8, 128), f32)
         u[b, 88:96] = jnp.zeros((8, 2, 8, 128), f32)
 
-    def fill(i, carry):
+    def fill(n, carry):
+        for q in range(4):
+            i = 4 * n + q
+            for b in range(3):
+                u[b, i + 16] = fs[pl.ds(b * 1024 + i, 16, stride=64), :].reshape(2, 8, 128)
+        return carry
+
+    lax.fori_loop(0, 16, fill, 0)
+
+    def pack_rows(i, carry):
         for b in range(3):
-            u[b, i + 8] = fs[pl.ds(b * 1280 + i, 16, stride=80), :].reshape(2, 8, 128)
-        cb[0, i + 8] = jnp.broadcast_to(cd[pl.ds(i, 1), :] * (0.5 * STEP), (8, 128))
-        return carry
-
-    lax.fori_loop(0, 80, fill, 0)
+            rs[0, i, b] = u[b, i + 72].reshape(16, 128).astype(bf16)
+            rs[1, i, b] = u[b, i + 16].reshape(16, 128).astype(bf16)
+        return carry
+
+    lax.fori_loop(0, 8, pack_rows, 0)
+    for c in row_copies:
+        c.start()
+    send_round(0, 1)
+    raw_copy(mine + 1, 1).wait()
+    turn(mine + 1, 1)
+    raw_copy(other + 1, 1).start()
+    for c in edge_copies + row_copies:
+        c.wait_recv()
+
+    def unpack_rows(i, carry):
+        for b in range(3):
+            u[b, i + 8] = rr[0, i, b].astype(f32).reshape(2, 8, 128)
+            u[b, i + 80] = rr[1, i, b].astype(f32).reshape(2, 8, 128)
+        return carry
+
+    lax.fori_loop(0, 8, unpack_rows, 0)
+
+    def fill_conduct(n, carry):
+        for q in range(4):
+            i = 4 * n + q
+            cb[0, i + 8] = jnp.broadcast_to(cd[pl.ds(i, 1), :] * (0.5 * STEP), (8, 128))
+        return carry
+
+    lax.fori_loop(0, 20, fill_conduct, 0)
     for s in range(4):
         cb[s, 0:8] = jnp.zeros((8, 8, 128), f32)
         cb[s, 88:96] = jnp.zeros((8, 8, 128), f32)
@@ -181,8 +214,8 @@
             here = in32 // 8 == q
             to_right = r if q == 0 else jnp.where(here, r, to_right)
             to_left = l if q == 0 else jnp.where(here, l, to_left)
-        xs[0, g] = to_right
-        xs[1, g] = to_left
+        xs[0, g] = to_right.reshape(16, 128).astype(bf16)
+        xs[1, g] = to_left.reshape(16, 128).astype(bf16)
         return carry
 
     lax.fori_loop(2, GROUPS - 2, pack, 0)
@@ -192,16 +225,31 @@
     ]
     for c in col_copies:
         c.start()
-    for kk in range(1, 4):
-        send_round(0, kk)
-    raw_copy(mine + 1, 1).wait()
-    turn(mine + 1, 1)
-    raw_copy(other + 1, 1).start()
-    for kk in range(4):
-        send_round(1, kk)
+    for rnd in range(2, 8):
+        send_round(rnd // 4, rnd % 4)
 
     raw_copy(other, 0).wait()
     turn(other, 0)
+    raw_copy(other + 1, 1).wait()
+    turn(other + 1, 1)
+
+    gram[...] = jnp.zeros((512, 512), f32)
+    nt = (((1,), (1,)), ((), ()))
+
+    def add_gram(t, carry):
+        x = jnp.concatenate([tr[t, i] for i in range(8)], axis=1)
+        gram[0:256] += lax.dot_general(x[0:256], x, nt, preferred_element_type=f32)
+        gram[256:512, 256:512] += lax.dot_general(x[256:512], x[256:512], nt, preferred_element_type=f32)
+        return carry
+
+    lax.fori_loop(0, 8, add_gram, 0)
+    gram[256:512, 0:256] = gram[0:256, 256:512].T
+    big = gram[...].astype(bf16)
+    small = (gram[...] - big.astype(f32)).astype(bf16)
+    part[...] = jnp.dot(hid[...], big, preferred_element_type=f32) + jnp.dot(
+        hid[...], small, preferred_element_type=f32
+    )
+
     for c in col_copies:
         c.wait_recv()
 
@@ -213,8 +261,8 @@
     right_ok = (jnp.zeros((2, 8, 128), jnp.int32) + col) < 7
 
     def unpack(g, carry):
-        gl = xr[0, g]
-        gr = xr[1, g]
+        gl = xr[0, g].astype(f32).reshape(2, 8, 128)
+        gr = xr[1, g].astype(f32).reshape(2, 8, 128)
         for q in range(4):
             o = u[3, 4 * g + q]
             a = pltpu.roll(gl, (16 - 8 * q) % 128, 2)
@@ -248,131 +296,106 @@
     lax.fori_loop(2, GROUPS - 2, shift_conduct, 0)
     first, last = lane == 0, lane == 127
 
-    def solve(blocks, size, after_step=None):
-        edge = blocks == (3,)
-        side = 2 if edge else 0
-        per = 8 // size
+    def run_step(s, with_main):
+        blocks = (0, 1, 2, 3) if with_main else (3,)
+        count = range(len(blocks))
+        ahead_s = s + 1 if with_main else s
         coef = [nl[b] for b in blocks]
+        active = [jnp.where(cnt[b] > (s if b < 3 else ahead_s), 1.0, 0.0).astype(f32) for b in blocks]
+        begin = (9 + s) // 4
 
         def kappa(v, i, n, shifted=0):
-            return cb[side + shifted, i][None] / (1.0 + coef[n] * v * v)
-
-        def one_step(s, carry):
-            active = [jnp.where(cnt[b] > s, 1.0, 0.0).astype(f32) for b in blocks]
-            begin = (9 + s) // size
-            r0 = size * begin
-
-            def ahead(i, vs):
-                out = []
+            return cb[(2 if blocks[n] == 3 else 0) + shifted, i][None] / (1.0 + coef[n] * v * v)
+
+        def ahead(i, vs):
+            out = []
+            for n, b in enumerate(blocks):
+                v = vs[n]
+                k = kappa(v, i, n)
+                vr = pltpu.roll(v, 127, 2)
+                across = (k + kappa(vr, i, n, 1)) * (vr - v)
+                if b < 3:
+                    across = jnp.where(last, fx[b, s % 2, i], across)
+                out.append((k, across))
+            return out
+
+        def keep(g, q, made):
+            for n, (k, across) in enumerate(made):
+                ks[blocks[n], (g % 2) * 4 + q] = k
+                ac[blocks[n], (g % 2) * 4 + q] = across
+
+        flows = []
+        for q in range(4):
+            vs = [u[b, 4 * begin + q] for b in blocks]
+            made = ahead(4 * begin + q, vs)
+            keep(begin, q, made)
+            if q == 0:
                 for n, b in enumerate(blocks):
-                    v = vs[n]
-                    k = kappa(v, i, n)
-                    vr = pltpu.roll(v, 127, 2)
-                    across = (k + kappa(vr, i, n, 1)) * (vr - v)
-                    if not edge:
-                        across = jnp.where(last, fx[b, s, i], across)
-                    out.append((k, across))
-                return out
-
-            def keep(g, q, made):
-                for n, (k, across) in enumerate(made):
-                    ks[n, (g % 2) * size + q] = k
-                    ac[n, (g % 2) * size + q] = across
-
-            flows = []
-            for q in range(size):
-                vs = [u[b, r0 + q] for b in blocks]
-                made = ahead(r0 + q, vs)
-                keep(begin, q, made)
-                if q == 0:
-                    for n, b in enumerate(blocks):
-                        before = u[b, r0 - 1]
-                        flows.append((made[n][0] + kappa(before, r0 - 1, n)) * (vs[n] - before))
-
-            def group(g, flow):
-                flow = list(flow)
-                base, now = size * g, (g % 2) * size
-                count = range(len(blocks))
-                v = [[u[b, base + q] for b in blocks] for q in range(size)]
-                k = [[ks[n, now + q] for n in count] for q in range(size)]
-                a = [[ac[n, now + q] for n in count] for q in range(size)]
-                v_next = [[u[b, base + size + q] for b in blocks] for q in range(size)]
-                made = [ahead(base + size + q, v_next[q]) for q in range(size)]
-                for q in range(size):
-                    for n, b in enumerate(blocks):
-                        vn = v[q + 1][n] if q + 1 < size else v_next[0][n]
-                        kn = k[q + 1][n] if q + 1 < size else made[0][n][0]
-                        flow_n = (k[q][n] + kn) * (vn - v[q][n])
-                        came = pltpu.roll(a[q][n], 1, 2)
-                        if edge:
-                            f = jnp.where(in32 == 8, pltpu.roll(a[q][n], 113, 2), a[q][n])
-                            for to in range(3):
-                                fx[to, s, base + q] = pltpu.roll(f, 120 - 32 * to, 2)
-                        else:
-                            came = jnp.where(first, fx[b, s, base + q], came)
-                        new = v[q][n] + active[n] * ((flow_n - flow[n]) + (a[q][n] - came))
-                        u[b, base + q] = new
-                        if not edge:
-                            snap[
-                                size * (g % per) // 2 + q // 2, 2 * (g // per) - 2 + q % 2, s, 16 * b : 16 * b + 16, :
-                            ] = new.reshape(16, 128).astype(bf16)
-                        flow[n] = flow_n
-                for q in range(size):
-                    keep(g + 1, q, made[q])
-                return tuple(flow)
-
-            lax.fori_loop(begin, ROWS // size - begin, group, tuple(flows))
-            for b in blocks:
-                clear(b)
-            if after_step is not None:
-                after_step(s)
-            return carry
-
-        lax.fori_loop(0, 8, one_step, 0)
-
-    solve((3,), 8)
-    raw_copy(other + 1, 1).wait()
-    turn(other + 1, 1)
+                    before = u[b, 4 * begin - 1]
+                    flows.append((made[n][0] + kappa(before, 4 * begin - 1, n)) * (vs[n] - before))
+
+        def group(g, flow):
+            flow = list(flow)
+            base, now = 4 * g, (g % 2) * 4
+            v = [[u[b, base + q] for b in blocks] for q in range(4)]
+            k = [[ks[b, now + q] for b in blocks] for q in range(4)]
+            a = [[ac[b, now + q] for b in blocks] for q in range(4)]
+            v_next = [[u[b, base + 4 + q] for b in blocks] for q in range(4)]
+            first_made = None
+            for q in range(4):
+                made = ahead(base + 4 + q, v_next[q])
+                first_made = made if q == 0 else first_made
+                for n, b in enumerate(blocks):
+                    vn = v[q + 1][n] if q < 3 else v_next[0][n]
+                    kn = k[q + 1][n] if q < 3 else first_made[n][0]
+                    flow_n = (k[q][n] + kn) * (vn - v[q][n])
+                    came = pltpu.roll(a[q][n], 1, 2)
+                    if b == 3:
+                        f = jnp.where(in32 == 8, pltpu.roll(a[q][n], 113, 2), a[q][n])
+                        for to in range(3):
+                            fx[to, ahead_s % 2, base + q] = pltpu.roll(f, 120 - 32 * to, 2)
+                    else:
+                        came = jnp.where(first, fx[b, s % 2, base + q], came)
+                    new = v[q][n] + active[n] * ((flow_n - flow[n]) + (a[q][n] - came))
+                    u[b, base + q] = new
+                    if b < 3:
+                        snap[2 * (g % 2) + q // 2, 2 * (g // 2) - 2 + q % 2, s, 16 * b : 16 * b + 16, :] = (
+                            new.reshape(16, 128).astype(bf16)
+                        )
+                    flow[n] = flow_n
+                keep(g + 1, q, made)
+            return tuple(flow)
+
+        lax.fori_loop(begin, GROUPS - begin, group, tuple(flows))
+        for b in blocks:
+            clear(b)
+
     pass_round(0, 0)
     pass_round(0, 1)
-    pass_round(0, 2)
-
-    def pass_at(s):
-        for at, hh, kk in ((2, 0, 3), (4, 1, 0), (6, 1, 1)):
+    run_step(0, False)
+
+    def one_step(s, carry):
+        run_step(s, True)
+        for at, hh, kk in ((0, 0, 2), (1, 0, 3), (2, 1, 0), (4, 1, 1), (6, 1, 2)):
 
             @pl.when(s == at)
             def _():
                 pass_round(hh, kk)
 
-    solve((0, 1, 2), 4, pass_at)
-    pass_round(1, 2)
-
-    def give_back(i, carry):
-        for b in range(3):
-            fs[pl.ds(b * 1280 + i, 16, stride=80), :] = u[b, i + 8].reshape(16, 128)
-        return carry
-
-    lax.fori_loop(8, 72, give_back, 0)
-    out_copy = pltpu.make_async_copy(fs3.at[:, pl.ds(8, 64), :], final, loc_sem.at[2])
+        return carry
+
+    lax.fori_loop(0, 8, one_step, 0)
+
+    def give_back(n, carry):
+        for q in range(4):
+            for b in range(3):
+                fs[pl.ds(b * 1024 + 4 * n + q, 16, stride=64), :] = u[b, 4 * n + q + 16].reshape(16, 128)
+        return carry
+
+    lax.fori_loop(0, 16, give_back, 0)
+    out_copy = pltpu.make_async_copy(fs3, final, loc_sem.at[2])
     out_copy.start()
-
-    gram[...] = jnp.zeros((512, 512), f32)
-    nt = (((1,), (1,)), ((), ()))
-
-    def add_gram(t, carry):
-        x = jnp.concatenate([tr[t, i] for i in range(8)], axis=1)
-        gram[0:256] += lax.dot_general(x[0:256], x, nt, preferred_element_type=f32)
-        gram[256:512, 256:512] += lax.dot_general(x[256:512], x[256:512], nt, preferred_element_type=f32)
-        return carry
-
-    lax.fori_loop(0, 8, add_gram, 0)
     pass_round(1, 3)
-    gram[256:512, 0:256] = gram[0:256, 256:512].T
-    big = gram[...].astype(bf16)
-    small = (gram[...] - big.astype(f32)).astype(bf16)
-    part[...] = jnp.dot(hid[...], big, preferred_element_type=f32) + jnp.dot(
-        hid[...], small, preferred_element_type=f32
-    )
 
     def square(n, total):
         x = snap[n // 16, 2 + n % 16].astype(f32).reshape(48, 8, 128)
@@ -412,7 +435,7 @@
     loss[...] = total
 
     out_copy.wait()
-    for c in row_copies + col_copies:
+    for c in row_copies + edge_copies + col_copies:
         c.wait_send()
     for hh in range(2):
         for kk in range(4):
@@ -557,15 +580,17 @@
         in_specs=[hbm, hbm, vmem, vmem, hbm, vmem],
         out_specs=(hbm, vmem, vmem),
         scratch_shapes=[
-            pltpu.VMEM((3840, 128), f32),
+            pltpu.VMEM((3072, 128), f32),
             pltpu.VMEM((80, 128), f32),
             pltpu.VMEM((4, ROWS, 2, 8, 128), f32),
             pltpu.VMEM((4, ROWS, 8, 128), f32),
-            pltpu.VMEM((2, GROUPS, 2, 8, 128), f32),
-            pltpu.VMEM((2, GROUPS, 2, 8, 128), f32),
-            pltpu.VMEM((3, 8, ROWS, 2, 8, 128), f32),
-            pltpu.VMEM((3, 16, 2, 8, 128), f32),
-            pltpu.VMEM((3, 16, 2, 8, 128), f32),
+            pltpu.VMEM((2, 8, 3, 16, 128), bf16),
+            pltpu.VMEM((2, 8, 3, 16, 128), bf16),
+            pltpu.VMEM((2, GROUPS, 16, 128), bf16),
+            pltpu.VMEM((2, GROUPS, 16, 128), bf16),
+            pltpu.VMEM((3, 2, ROWS, 2, 8, 128), f32),
+            pltpu.VMEM((4, 8, 2, 8, 128), f32),
+            pltpu.VMEM((4, 8, 2, 8, 128), f32),
             pltpu.VMEM((4, 20, 8, 48, 128), bf16),
             pltpu.VMEM((8, 8, 512, 128), bf16),
             pltpu.VMEM((4, 16, 512, 128), bf16),

time: 178 us -> 165 us (0.927)
  Pallas kernels: 155 us -> 142 us
    pallas_call x1, Pallas kernels: 114 us -> 99.3 us  [per_device(): pl.pallas_call(main_kernel, name='solve_and_learn', out_shape=(jax.ShapeD...]
    pallas_call x1, Pallas kernels: 40.9 us -> 43.1 us  [per_device(): pl.pallas_call(reduce_kernel, name='reduce_grad', out_shape=(jax.ShapeDty...]
where the time goes in v3:
time: 165 us
  Pallas kernels  142 us (86%)
  matrix products  8.33 us (5%)
  local copies, waits for them, and re-layouts  7.73 us (5%)
  other arithmetic  3.61 us (2%)
  between operations  2.59 us (2%)
    pallas_call x1, Pallas kernels, per_device(): pl.pallas_call(main_kernel, name='solve_and_learn', out_shape=(jax.ShapeD...  99.3 us
    pallas_call x1, Pallas kernels, per_device(): pl.pallas_call(reduce_kernel, name='reduce_grad', out_shape=(jax.ShapeDty...  43.1 us
    dot_general x1, matrix products, per_device(): lax.dot_general(grad, w_out, (((1,), (1,)), ((), ())), preferred_element_...  3.41 us

profile of v3, /device:TPU:1, one launch (start us, length us, event | category | flops | bytes accessed | tf_op | source)
XLA Modules:
  0.0 164.7 jit_solution(17773668644663292940)
XLA Ops:
  0.6 0.8 fusion.13
  1.5 0.1 broadcast_in_dim.70
  1.5 0.1 broadcast_in_dim.69
  1.7 0.1 pad.13.clone
  1.8 0.1 maximum_bitcast_fusion
  1.8 0.7 broadcast_in_dim.36
  2.6 0.1 broadcast_in_dim.37
  2.7 0.6 pad_maximum_fusion.nl
  3.3 0.8 fusion.12
  4.1 0.1 broadcast_in_dim.76
  4.2 0.1 broadcast_in_dim.75
  4.2 0.1 broadcast_in_dim.74
  4.3 0.1 pad.7.clone
  4.4 0.1 add_bitcast_fusion
  4.5 0.7 broadcast_in_dim.72
  5.2 0.1 broadcast_in_dim.73
  5.3 0.1 select_dynamic-update-slice_fusion.cnt
  5.4 0.7 convert_element_type.26
  6.1 0.8 convert.1
  7.0 0.7 copy-done
  7.7 1.3 convolution_add_fusion
  9.1 1.1 copy-done.2
  10.2 0.7 fusion.9
  10.9 0.8 dynamic-slice_convert_fusion.hid
  11.6 99.3 %solve_and_learn.1 = (f32[48,64,128]{2,1,0:T(8,128)}, f32[384,512]{1,0:T(8,128)}, f32[8,128]{1,0:T(8,128)}) custom-call(f32[48,64,128]{2,1,0:T(8,128)} %field.1, f32[64,128]{1,0:T(8,128)} %conduct.1, f32[4,2,8,128]{3,2,1,0:T(8,128)} %pad_maximum_fusion.nl, s32[4,2,8,128]{3,2,1,0:T(8,128)} %copy-done.6, bf16[4096,1024]{1,0:T(8,128)(2,1)} %bitcast.18, ...), custom_call_target="tpu_custom_call" | custom-call | tf_op jit(solution)/shard_map/solve_and_learn/pallas_call | solution.py:572
  110.9 43.1 %reduce_grad.1 = (bf16[768,512]{1,0:T(8,128)(2,1)}, f32[8,128]{1,0:T(8,128)}) custom-call(f32[384,512]{1,0:T(8,128)} %get-tuple-element.23.part, f32[8,128]{1,0:T(8,128)} %get-tuple-element.24.loss_in), custom_call_target="tpu_custom_call" | custom-call | tf_op jit(solution)/shard_map/reduce_grad/pallas_call | solution.py:609
  154.1 3.4 %fusion.10 = (f32[512]{0:T(512)S(1)}, bf16[768,512]{1,0:T(8,128)(2,1)S(1)}) fusion(f32[768,512]{1,0:T(8,128)} %copy-done.2, bf16[768,512]{1,0:T(8,128)(2,1)} %get-tuple-element.25, bf16[512,512]{1,0:T(8,128)(2,1)} %param.20), kind=kOutput, calls=%fused_computation.26 | convolution fusion | flops 410910208 | bytes 3672064 | tf_op jit(solution)/shard_map/dot_general | solution.py:630
  157.6 1.2 fusion.7
  158.7 0.6 multiply_subtract_fusion
  159.4 1.8 %fusion.6 = f32[512,512]{1,0:T(8,128)} fusion(bf16[768,512]{1,0:T(8,128)(2,1)S(1)} %copy-done.9, bf16[512,512]{1,0:T(8,128)(2,1)S(1)} %copy-done.11, f32[768,512]{1,0:T(8,128)S(1)} %copy-done.3), kind=kOutput, calls=%fused_computation.11 | convolution fusion | flops 406978560 | bytes 3932160 | tf_op jit(solution)/shard_map/dot_general | solution.py:629
  161.1 0.6 reduce_sum.19
  162.4 1.1 copy.17
  (28 shorter events, 0.2 us)
Async XLA Ops:
  2.7 7.5 %copy-start.10 = (bf16[512,512]{1,0:T(8,128)(2,1)S(1)}, bf16[512,512]{1,0:T(8,128)(2,1)}, u32[]{:S(2)}) copy-start(bf16[512,512]{1,0:T(8,128)(2,1)} %param.20) | copy-start | bytes 1572868
  5.4 1.6 copy-start.6
  7.0 0.7 copy-start
  9.0 1.1 copy-start.2
  154.1 3.5 %copy-start.1 = (bf16[2,8,48,256]{3,2,1,0:T(8,128)(2,1)S(1)}, bf16[2,8,48,256]{3,2,1,0:T(8,128)(2,1)}, u32[]{:S(2)}) copy-start(bf16[2,8,48,256]{3,2,1,0:T(8,128)(2,1)} %copy-done) | copy-start | bytes 1179652
  154.1 3.5 %copy-start.5 = (bf16[256,512]{1,0:T(8,128)(2,1)S(1)}, bf16[256,512]{1,0:T(8,128)(2,1)}, u32[]{:S(2)}) copy-start(bf16[256,512]{1,0:T(8,128)(2,1)} %param.18) | copy-start | bytes 786436
  154.1 5.3 %copy-start.9 = (bf16[768,512]{1,0:T(8,128)(2,1)S(1)}, bf16[768,512]{1,0:T(8,128)(2,1)}, u32[]{:S(2)}) copy-start(bf16[768,512]{1,0:T(8,128)(2,1)} %get-tuple-element.25) | copy-start | bytes 2359300
  154.1 5.2 %copy-start.11 = (bf16[512,512]{1,0:T(8,128)(2,1)S(1)}, bf16[512,512]{1,0:T(8,128)(2,1)}, u32[]{:S(2)}) copy-start(bf16[512,512]{1,0:T(8,128)(2,1)} %param.20) | copy-start | bytes 1572868
  157.5 1.2 copy-start.7
  157.5 1.8 %copy-start.3 = (f32[768,512]{1,0:T(8,128)S(1)}, f32[768,512]{1,0:T(8,128)}, u32[]{:S(2)}) copy-start(f32[768,512]{1,0:T(8,128)} %copy-done.2) | copy-start | bytes 4718596
  159.3 1.8 %copy-start.8 = (f32[8,128]{1,0:T(8,128)S(1)}, f32[8,128]{1,0:T(8,128)}, u32[]{:S(2)}) copy-start(f32[8,128]{1,0:T(8,128)} %get-tuple-element.26) | copy-start | bytes 12292
  159.3 3.0 %copy-start.4 = (f32[48,64,128]{2,1,0:T(8,128)S(1)}, f32[48,64,128]{2,1,0:T(8,128)}, u32[]{:S(2)}) copy-start(f32[48,64,128]{2,1,0:T(8,128)} %get-tuple-element.42) | copy-start | bytes 4718596

commit v4 on v3

--- a/solution.py
+++ b/solution.py
@@ -30,7 +30,7 @@
 def main_kernel(
     field, conduct, nl, cnt, decoder, hid,
     final, part, loss,
-    fs, cd, u, cb, rs, rr, xs, xr, fx, ks, ac, snap, tr, dl, raw, tf, gram, acc,
+    fs, cd, u, cb, rr, xs, xr, fx, ks, ac, snap, tr, dl, raw, tf, gram, acc,
     loc_sem, raw_sem, row_send, row_recv, col_send, col_recv, dec_send, dec_recv, own_sem, fwd_send, fwd_recv,
 ):
     core, row, col = (lax.axis_index(n) for n in ("run", "row", "col"))
@@ -42,14 +42,30 @@
     signal_all([(core, row, t) for t in targets] + [up, down, sibling])
 
     fs3 = fs.reshape(48, 64, 128)
-    row_copies = [
-        remote(rs.at[0], rr.at[0], row_send.at[0], row_recv.at[0], down),
-        remote(rs.at[1], rr.at[1], row_send.at[1], row_recv.at[1], up),
-    ]
-    edge_copies = [
-        remote(conduct.at[pl.ds(56, 8), :], cd.at[pl.ds(0, 8), :], row_send.at[2], row_recv.at[2], down),
-        remote(conduct.at[pl.ds(0, 8), :], cd.at[pl.ds(72, 8), :], row_send.at[3], row_recv.at[3], up),
-    ]
+    rows_in_field = [field.at[:, pl.ds(56, 8), :], field.at[:, pl.ds(0, 8), :]]
+    rows_of_conduct = [conduct.at[pl.ds(56, 8), :], conduct.at[pl.ds(0, 8), :]]
+    rr4 = rr.reshape(2, 48, 8, 128)
+
+    def row_copies(way):
+        peer = (down, up)[way]
+        return [
+            remote(rows_in_field[way], rr4.at[way], row_send.at[way], row_recv.at[way], peer),
+            remote(
+                rows_of_conduct[way], cd.at[pl.ds(72 * way, 8), :], row_send.at[2 + way], row_recv.at[2 + way], peer
+            ),
+        ]
+
+    may_send = [row < 7, row > 0]
+    may_get = [row > 0, row < 7]
+
+    def each_row_copy(allowed, act):
+        for way in range(2):
+
+            @pl.when(allowed[way])
+            def _():
+                for c in row_copies(way):
+                    act(c)
+
     loc_copies = [
         pltpu.make_async_copy(field, fs3, loc_sem.at[0]),
         pltpu.make_async_copy(conduct, cd.at[pl.ds(8, 64), :], loc_sem.at[1]),
@@ -112,9 +128,10 @@
         own_copy(hh, kk).wait()
         fwd_copy(hh, kk).start()
 
-    for c in loc_copies + edge_copies:
+    each_row_copy(may_send, lambda c: c.start())
+    raw_copy(mine, 0).start()
+    for c in loc_copies:
         c.start()
-    raw_copy(mine, 0).start()
     raw_copy(mine + 1, 1).start()
     raw_copy(mine, 0).wait()
     turn(mine, 0)
@@ -136,26 +153,16 @@
 
     lax.fori_loop(0, 16, fill, 0)
 
-    def pack_rows(i, carry):
-        for b in range(3):
-            rs[0, i, b] = u[b, i + 72].reshape(16, 128).astype(bf16)
-            rs[1, i, b] = u[b, i + 16].reshape(16, 128).astype(bf16)
-        return carry
-
-    lax.fori_loop(0, 8, pack_rows, 0)
-    for c in row_copies:
-        c.start()
     send_round(0, 1)
     raw_copy(mine + 1, 1).wait()
     turn(mine + 1, 1)
     raw_copy(other + 1, 1).start()
-    for c in edge_copies + row_copies:
-        c.wait_recv()
+    each_row_copy(may_get, lambda c: c.wait_recv())
 
     def unpack_rows(i, carry):
         for b in range(3):
-            u[b, i + 8] = rr[0, i, b].astype(f32).reshape(2, 8, 128)
-            u[b, i + 80] = rr[1, i, b].astype(f32).reshape(2, 8, 128)
+            for way in range(2):
+                u[b, i + 8 + 72 * way] = rr[way, pl.ds(b * 128 + i, 16, stride=8), :].reshape(2, 8, 128)
         return carry
 
     lax.fori_loop(0, 8, unpack_rows, 0)
@@ -246,9 +253,11 @@
     gram[256:512, 0:256] = gram[0:256, 256:512].T
     big = gram[...].astype(bf16)
     small = (gram[...] - big.astype(f32)).astype(bf16)
-    part[...] = jnp.dot(hid[...], big, preferred_element_type=f32) + jnp.dot(
+    product = jnp.dot(hid[...], big, preferred_element_type=f32) + jnp.dot(
         hid[...], small, preferred_element_type=f32
     )
+    for t in range(4):
+        part[t] = product[:, 128 * t : 128 * t + 128]
 
     for c in col_copies:
         c.wait_recv()
@@ -428,14 +437,15 @@
     for hh in range(2):
         for half in range(2):
             at = slice(256 * half + 128 * hh, 256 * half + 128 * hh + 128)
-            a = part[:, at]
+            a = part[2 * half + hh]
             c = acc[hh, :, 128 * half : 128 * half + 128]
-            part[:, at] = a - c
+            part[2 * half + hh] = a - c
             total = total + jnp.sum((hid[:, at].astype(f32) * (a - 2.0 * c)).reshape(48, 8, 128), axis=0)
     loss[...] = total
 
     out_copy.wait()
-    for c in row_copies + edge_copies + col_copies:
+    each_row_copy(may_send, lambda c: c.wait_send())
+    for c in col_copies:
         c.wait_send()
     for hh in range(2):
         for kk in range(4):
@@ -444,99 +454,93 @@
             fwd_copy(hh, kk).wait_send()
 
 
-def reduce_kernel(part, loss_in, grad, loss_out, r1, q1, r2, q2, l1, l2, l3, g_stage, sem_s, sem_r):
+def reduce_kernel(part, loss_in, grad, loss_out, r1, l1, l2, got, send1, recv1, send2, recv2, lsend, lrecv, lsend2, xsend, xrecv):
     core, row, col = (lax.axis_index(n) for n in ("run", "row", "col"))
-    x, zl = row % 4, row // 4
-    y, zh = col // 2, col % 2
-    spot = y * 4 + zh * 2 + zl
-
-    def at_x(v):
-        return (core, zl * 4 + v, col)
-
-    def at_spot(p):
-        return (core, (p % 2) * 4 + x, (p // 4) * 2 + (p // 2) % 2)
-
-    xs = [(x + j) % 4 for j in range(1, 4)]
-    spots = [(spot + j) % 16 for j in range(1, 16)]
+    x, y, z = row % 4, col // 2, (col % 2) * 2 + row // 4
     sibling = (1 - core, row, col)
-    signal_all([at_x(v) for v in xs] + [at_spot(p) for p in spots] + [sibling])
-    done = []
-
-    def go(copies):
-        for c in copies:
+    me = row * 8 + col
+
+    def chip(j):
+        x1, y1, z1 = (x + j % 4) % 4, (y + j // 4 % 4) % 4, (z + j // 16) % 4
+        return (z1 % 2) * 4 + x1, y1 * 2 + z1 // 2
+
+    offsets = list(range(1, 64))
+    offsets.sort(key=lambda j: -sum(min(d, 4 - d) for d in (j % 4, j // 4 % 4, j // 16)))
+    peers = [(core, *chip(j)) for j in offsets]
+    signal_all(peers + [sibling])
+
+    def piece(p):
+        return part.at[p // 16, pl.ds(pl.multiple_of(24 * (p % 16), 8), 24), :]
+
+    first = []
+    for n, j in enumerate(offsets):
+        r, c = chip(j)
+        first.append(remote(piece(r * 8 + c), r1.at[n], send1.at[n], recv1.at[n], peers[n]))
+    to_zero = remote(loss_in, l1.at[me], lsend, lrecv.at[me], (core, 0, 0))
+
+    @pl.when(me > 0)
+    def _():
+        to_zero.start()
+
+    for c in first:
+        c.start()
+    total = part[me // 16, pl.ds(pl.multiple_of(24 * (me % 16), 8), 24), :]
+    for n, c in enumerate(first):
+        c.wait_recv()
+        total = total + r1[n]
+    got[core, me] = jnp.concatenate([total * (1.0 / 768.0), jnp.zeros((8, 128), f32)], axis=0).astype(bf16)
+
+    second = [remote(got.at[core, me], got.at[core, me], send2.at[n], recv2.at[n], peers[n]) for n in range(63)]
+    for c in second:
+        c.start()
+    spread_loss = [remote(l2.at[core], l2.at[core], lsend2.at[n], lrecv.at[64], peers[n]) for n in range(63)]
+
+    @pl.when(me == 0)
+    def _():
+        sums = loss_in[...]
+        for p in range(1, 64):
+            remote(loss_in, l1.at[p], lsend, lrecv.at[p], (core, 0, 0)).wait_recv()
+            sums = sums + l1[p]
+        l2[core] = sums
+        for c in spread_loss:
             c.start()
-        done.extend(copies)
-
-    first = [
-        remote(part.at[pl.ds(pl.multiple_of(96 * v, 8), 96), :], r1.at[j], sem_s.at[j], sem_r.at[j], at_x(v))
-        for j, v in enumerate(xs)
-    ]
-    lfirst = [
-        remote(loss_in, l1.at[x], sem_s.at[3 + j], sem_r.at[3 + j], at_x(v)) for j, v in enumerate(xs)
-    ]
-    go(first + lfirst)
-    l1[x] = loss_in[...]
-    for c in first + lfirst:
+
+    for c in second:
         c.wait_recv()
-    total = part[pl.ds(pl.multiple_of(96 * x, 8), 96), :]
-    for j in range(3):
-        total = total + r1[j]
-    for b in range(4):
-        q1[b] = total[:, 128 * b : 128 * b + 128]
-    l2[spot] = (l1[0] + l1[1]) + (l1[2] + l1[3])
-
-    def tile(ref, p):
-        return ref.at[p % 4, pl.ds(pl.multiple_of(24 * (p // 4), 8), 24), :]
-
-    second = [
-        remote(tile(q1, p), r2.at[j], sem_s.at[6 + j], sem_r.at[6 + j], at_spot(p)) for j, p in enumerate(spots)
-    ]
-    lsecond = [
-        remote(l2.at[spot], l2.at[spot], sem_s.at[21 + j], sem_r.at[21 + j], at_spot(p))
-        for j, p in enumerate(spots)
-    ]
-    go(second + lsecond)
-    for c in second + lsecond:
-        c.wait_recv()
-    mine = q1[spot % 4, pl.ds(pl.multiple_of(24 * (spot // 4), 8), 24), :]
-    for j in range(15):
-        mine = mine + r2[j]
-    q2[spot % 4, pl.ds(pl.multiple_of(24 * (spot // 4), 8), 24), :] = mine * (1.0 / 768.0)
-    lsum = l2[0]
-    for p in range(1, 16):
-        lsum = lsum + l2[p]
-    l3[core] = lsum
-
-    third = [
-        remote(tile(q2, spot), tile(q2, spot), sem_s.at[36 + j], sem_r.at[36 + j], at_spot(p))
-        for j, p in enumerate(spots)
-    ]
-    lthird = [remote(l3.at[core], l3.at[core], sem_s.at[51], sem_r.at[51], sibling)]
-    go(third + lthird)
-    for c in third:
-        c.wait_recv()
-    for b in range(4):
-        g_stage[core, x, :, 128 * b : 128 * b + 128] = q2[b].astype(bf16)
-
-    def block(c, v):
-        return g_stage.at[c, v]
-
-    fourth = [
-        remote(block(core, x), block(core, x), sem_s.at[52 + j], sem_r.at[52 + j], at_x(v)) for j, v in enumerate(xs)
-    ]
-    cross = [
-        remote(block(core, v), block(core, v), sem_s.at[55 + j], sem_r.at[55 + j], sibling)
-        for j, v in enumerate([x] + [(x + 4 - j) % 4 for j in range(1, 4)])
-    ]
-    go(fourth + cross[:1])
-    for j in range(3):
-        fourth[j].wait_recv()
-        go([cross[1 + j]])
-    for c in cross + lthird:
-        c.wait_recv()
-    grad[...] = g_stage[...].reshape(768, 512)
-    loss_out[...] = l3[0] + l3[1]
-    for c in done:
+    cross = remote(got.at[core], got.at[core], xsend.at[0], xrecv.at[0], sibling)
+    cross.start()
+
+    @pl.when(me > 0)
+    def _():
+        spread_loss[0].wait_recv()
+
+    cross_loss = remote(l2.at[core], l2.at[core], xsend.at[1], xrecv.at[1], sibling)
+    cross_loss.start()
+
+    def place(own):
+        for t in range(4):
+            for q in range(8):
+                pair = jnp.concatenate(
+                    [got[own, 16 * t + 2 * q + i].astype(f32)[0:24] for i in range(2)], axis=0
+                ).astype(bf16)
+                grad[own, 48 * q : 48 * q + 48, 128 * t : 128 * t + 128] = pair
+
+    place(core)
+    cross.wait_recv()
+    place(1 - core)
+    cross_loss.wait_recv()
+    loss_out[...] = l2[0] + l2[1]
+
+    @pl.when(me > 0)
+    def _():
+        to_zero.wait_send()
+
+    @pl.when(me == 0)
+    def _():
+        for c in spread_loss:
+            c.wait_send()
+
+    for c in first + second + [cross, cross_loss]:
         c.wait_send()
 
 
@@ -574,7 +578,7 @@
         name="solve_and_learn",
         out_shape=(
             jax.ShapeDtypeStruct((48, 64, 128), f32),
-            jax.ShapeDtypeStruct((384, 512), f32),
+            jax.ShapeDtypeStruct((4, 384, 128), f32),
             jax.ShapeDtypeStruct((8, 128), f32),
         ),
         in_specs=[hbm, hbm, vmem, vmem, hbm, vmem],
@@ -584,8 +588,7 @@
             pltpu.VMEM((80, 128), f32),
             pltpu.VMEM((4, ROWS, 2, 8, 128), f32),
             pltpu.VMEM((4, ROWS, 8, 128), f32),
-            pltpu.VMEM((2, 8, 3, 16, 128), bf16),
-            pltpu.VMEM((2, 8, 3, 16, 128), bf16),
+            pltpu.VMEM((2, 384, 128), f32),
             pltpu.VMEM((2, GROUPS, 16, 128), bf16),
             pltpu.VMEM((2, GROUPS, 16, 128), bf16),
             pltpu.VMEM((3, 2, ROWS, 2, 8, 128), f32),
@@ -609,22 +612,19 @@
     grad, loss_sum = pl.pallas_call(
         reduce_kernel,
         name="reduce_grad",
-        out_shape=(jax.ShapeDtypeStruct((768, 512), bf16), jax.ShapeDtypeStruct((8, 128), f32)),
+        out_shape=(jax.ShapeDtypeStruct((2, 384, 512), bf16), jax.ShapeDtypeStruct((8, 128), f32)),
         in_specs=[vmem, vmem],
         out_specs=(vmem, vmem),
         scratch_shapes=[
-            pltpu.VMEM((3, 96, 512), f32),
-            pltpu.VMEM((4, 96, 128), f32),
-            pltpu.VMEM((15, 24, 128), f32),
-            pltpu.VMEM((4, 96, 128), f32),
-            pltpu.VMEM((4, 8, 128), f32),
-            pltpu.VMEM((16, 8, 128), f32),
+            pltpu.VMEM((63, 24, 128), f32),
+            pltpu.VMEM((64, 8, 128), f32),
             pltpu.VMEM((2, 8, 128), f32),
-            pltpu.VMEM((2, 4, 96, 512), bf16),
-            dma((60,)), dma((60,)),
+            pltpu.VMEM((2, 64, 32, 128), bf16),
+            dma((63,)), dma((63,)), dma((63,)), dma((63,)), dma(()), dma((65,)), dma((63,)), dma((2,)), dma((2,)),
         ],
         compiler_params=pltpu.CompilerParams(collective_id=1, has_side_effects=True),
     )(part, loss)
+    grad = grad.reshape(768, 512)
 
     grad_out = lax.dot_general(act, grad, (((0,), (0,)), ((), ())), preferred_element_type=f32)
     back = lax.dot_general(grad, w_out, (((1,), (1,)), ((), ())), preferred_element_type=f32)

time: 165 us -> 162 us (0.982)
  Pallas kernels: 142 us -> 139 us
    pallas_call x1, Pallas kernels: 43.1 us -> 36.8 us  [per_device(): pl.pallas_call(reduce_kernel, name='reduce_grad', out_shape=(jax.ShapeDty...]
    pallas_call x1, Pallas kernels: 99.3 us -> 102 us  [per_device(): pl.pallas_call(main_kernel, name='solve_and_learn', out_shape=(jax.ShapeD...]
where the time goes in v4:
time: 162 us; the launch traced here: 161 us
  Pallas kernels  139 us (86%)
  matrix products  8.31 us (5%)
  local copies, waits for them, and re-layouts  7.73 us (5%)
  other arithmetic  3.61 us (2%)
  between operations  2.59 us (2%)
    pallas_call x1, Pallas kernels, per_device(): pl.pallas_call(main_kernel, name='solve_and_learn', out_shape=(jax.ShapeD...  102 us
    pallas_call x1, Pallas kernels, per_device(): pl.pallas_call(reduce_kernel, name='reduce_grad', out_shape=(jax.ShapeDty...  36.8 us
    dot_general x1, matrix products, per_device(): lax.dot_general(grad, w_out, (((1,), (1,)), ((), ())), preferred_element_...  3.41 us

profile of v4, /device:TPU:1, one launch (start us, length us, event | category | flops | bytes accessed | tf_op | source)
XLA Modules:
  0.0 161.3 jit_solution(12758918444101941429)
XLA Ops:
  0.6 0.8 fusion.13
  1.5 0.1 broadcast_in_dim.70
  1.5 0.1 broadcast_in_dim.69
  1.6 0.1 broadcast_in_dim.68
  1.7 0.1 pad.13.clone
  1.8 0.1 maximum_bitcast_fusion
  1.8 0.7 broadcast_in_dim.36
  2.6 0.1 broadcast_in_dim.37
  2.7 0.6 pad_maximum_fusion.nl
  3.3 0.8 fusion.12
  4.1 0.1 broadcast_in_dim.76
  4.2 0.1 broadcast_in_dim.75
  4.3 0.1 pad.7.clone
  4.4 0.1 add_bitcast_fusion
  4.5 0.7 broadcast_in_dim.72
  5.2 0.1 broadcast_in_dim.73
  5.3 0.1 select_dynamic-update-slice_fusion.cnt
  5.4 0.7 convert_element_type.26
  6.1 0.8 convert.1
  7.0 0.7 copy-done
  7.7 1.3 convolution_add_fusion
  9.1 1.1 copy-done.2
  10.2 0.7 fusion.9
  10.9 0.8 dynamic-slice_convert_fusion.hid
  11.6 102.3 %solve_and_learn.1 = (f32[48,64,128]{2,1,0:T(8,128)}, f32[4,384,128]{2,1,0:T(8,128)}, f32[8,128]{1,0:T(8,128)}) custom-call(f32[48,64,128]{2,1,0:T(8,128)} %field.1, f32[64,128]{1,0:T(8,128)} %conduct.1, f32[4,2,8,128]{3,2,1,0:T(8,128)} %pad_maximum_fusion.nl, s32[4,2,8,128]{3,2,1,0:T(8,128)} %copy-done.6, bf16[4096,1024]{1,0:T(8,128)(2,1)} %bitcast.19, ...), custom_call_target="tpu_custom_call" | custom-call | tf_op jit(solution)/shard_map/solve_and_learn/pallas_call | solution.py:576
  114.0 36.8 %reduce_grad.1 = (bf16[2,384,512]{2,1,0:T(8,128)(2,1)}, f32[8,128]{1,0:T(8,128)}) custom-call(f32[4,384,128]{2,1,0:T(8,128)} %get-tuple-element.23.part, f32[8,128]{1,0:T(8,128)} %get-tuple-element.24.loss_in), custom_call_target="tpu_custom_call" | custom-call | tf_op jit(solution)/shard_map/reduce_grad/pallas_call | solution.py:612
  150.8 3.4 %fusion.10 = (f32[512]{0:T(512)S(1)}, bf16[768,512]{1,0:T(8,128)(2,1)S(1)}) fusion(f32[768,512]{1,0:T(8,128)} %copy-done.2, bf16[768,512]{1,0:T(8,128)(2,1)} %bitcast.23, bf16[512,512]{1,0:T(8,128)(2,1)} %param.20), kind=kOutput, calls=%fused_computation.26 | convolution fusion | flops 410910208 | bytes 3672064 | tf_op jit(solution)/shard_map/dot_general | solution.py:630
  154.3 1.2 fusion.7
  155.4 0.6 multiply_subtract_fusion
  156.1 1.8 %fusion.6 = f32[512,512]{1,0:T(8,128)} fusion(bf16[768,512]{1,0:T(8,128)(2,1)S(1)} %bitcast.24, bf16[512,512]{1,0:T(8,128)(2,1)S(1)} %copy-done.11, f32[768,512]{1,0:T(8,128)S(1)} %copy-done.3), kind=kOutput, calls=%fused_computation.11 | convolution fusion | flops 406978560 | bytes 3932160 | tf_op jit(solution)/shard_map/dot_general | solution.py:629
  157.8 0.6 reduce_sum.19
  159.1 1.1 copy.17
  (28 shorter events, 0.2 us)
Async XLA Ops:
  2.7 7.5 %copy-start.10 = (bf16[512,512]{1,0:T(8,128)(2,1)S(1)}, bf16[512,512]{1,0:T(8,128)(2,1)}, u32[]{:S(2)}) copy-start(bf16[512,512]{1,0:T(8,128)(2,1)} %param.20) | copy-start | bytes 1572868
  5.4 1.6 copy-start.6
  7.0 0.7 copy-start
  9.0 1.1 copy-start.2
  150.8 3.5 %copy-start.1 = (bf16[2,8,48,256]{3,2,1,0:T(8,128)(2,1)S(1)}, bf16[2,8,48,256]{3,2,1,0:T(8,128)(2,1)}, u32[]{:S(2)}) copy-start(bf16[2,8,48,256]{3,2,1,0:T(8,128)(2,1)} %copy-done) | copy-start | bytes 1179652
  150.8 3.5 %copy-start.5 = (bf16[256,512]{1,0:T(8,128)(2,1)S(1)}, bf16[256,512]{1,0:T(8,128)(2,1)}, u32[]{:S(2)}) copy-start(bf16[256,512]{1,0:T(8,128)(2,1)} %param.18) | copy-start | bytes 786436
  150.8 5.3 %copy-start.9 = (bf16[2,384,512]{2,1,0:T(8,128)(2,1)S(1)}, bf16[2,384,512]{2,1,0:T(8,128)(2,1)}, u32[]{:S(2)}) copy-start(bf16[2,384,512]{2,1,0:T(8,128)(2,1)} %get-tuple-element.25) | copy-start | bytes 2359300
  150.8 5.2 %copy-start.11 = (bf16[512,512]{1,0:T(8,128)(2,1)S(1)}, bf16[512,512]{1,0:T(8,128)(2,1)}, u32[]{:S(2)}) copy-start(bf16[512,512]{1,0:T(8,128)(2,1)} %param.20) | copy-start | bytes 1572868
  154.2 1.2 copy-start.7
  154.2 1.8 %copy-start.3 = (f32[768,512]{1,0:T(8,128)S(1)}, f32[768,512]{1,0:T(8,128)}, u32[]{:S(2)}) copy-start(f32[768,512]{1,0:T(8,128)} %copy-done.2) | copy-start | bytes 4718596
  156.0 1.8 %copy-start.8 = (f32[8,128]{1,0:T(8,128)S(1)}, f32[8,128]{1,0:T(8,128)}, u32[]{:S(2)}) copy-start(f32[8,128]{1,0:T(8,128)} %get-tuple-element.26) | copy-start | bytes 12292
  156.0 3.0 %copy-start.4 = (f32[48,64,128]{2,1,0:T(8,128)S(1)}, f32[48,64,128]{2,1,0:T(8,128)}, u32[]{:S(2)}) copy-start(f32[48,64,128]{2,1,0:T(8,128)} %get-tuple-element.42) | copy-start | bytes 4718596

commit v5 on v4

--- a/solution.py
+++ b/solution.py
@@ -30,7 +30,7 @@
 def main_kernel(
     field, conduct, nl, cnt, decoder, hid,
     final, part, loss,
-    fs, cd, u, cb, rr, xs, xr, fx, ks, ac, snap, tr, dl, raw, tf, gram, acc,
+    fs, cd, u, cb, rs, rr, xs, xr, fx, ks, ac, snap, tr, dl, raw, tf, gram, acc,
     loc_sem, raw_sem, row_send, row_recv, col_send, col_recv, dec_send, dec_recv, own_sem, fwd_send, fwd_recv,
 ):
     core, row, col = (lax.axis_index(n) for n in ("run", "row", "col"))
@@ -42,14 +42,12 @@
     signal_all([(core, row, t) for t in targets] + [up, down, sibling])
 
     fs3 = fs.reshape(48, 64, 128)
-    rows_in_field = [field.at[:, pl.ds(56, 8), :], field.at[:, pl.ds(0, 8), :]]
     rows_of_conduct = [conduct.at[pl.ds(56, 8), :], conduct.at[pl.ds(0, 8), :]]
-    rr4 = rr.reshape(2, 48, 8, 128)
 
     def row_copies(way):
         peer = (down, up)[way]
         return [
-            remote(rows_in_field[way], rr4.at[way], row_send.at[way], row_recv.at[way], peer),
+            remote(rs.at[way], rr.at[way], row_send.at[way], row_recv.at[way], peer),
             remote(
                 rows_of_conduct[way], cd.at[pl.ds(72 * way, 8), :], row_send.at[2 + way], row_recv.at[2 + way], peer
             ),
@@ -128,18 +126,26 @@
         own_copy(hh, kk).wait()
         fwd_copy(hh, kk).start()
 
-    each_row_copy(may_send, lambda c: c.start())
-    raw_copy(mine, 0).start()
     for c in loc_copies:
         c.start()
+    raw_copy(mine, 0).start()
     raw_copy(mine + 1, 1).start()
+    for c in loc_copies:
+        c.wait()
+
+    def pack_rows(i, carry):
+        for b in range(3):
+            for way in range(2):
+                rs[way, i, b] = fs[pl.ds(b * 1024 + i + 56 * (1 - way), 16, stride=64), :].astype(bf16)
+        return carry
+
+    lax.fori_loop(0, 8, pack_rows, 0)
+    each_row_copy(may_send, lambda c: c.start())
     raw_copy(mine, 0).wait()
     turn(mine, 0)
     raw_copy(other, 0).start()
     send_round(0, 0)
 
-    for c in loc_copies:
-        c.wait()
     for b in range(3):
         u[b, 0:8] = jnp.zeros((8, 2, 8, 128), f32)
         u[b, 88:96] = jnp.zeros((8, 2, 8, 128), f32)
@@ -153,16 +159,12 @@
 
     lax.fori_loop(0, 16, fill, 0)
 
-    send_round(0, 1)
-    raw_copy(mine + 1, 1).wait()
-    turn(mine + 1, 1)
-    raw_copy(other + 1, 1).start()
     each_row_copy(may_get, lambda c: c.wait_recv())
 
     def unpack_rows(i, carry):
         for b in range(3):
             for way in range(2):
-                u[b, i + 8 + 72 * way] = rr[way, pl.ds(b * 128 + i, 16, stride=8), :].reshape(2, 8, 128)
+                u[b, i + 8 + 72 * way] = rr[way, i, b].astype(f32).reshape(2, 8, 128)
         return carry
 
     lax.fori_loop(0, 8, unpack_rows, 0)
@@ -227,16 +229,18 @@
 
     lax.fori_loop(2, GROUPS - 2, pack, 0)
     col_copies = [
-        remote(xs.at[0], xr.at[0], col_send.at[0], col_recv.at[0], right),
-        remote(xs.at[1], xr.at[1], col_send.at[1], col_recv.at[1], left),
+        remote(xs.at[0, pl.ds(2, 20)], xr.at[0, pl.ds(2, 20)], col_send.at[0], col_recv.at[0], right),
+        remote(xs.at[1, pl.ds(2, 20)], xr.at[1, pl.ds(2, 20)], col_send.at[1], col_recv.at[1], left),
     ]
     for c in col_copies:
         c.start()
-    for rnd in range(2, 8):
-        send_round(rnd // 4, rnd % 4)
-
+    raw_copy(mine + 1, 1).wait()
+    turn(mine + 1, 1)
+    raw_copy(other + 1, 1).start()
     raw_copy(other, 0).wait()
     turn(other, 0)
+    for rnd in range(1, 8):
+        send_round(rnd // 4, rnd % 4)
     raw_copy(other + 1, 1).wait()
     turn(other + 1, 1)
 
@@ -380,12 +384,11 @@
             clear(b)
 
     pass_round(0, 0)
-    pass_round(0, 1)
     run_step(0, False)
 
     def one_step(s, carry):
         run_step(s, True)
-        for at, hh, kk in ((0, 0, 2), (1, 0, 3), (2, 1, 0), (4, 1, 1), (6, 1, 2)):
+        for at, hh, kk in ((0, 0, 1), (1, 0, 2), (3, 0, 3), (4, 1, 0), (5, 1, 1), (6, 1, 2)):
 
             @pl.when(s == at)
             def _():
@@ -394,6 +397,8 @@
         return carry
 
     lax.fori_loop(0, 8, one_step, 0)
+
+    pass_round(1, 3)
 
     def give_back(n, carry):
         for q in range(4):
@@ -404,7 +409,6 @@
     lax.fori_loop(0, 16, give_back, 0)
     out_copy = pltpu.make_async_copy(fs3, final, loc_sem.at[2])
     out_copy.start()
-    pass_round(1, 3)
 
     def square(n, total):
         x = snap[n // 16, 2 + n % 16].astype(f32).reshape(48, 8, 128)
@@ -588,7 +592,8 @@
             pltpu.VMEM((80, 128), f32),
             pltpu.VMEM((4, ROWS, 2, 8, 128), f32),
             pltpu.VMEM((4, ROWS, 8, 128), f32),
-            pltpu.VMEM((2, 384, 128), f32),
+            pltpu.VMEM((2, 8, 3, 16, 128), bf16),
+            pltpu.VMEM((2, 8, 3, 16, 128), bf16),
             pltpu.VMEM((2, GROUPS, 16, 128), bf16),
             pltpu.VMEM((2, GROUPS, 16, 128), bf16),
             pltpu.VMEM((3, 2, ROWS, 2, 8, 128), f32),

time: 162 us -> 146 us (0.901)
  Pallas kernels: 139 us -> 123 us
    pallas_call x1, Pallas kernels: 102 us -> 85.6 us  [per_device(): pl.pallas_call(main_kernel, name='solve_and_learn', out_shape=(jax.ShapeD...]
where the time goes in v5:
time: 146 us; the launch traced here: 145 us
  Pallas kernels  123 us (84%)
  matrix products  8.32 us (6%)
  local copies, waits for them, and re-layouts  7.73 us (5%)
  other arithmetic  3.61 us (2%)
  between operations  2.59 us (2%)
    pallas_call x1, Pallas kernels, per_device(): pl.pallas_call(main_kernel, name='solve_and_learn', out_shape=(jax.ShapeD...  85.6 us
    pallas_call x1, Pallas kernels, per_device(): pl.pallas_call(reduce_kernel, name='reduce_grad', out_shape=(jax.ShapeDty...  37.4 us
    dot_general x1, matrix products, per_device(): lax.dot_general(grad, w_out, (((1,), (1,)), ((), ())), preferred_element_...  3.41 us
    unnamed x25, local copies, waits for them, and re-layouts  3.06 us

profile of v5, /device:TPU:1, one launch (start us, length us, event | category | flops | bytes accessed | tf_op | source)
XLA Modules:
  0.0 145.2 jit_solution(18437289562177086324)
XLA Ops:
  0.6 0.8 fusion.13
  1.5 0.1 broadcast_in_dim.70
  1.5 0.1 broadcast_in_dim.69
  1.6 0.1 broadcast_in_dim.68
  1.7 0.1 pad.13.clone
  1.8 0.1 maximum_bitcast_fusion
  1.8 0.7 broadcast_in_dim.36
  2.6 0.1 broadcast_in_dim.37
  2.7 0.6 pad_maximum_fusion.nl
  3.3 0.8 fusion.12
  4.1 0.1 broadcast_in_dim.76
  4.2 0.1 broadcast_in_dim.75
  4.3 0.1 pad.7.clone
  4.4 0.1 add_bitcast_fusion
  4.5 0.7 broadcast_in_dim.72
  5.2 0.1 broadcast_in_dim.73
  5.3 0.1 select_dynamic-update-slice_fusion.cnt
  5.4 0.7 convert_element_type.26
  6.1 0.8 convert.1
  7.0 0.7 copy-done
  7.7 1.3 convolution_add_fusion
  9.1 1.1 copy-done.2
  10.2 0.7 fusion.9
  10.9 0.8 dynamic-slice_convert_fusion.hid
  11.6 85.6 %solve_and_learn.1 = (f32[48,64,128]{2,1,0:T(8,128)}, f32[4,384,128]{2,1,0:T(8,128)}, f32[8,128]{1,0:T(8,128)}) custom-call(f32[48,64,128]{2,1,0:T(8,128)} %field.1, f32[64,128]{1,0:T(8,128)} %conduct.1, f32[4,2,8,128]{3,2,1,0:T(8,128)} %pad_maximum_fusion.nl, s32[4,2,8,128]{3,2,1,0:T(8,128)} %copy-done.6, bf16[4096,1024]{1,0:T(8,128)(2,1)} %bitcast.19, ...), custom_call_target="tpu_custom_call" | custom-call | tf_op jit(solution)/shard_map/solve_and_learn/pallas_call | solution.py:580
  97.3 37.4 %reduce_grad.1 = (bf16[2,384,512]{2,1,0:T(8,128)(2,1)}, f32[8,128]{1,0:T(8,128)}) custom-call(f32[4,384,128]{2,1,0:T(8,128)} %get-tuple-element.23.part, f32[8,128]{1,0:T(8,128)} %get-tuple-element.24.loss_in), custom_call_target="tpu_custom_call" | custom-call | tf_op jit(solution)/shard_map/reduce_grad/pallas_call | solution.py:617
  134.7 3.4 %fusion.10 = (f32[512]{0:T(512)S(1)}, bf16[768,512]{1,0:T(8,128)(2,1)S(1)}) fusion(f32[768,512]{1,0:T(8,128)} %copy-done.2, bf16[768,512]{1,0:T(8,128)(2,1)} %bitcast.23, bf16[512,512]{1,0:T(8,128)(2,1)} %param.20), kind=kOutput, calls=%fused_computation.26 | convolution fusion | flops 410910208 | bytes 3672064 | tf_op jit(solution)/shard_map/dot_general | solution.py:635
  138.1 1.2 fusion.7
  139.3 0.6 multiply_subtract_fusion
  139.9 1.8 %fusion.6 = f32[512,512]{1,0:T(8,128)} fusion(bf16[768,512]{1,0:T(8,128)(2,1)S(1)} %bitcast.24, bf16[512,512]{1,0:T(8,128)(2,1)S(1)} %copy-done.11, f32[768,512]{1,0:T(8,128)S(1)} %copy-done.3), kind=kOutput, calls=%fused_computation.11 | convolution fusion | flops 406978560 | bytes 3932160 | tf_op jit(solution)/shard_map/dot_general | solution.py:634
  141.7 0.6 reduce_sum.19
  142.9 1.1 copy.17
  (28 shorter events, 0.2 us)
Async XLA Ops:
  2.7 7.5 %copy-start.10 = (bf16[512,512]{1,0:T(8,128)(2,1)S(1)}, bf16[512,512]{1,0:T(8,128)(2,1)}, u32[]{:S(2)}) copy-start(bf16[512,512]{1,0:T(8,128)(2,1)} %param.20) | copy-start | bytes 1572868
  5.4 1.6 %copy-start.6 = (s32[4,2,8,128]{3,2,1,0:T(8,128)}, s32[4,2,8,128]{3,2,1,0:T(8,128)S(1)}, u32[]{:S(2)}) copy-start(s32[4,2,8,128]{3,2,1,0:T(8,128)S(1)} %select_dynamic-update-slice_fusion.cnt) | copy-start | bytes 98308
  7.0 0.7 copy-start
  9.0 1.1 copy-start.2
  134.6 3.5 %copy-start.1 = (bf16[2,8,48,256]{3,2,1,0:T(8,128)(2,1)S(1)}, bf16[2,8,48,256]{3,2,1,0:T(8,128)(2,1)}, u32[]{:S(2)}) copy-start(bf16[2,8,48,256]{3,2,1,0:T(8,128)(2,1)} %copy-done) | copy-start | bytes 1179652
  134.6 3.5 %copy-start.5 = (bf16[256,512]{1,0:T(8,128)(2,1)S(1)}, bf16[256,512]{1,0:T(8,128)(2,1)}, u32[]{:S(2)}) copy-start(bf16[256,512]{1,0:T(8,128)(2,1)} %param.18) | copy-start | bytes 786436
  134.6 5.3 %copy-start.9 = (bf16[2,384,512]{2,1,0:T(8,128)(2,1)S(1)}, bf16[2,384,512]{2,1,0:T(8,128)(2,1)}, u32[]{:S(2)}) copy-start(bf16[2,384,512]{2,1,0:T(8,128)(2,1)} %get-tuple-element.25) | copy-start | bytes 2359300
  134.7 5.2 %copy-start.11 = (bf16[512,512]{1,0:T(8,128)(2,1)S(1)}, bf16[512,512]{1,0:T(8,128)(2,1)}, u32[]{:S(2)}) copy-start(bf16[512,512]{1,0:T(8,128)(2,1)} %param.20) | copy-start | bytes 1572868
  138.1 1.2 copy-start.7
  138.1 1.8 %copy-start.3 = (f32[768,512]{1,0:T(8,128)S(1)}, f32[768,512]{1,0:T(8,128)}, u32[]{:S(2)}) copy-start(f32[768,512]{1,0:T(8,128)} %copy-done.2) | copy-start | bytes 4718596
  139.9 1.8 %copy-start.8 = (f32[8,128]{1,0:T(8,128)S(1)}, f32[8,128]{1,0:T(8,128)}, u32[]{:S(2)}) copy-start(f32[8,128]{1,0:T(8,128)} %get-tuple-element.26) | copy-start | bytes 12292
  139.9 3.0 %copy-start.4 = (f32[48,64,128]{2,1,0:T(8,128)S(1)}, f32[48,64,128]{2,1,0:T(8,128)}, u32[]{:S(2)}) copy-start(f32[48,64,128]{2,1,0:T(8,128)} %get-tuple-element.42) | copy-start | bytes 4718596

commit v6 on v5

--- a/solution.py
+++ b/solution.py
@@ -28,9 +28,9 @@
 
 
 def main_kernel(
-    field, conduct, nl, cnt, decoder, hid,
+    field, conduct, nonlin, counts, desc, code, w_in, bias, w_out, decoder,
     final, part, loss,
-    fs, cd, u, cb, rs, rr, xs, xr, fx, ks, ac, snap, tr, dl, raw, tf, gram, acc,
+    nl, cnt, hid, fs, cd, u, cb, rs, rr, xs, xr, fx, ks, ac, snap, tr, dl, raw, tf, gram, acc,
     loc_sem, raw_sem, row_send, row_recv, col_send, col_recv, dec_send, dec_recv, own_sem, fwd_send, fwd_recv,
 ):
     core, row, col = (lax.axis_index(n) for n in ("run", "row", "col"))
@@ -244,6 +244,12 @@
     raw_copy(other + 1, 1).wait()
     turn(other + 1, 1)
 
+    wide = desc[pl.ds(pl.multiple_of(core * 48, 16), 48), :].astype(f32)
+    for s in range(8):
+        rows_s = (wide + code[s : s + 1, :].astype(f32)).astype(bf16)
+        act_s = jax.nn.gelu(jnp.dot(rows_s, w_in[...], preferred_element_type=f32) + bias[...]).astype(bf16)
+        hid[48 * s : 48 * s + 48, :] = jnp.dot(act_s, w_out[...], preferred_element_type=f32).astype(bf16)
+
     gram[...] = jnp.zeros((512, 512), f32)
     nt = (((1,), (1,)), ((), ()))
 
@@ -266,12 +272,29 @@
     for c in col_copies:
         c.wait_recv()
 
+    def of_runs(ref, b):
+        return jnp.broadcast_to(ref[16 * b : 16 * b + 16, :], (16, 128)).reshape(2, 8, 128)
+
+    def lanes_of_runs(ref):
+        out = jnp.zeros((2, 8, 128), ref.dtype)
+        for b in range(3):
+            out = jnp.where(lane // 32 == b, of_runs(ref, b), out)
+        return out
+
+    for b in range(3):
+        nl[b] = of_runs(nonlin, b)
+        cnt[b] = of_runs(counts, b)
+    nl[3] = lanes_of_runs(nonlin)
+
     u[3, 0:8] = jnp.zeros((8, 2, 8, 128), f32)
     u[3, 88:96] = jnp.zeros((8, 2, 8, 128), f32)
     from_left = (in32 >= 16) & (in32 < 24)
     from_right = (in32 >= 8) & (in32 < 16)
     left_ok = (jnp.zeros((2, 8, 128), jnp.int32) + col) > 0
     right_ok = (jnp.zeros((2, 8, 128), jnp.int32) + col) < 7
+
+    taken = jnp.where(from_left & jnp.logical_not(left_ok), 0, lanes_of_runs(counts))
+    cnt[3] = jnp.where(from_right & jnp.logical_not(right_ok), 0, taken)
 
     def unpack(g, carry):
         gl = xr[0, g].astype(f32).reshape(2, 8, 128)
@@ -458,7 +481,11 @@
             fwd_copy(hh, kk).wait_send()
 
 
-def reduce_kernel(part, loss_in, grad, loss_out, r1, l1, l2, got, send1, recv1, send2, recv2, lsend, lrecv, lsend2, xsend, xrecv):
+def reduce_kernel(
+    part, loss_in, desc, code, w_in, bias, w_out,
+    new_in, new_bias, new_out, loss_out,
+    rows, act, slope, grad, back, r1, l1, l2, got, send1, recv1, send2, recv2, lsend, lrecv, lsend2, xsend, xrecv,
+):
     core, row, col = (lax.axis_index(n) for n in ("run", "row", "col"))
     x, y, z = row % 4, col // 2, (col % 2) * 2 + row // 4
     sibling = (1 - core, row, col)
@@ -488,6 +515,19 @@
 
     for c in first:
         c.start()
+
+    def trunk(n, carry):
+        at = pl.multiple_of(48 * n, 48)
+        half = pl.multiple_of(48 * (n // 8), 48)
+        rows_n = (desc[pl.ds(half, 48), :].astype(f32) + code[n % 8]).astype(bf16)
+        pre = jnp.dot(rows_n, w_in[...], preferred_element_type=f32) + bias[...]
+        value, pull = jax.vjp(jax.nn.gelu, pre)
+        rows[pl.ds(at, 48), :] = rows_n
+        act[pl.ds(at, 48), :] = value.astype(bf16)
+        slope[pl.ds(at, 48), :] = pull(jnp.ones_like(pre))[0]
+        return carry
+
+    lax.fori_loop(0, 16, trunk, 0)
     total = part[me // 16, pl.ds(pl.multiple_of(24 * (me % 16), 8), 24), :]
     for n, c in enumerate(first):
         c.wait_recv()
@@ -527,11 +567,22 @@
                 pair = jnp.concatenate(
                     [got[own, 16 * t + 2 * q + i].astype(f32)[0:24] for i in range(2)], axis=0
                 ).astype(bf16)
-                grad[own, 48 * q : 48 * q + 48, 128 * t : 128 * t + 128] = pair
+                grad[pl.ds(pl.multiple_of(384 * own + 48 * q, 48), 48), 128 * t : 128 * t + 128] = pair
 
     place(core)
     cross.wait_recv()
     place(1 - core)
+    tn = (((0,), (0,)), ((), ()))
+    new_out[...] = w_out[...].astype(f32) - RATE * lax.dot_general(
+        act[...], grad[...], tn, preferred_element_type=f32
+    )
+    back[...] = (
+        lax.dot_general(grad[...], w_out[...], (((1,), (1,)), ((), ())), preferred_element_type=f32) * slope[...]
+    )
+    new_bias[...] = bias[...] - RATE * jnp.sum(back[...], axis=0, keepdims=True)
+    new_in[...] = w_in[...].astype(f32) - RATE * lax.dot_general(
+        rows[...], back[...].astype(bf16), tn, preferred_element_type=f32
+    )
     cross_loss.wait_recv()
     loss_out[...] = l2[0] + l2[1]
 
@@ -546,34 +597,12 @@
 
     for c in first + second + [cross, cross_loss]:
         c.wait_send()
-
-
-def spread(values):
-    three = values.reshape(3, 16)
-    wide = jnp.broadcast_to(three[:, :, None], (3, 16, 128))
-    edge = jnp.concatenate(
-        [jnp.broadcast_to(three[b][:, None], (16, 32)) for b in range(3)] + [jnp.zeros((16, 32), values.dtype)],
-        axis=1,
-    )
-    return jnp.concatenate([wide, edge[None]], axis=0).reshape(4, 2, 8, 128)
 
 
 def per_device(
     init_field, conduct, nonlin, counts, descriptors, time_code, w_in, bias_in, w_out, decoder
 ):
-    core = lax.axis_index("run")
-    col = lax.axis_index("col")
-    wide = descriptors.astype(f32).reshape(2, 1, 48, 256) + time_code.astype(f32).reshape(1, 8, 1, 256)
-    rows_in = wide.astype(bf16).reshape(768, 256)
-    pre = jnp.dot(rows_in, w_in, preferred_element_type=f32) + bias_in
-    act = jax.nn.gelu(pre).astype(bf16)
-    hidden = jnp.dot(act, w_out, preferred_element_type=f32).astype(bf16)
-    hid = lax.dynamic_slice_in_dim(hidden, core * 384, 384, 0)
-
-    lanes = jnp.arange(128) % 32
-    outside = ((lanes >= 16) & (lanes < 24) & (col == 0)) | ((lanes >= 8) & (lanes < 16) & (col == 7))
-    cnt = spread(counts)
-    cnt = cnt.at[3].set(jnp.where(outside[None, None, :], 0, cnt[3]))
+    bias_row = bias_in.reshape(1, 512)
     vmem = pl.BlockSpec(memory_space=pltpu.VMEM)
     hbm = pl.BlockSpec(memory_space=pl.ANY)
     dma = pltpu.SemaphoreType.DMA
@@ -585,9 +614,12 @@
             jax.ShapeDtypeStruct((4, 384, 128), f32),
             jax.ShapeDtypeStruct((8, 128), f32),
         ),
-        in_specs=[hbm, hbm, vmem, vmem, hbm, vmem],
+        in_specs=[hbm, hbm, vmem, vmem, vmem, vmem, vmem, vmem, vmem, hbm],
         out_specs=(hbm, vmem, vmem),
         scratch_shapes=[
+            pltpu.VMEM((4, 2, 8, 128), f32),
+            pltpu.VMEM((4, 2, 8, 128), jnp.int32),
+            pltpu.VMEM((384, 512), bf16),
             pltpu.VMEM((3072, 128), f32),
             pltpu.VMEM((80, 128), f32),
             pltpu.VMEM((4, ROWS, 2, 8, 128), f32),
@@ -612,15 +644,28 @@
         compiler_params=pltpu.CompilerParams(
             collective_id=0, has_side_effects=True, vmem_limit_bytes=VMEM_ALL - (1 << 16)
         ),
-    )(init_field, conduct, spread(nonlin), cnt, decoder.reshape(4096, 1024), hid)
-
-    grad, loss_sum = pl.pallas_call(
+    )(
+        init_field, conduct, nonlin.reshape(48, 1), counts.reshape(48, 1),
+        descriptors, time_code, w_in, bias_row, w_out, decoder.reshape(4096, 1024),
+    )
+
+    new_w_in, new_bias, new_w_out, loss_sum = pl.pallas_call(
         reduce_kernel,
         name="reduce_grad",
-        out_shape=(jax.ShapeDtypeStruct((2, 384, 512), bf16), jax.ShapeDtypeStruct((8, 128), f32)),
-        in_specs=[vmem, vmem],
-        out_specs=(vmem, vmem),
+        out_shape=(
+            jax.ShapeDtypeStruct((256, 512), f32),
+            jax.ShapeDtypeStruct((1, 512), f32),
+            jax.ShapeDtypeStruct((512, 512), f32),
+            jax.ShapeDtypeStruct((8, 128), f32),
+        ),
+        in_specs=[vmem] * 7,
+        out_specs=(vmem,) * 4,
         scratch_shapes=[
+            pltpu.VMEM((768, 256), bf16),
+            pltpu.VMEM((768, 512), bf16),
+            pltpu.VMEM((768, 512), f32),
+            pltpu.VMEM((768, 512), bf16),
+            pltpu.VMEM((768, 512), f32),
             pltpu.VMEM((63, 24, 128), f32),
             pltpu.VMEM((64, 8, 128), f32),
             pltpu.VMEM((2, 8, 128), f32),
@@ -628,21 +673,9 @@
             dma((63,)), dma((63,)), dma((63,)), dma((63,)), dma(()), dma((65,)), dma((63,)), dma((2,)), dma((2,)),
         ],
         compiler_params=pltpu.CompilerParams(collective_id=1, has_side_effects=True),
-    )(part, loss)
-    grad = grad.reshape(768, 512)
-
-    grad_out = lax.dot_general(act, grad, (((0,), (0,)), ((), ())), preferred_element_type=f32)
-    back = lax.dot_general(grad, w_out, (((1,), (1,)), ((), ())), preferred_element_type=f32)
-    _, pull = jax.vjp(jax.nn.gelu, pre)
-    grad_pre = pull(back)[0]
-    grad_in = lax.dot_general(
-        rows_in, grad_pre.astype(bf16), (((0,), (0,)), ((), ())), preferred_element_type=f32
-    )
-    new_w_in = w_in.astype(f32) - RATE * grad_in
-    new_bias = bias_in - RATE * jnp.sum(grad_pre, axis=0)
-    new_w_out = w_out.astype(f32) - RATE * grad_out
+    )(part, loss, descriptors, time_code.astype(f32).reshape(8, 1, 256), w_in, bias_row, w_out)
     mean_loss = jnp.sum(loss_sum) / (768 * 512 * 1024)
-    return final, new_w_in, new_bias, new_w_out, mean_loss
+    return final, new_w_in, new_bias.reshape(512), new_w_out, mean_loss
 
 
 def solution(mesh):

time: 146 us -> 137 us (0.938)
  matrix products: 8.32 us -> 0 us
  Pallas kernels: 123 us -> 126 us
  other arithmetic: 3.61 us -> 1.29 us
    dot_general x5 -> x0, matrix products: 8.32 us -> none  [the longest x1 3.41 us: per_device(): lax.dot_general(grad, w_out, (((1,), (1,)), ((), ())), preferred_element_...]
    reshape x0 -> x3, local copies, waits for them, and re-layouts: none -> 3.99 us  [the longest x1 1.35 us: per_device(): nonlin.reshape(48, 1)]
    broadcast_in_dim x12 -> x0, local copies, waits for them, and re-layouts: 2.06 us -> none  [the longest x4 1.64 us: spread(): wide = jnp.broadcast_to(three[:, :, None], (3, 16, 128))]
    pallas_call x1, Pallas kernels: 37.4 us -> 39.2 us  [per_device(): pl.pallas_call(reduce_kernel, name='reduce_grad', out_shape=(jax.ShapeDty...]
    slice x2 -> x0, local copies, waits for them, and re-layouts: 1.68 us -> none  [spread(): three[b][:, None]]
    unnamed x25 -> x12, local copies, waits for them, and re-layouts: 3.06 us -> 3.63 us
where the time goes in v6:
time: 137 us
  Pallas kernels  126 us (92%)
  local copies, waits for them, and re-layouts  7.61 us (6%)
  between operations  2.47 us (2%)
    pallas_call x1, Pallas kernels, per_device(): pl.pallas_call(main_kernel, name='solve_and_learn', out_shape=(jax.ShapeD...  86.4 us
    pallas_call x1, Pallas kernels, per_device(): pl.pallas_call(reduce_kernel, name='reduce_grad', out_shape=(jax.ShapeDty...  39.2 us
    unnamed x12, local copies, waits for them, and re-layouts  3.63 us

profile of v6, /device:TPU:1, one launch (start us, length us, event | category | flops | bytes accessed | tf_op | source)
XLA Modules:
  0.0 137.0 jit_solution(14467951441282285871)
XLA Ops:
  0.6 1.3 reshape.38.code
  1.9 1.3 copy.15.nonlin
  3.3 1.3 copy.16.counts
  4.6 86.4 %solve_and_learn.1 = (f32[48,64,128]{2,1,0:T(8,128)}, f32[4,384,128]{2,1,0:T(8,128)}, f32[8,128]{1,0:T(8,128)}) custom-call(f32[48,64,128]{2,1,0:T(8,128)} %field.1, f32[64,128]{1,0:T(8,128)} %conduct.1, f32[48,1]{1,0:T(8,128)} %copy.15.nonlin, s32[48,1]{1,0:T(8,128)} %copy.16.counts, bf16[96,256]{1,0:T(8,128)(2,1)} %desc.3, bf16[8,256]{1,0:T(8,128)(2,1)} %code.1, ...), custom_call_target="tpu_custom_call" | custom-call | tf_op jit(solution)/shard_map/solve_and_learn/pallas_call | solution.py:609
  91.0 0.0 copy-start
  91.0 39.2 %reduce_grad.1 = (f32[256,512]{1,0:T(8,128)}, f32[1,512]{1,0:T(1,128)}, f32[512,512]{1,0:T(8,128)}, f32[8,128]{1,0:T(8,128)}) custom-call(f32[4,384,128]{2,1,0:T(8,128)} %get-tuple-element.13.part, f32[8,128]{1,0:T(8,128)} %get-tuple-element.14.loss_in, bf16[96,256]{1,0:T(8,128)(2,1)} %desc.3, f32[8,1,256]{2,1,0:T(1,128)} %reshape.38.code, ...), custom_call_target="tpu_custom_call" | custom-call | tf_op jit(solution)/shard_map/reduce_grad/pallas_call | solution.py:652
  130.2 1.3 reduce_sum.9
  132.2 0.0 copy-done
  132.2 0.0 copy-start.2
  132.2 0.0 copy-start.3
  132.2 0.0 copy-start.1
  132.2 1.1 copy.21
  133.4 0.1 copy-done.2
  133.5 0.8 copy.22
  134.3 0.0 copy-done.3
  134.3 0.6 copy.23
  134.9 0.0 copy-done.1
  134.9 1.0 copy.24
Async XLA Ops:
  91.0 41.2 %copy-start = (f32[48,64,128]{2,1,0:T(8,128)S(1)}, f32[48,64,128]{2,1,0:T(8,128)}, u32[]{:S(2)}) copy-start(f32[48,64,128]{2,1,0:T(8,128)} %get-tuple-element.24) | copy-start | bytes 4718596
  132.2 1.3 copy-start.2
  132.2 2.1 %copy-start.3 = (f32[1,512]{1,0:T(1,128)S(1)}, f32[1,512]{1,0:T(1,128)}, u32[]{:S(2)}) copy-start(f32[1,512]{1,0:T(1,128)} %get-tuple-element.16) | copy-start | bytes 6148
  132.2 2.7 %copy-start.1 = (f32[512,512]{1,0:T(8,128)S(1)}, f32[512,512]{1,0:T(8,128)}, u32[]{:S(2)}) copy-start(f32[512,512]{1,0:T(8,128)} %get-tuple-element.27) | copy-start | bytes 3145732

commit v7 on v6

--- a/solution.py
+++ b/solution.py
@@ -39,7 +39,7 @@
     down, up = (core, (row + 1) % 8, col), (core, (row + 7) % 8, col)
     right, left = (core, row, (col + 1) % 8), (core, row, (col + 7) % 8)
     targets = [((y + dy) % 4) * 2 + (zh + dz) % 2 for dy, dz in OFFSETS]
-    signal_all([(core, row, t) for t in targets] + [up, down, sibling])
+    signal_all([(core, q // 8, q % 8) for q in [(row * 8 + col + j) % 64 for j in range(1, 64)]] + [sibling])
 
     fs3 = fs.reshape(48, 64, 128)
     rows_of_conduct = [conduct.at[pl.ds(56, 8), :], conduct.at[pl.ds(0, 8), :]]
@@ -272,19 +272,24 @@
     for c in col_copies:
         c.wait_recv()
 
+    place_of = lax.broadcasted_iota(jnp.int32, (2, 8, 128), 0) * 8 + lax.broadcasted_iota(jnp.int32, (2, 8, 128), 1)
+
     def of_runs(ref, b):
-        return jnp.broadcast_to(ref[16 * b : 16 * b + 16, :], (16, 128)).reshape(2, 8, 128)
-
-    def lanes_of_runs(ref):
-        out = jnp.zeros((2, 8, 128), ref.dtype)
+        out = jnp.zeros((2, 8, 128), f32)
+        for i in range(16):
+            out = jnp.where(place_of == i, ref[16 * b + i].astype(f32), out)
+        return out
+
+    def lanes_of_runs(made):
+        out = jnp.zeros((2, 8, 128), f32)
         for b in range(3):
-            out = jnp.where(lane // 32 == b, of_runs(ref, b), out)
+            out = jnp.where(lane // 32 == b, made[b], out)
         return out
 
     for b in range(3):
         nl[b] = of_runs(nonlin, b)
         cnt[b] = of_runs(counts, b)
-    nl[3] = lanes_of_runs(nonlin)
+    nl[3] = lanes_of_runs(nl)
 
     u[3, 0:8] = jnp.zeros((8, 2, 8, 128), f32)
     u[3, 88:96] = jnp.zeros((8, 2, 8, 128), f32)
@@ -293,8 +298,8 @@
     left_ok = (jnp.zeros((2, 8, 128), jnp.int32) + col) > 0
     right_ok = (jnp.zeros((2, 8, 128), jnp.int32) + col) < 7
 
-    taken = jnp.where(from_left & jnp.logical_not(left_ok), 0, lanes_of_runs(counts))
-    cnt[3] = jnp.where(from_right & jnp.logical_not(right_ok), 0, taken)
+    taken = jnp.where(from_left & jnp.logical_not(left_ok), 0.0, lanes_of_runs(cnt))
+    cnt[3] = jnp.where(from_right & jnp.logical_not(right_ok), 0.0, taken)
 
     def unpack(g, carry):
         gl = xr[0, g].astype(f32).reshape(2, 8, 128)
@@ -337,7 +342,7 @@
         count = range(len(blocks))
         ahead_s = s + 1 if with_main else s
         coef = [nl[b] for b in blocks]
-        active = [jnp.where(cnt[b] > (s if b < 3 else ahead_s), 1.0, 0.0).astype(f32) for b in blocks]
+        active = [jnp.where(cnt[b] > (s if b < 3 else ahead_s).astype(f32), 1.0, 0.0) for b in blocks]
         begin = (9 + s) // 4
 
         def kappa(v, i, n, shifted=0):
@@ -407,7 +412,7 @@
             clear(b)
 
     pass_round(0, 0)
-    run_step(0, False)
+    run_step(jnp.int32(0), False)
 
     def one_step(s, carry):
         run_step(s, True)
@@ -484,7 +489,7 @@
 def reduce_kernel(
     part, loss_in, desc, code, w_in, bias, w_out,
     new_in, new_bias, new_out, loss_out,
-    rows, act, slope, grad, back, r1, l1, l2, got, send1, recv1, send2, recv2, lsend, lrecv, lsend2, xsend, xrecv,
+    code_wide, rows, act, slope, grad, back, r1, l1, l2, got, send1, recv1, send2, recv2, lsend, lrecv, lsend2, xsend, xrecv,
 ):
     core, row, col = (lax.axis_index(n) for n in ("run", "row", "col"))
     x, y, z = row % 4, col // 2, (col % 2) * 2 + row // 4
@@ -498,7 +503,6 @@
     offsets = list(range(1, 64))
     offsets.sort(key=lambda j: -sum(min(d, 4 - d) for d in (j % 4, j // 4 % 4, j // 16)))
     peers = [(core, *chip(j)) for j in offsets]
-    signal_all(peers + [sibling])
 
     def piece(p):
         return part.at[p // 16, pl.ds(pl.multiple_of(24 * (p % 16), 8), 24), :]
@@ -516,10 +520,12 @@
     for c in first:
         c.start()
 
+    code_wide[...] = code[...].astype(f32)
+
     def trunk(n, carry):
         at = pl.multiple_of(48 * n, 48)
         half = pl.multiple_of(48 * (n // 8), 48)
-        rows_n = (desc[pl.ds(half, 48), :].astype(f32) + code[n % 8]).astype(bf16)
+        rows_n = (desc[pl.ds(half, 48), :].astype(f32) + code_wide[pl.ds(n % 8, 1), :]).astype(bf16)
         pre = jnp.dot(rows_n, w_in[...], preferred_element_type=f32) + bias[...]
         value, pull = jax.vjp(jax.nn.gelu, pre)
         rows[pl.ds(at, 48), :] = rows_n
@@ -584,7 +590,7 @@
         rows[...], back[...].astype(bf16), tn, preferred_element_type=f32
     )
     cross_loss.wait_recv()
-    loss_out[...] = l2[0] + l2[1]
+    loss_out[...] = jnp.sum(l2[0] + l2[1], keepdims=True) * (1.0 / (768 * 512 * 1024))
 
     @pl.when(me > 0)
     def _():
@@ -606,75 +612,73 @@
     vmem = pl.BlockSpec(memory_space=pltpu.VMEM)
     hbm = pl.BlockSpec(memory_space=pl.ANY)
     dma = pltpu.SemaphoreType.DMA
-    final, part, loss = pl.pallas_call(
-        main_kernel,
+    first = [
+        pltpu.VMEM((4, 2, 8, 128), f32),
+        pltpu.VMEM((4, 2, 8, 128), f32),
+        pltpu.VMEM((384, 512), bf16),
+        pltpu.VMEM((3072, 128), f32),
+        pltpu.VMEM((80, 128), f32),
+        pltpu.VMEM((4, ROWS, 2, 8, 128), f32),
+        pltpu.VMEM((4, ROWS, 8, 128), f32),
+        pltpu.VMEM((2, 8, 3, 16, 128), bf16),
+        pltpu.VMEM((2, 8, 3, 16, 128), bf16),
+        pltpu.VMEM((2, GROUPS, 16, 128), bf16),
+        pltpu.VMEM((2, GROUPS, 16, 128), bf16),
+        pltpu.VMEM((3, 2, ROWS, 2, 8, 128), f32),
+        pltpu.VMEM((4, 8, 2, 8, 128), f32),
+        pltpu.VMEM((4, 8, 2, 8, 128), f32),
+        pltpu.VMEM((4, 20, 8, 48, 128), bf16),
+        pltpu.VMEM((8, 8, 512, 128), bf16),
+        pltpu.VMEM((4, 16, 512, 128), bf16),
+        pltpu.VMEM((2, 1024, 1024), bf16),
+        pltpu.VMEM((8, 256, 128), f32),
+        pltpu.VMEM((512, 512), f32),
+        pltpu.VMEM((2, 384, 256), f32),
+        dma((3,)), dma((2,)), dma((4,)), dma((4,)), dma((2,)), dma((2,)),
+        dma((8, 7)), dma((8, 7)), dma((8,)), dma((8,)), dma((8,)),
+    ]
+    second = [
+        pltpu.VMEM((8, 256), f32),
+        pltpu.VMEM((768, 256), bf16),
+        pltpu.VMEM((768, 512), bf16),
+        pltpu.VMEM((768, 512), f32),
+        pltpu.VMEM((768, 512), bf16),
+        pltpu.VMEM((768, 512), f32),
+        pltpu.VMEM((63, 24, 128), f32),
+        pltpu.VMEM((64, 8, 128), f32),
+        pltpu.VMEM((2, 8, 128), f32),
+        pltpu.VMEM((2, 64, 32, 128), bf16),
+        dma((63,)), dma((63,)), dma((63,)), dma((63,)), dma(()), dma((65,)), dma((63,)), dma((2,)), dma((2,)),
+    ]
+    part_and_loss = [pltpu.VMEM((4, 384, 128), f32), pltpu.VMEM((8, 128), f32)]
+
+    def whole_kernel(field, cond, nonlin, counts, desc, code, w_in, bias, w_out, dec, final, new_in, new_bias, new_out, total, part, loss, *rest):
+        main_kernel(field, cond, nonlin, counts, desc, code, w_in, bias, w_out, dec, final, part, loss, *rest[: len(first)])
+        reduce_kernel(
+            part, loss, desc, code, w_in, bias, w_out, new_in, new_bias, new_out, total, *rest[len(first) :]
+        )
+
+    final, new_w_in, new_bias, new_w_out, loss_sum = pl.pallas_call(
+        whole_kernel,
         name="solve_and_learn",
         out_shape=(
             jax.ShapeDtypeStruct((48, 64, 128), f32),
-            jax.ShapeDtypeStruct((4, 384, 128), f32),
-            jax.ShapeDtypeStruct((8, 128), f32),
+            jax.ShapeDtypeStruct((256, 512), f32),
+            jax.ShapeDtypeStruct((1, 512), f32),
+            jax.ShapeDtypeStruct((512, 512), f32),
+            jax.ShapeDtypeStruct((1, 1), f32),
         ),
-        in_specs=[hbm, hbm, vmem, vmem, vmem, vmem, vmem, vmem, vmem, hbm],
-        out_specs=(hbm, vmem, vmem),
-        scratch_shapes=[
-            pltpu.VMEM((4, 2, 8, 128), f32),
-            pltpu.VMEM((4, 2, 8, 128), jnp.int32),
-            pltpu.VMEM((384, 512), bf16),
-            pltpu.VMEM((3072, 128), f32),
-            pltpu.VMEM((80, 128), f32),
-            pltpu.VMEM((4, ROWS, 2, 8, 128), f32),
-            pltpu.VMEM((4, ROWS, 8, 128), f32),
-            pltpu.VMEM((2, 8, 3, 16, 128), bf16),
-            pltpu.VMEM((2, 8, 3, 16, 128), bf16),
-            pltpu.VMEM((2, GROUPS, 16, 128), bf16),
-            pltpu.VMEM((2, GROUPS, 16, 128), bf16),
-            pltpu.VMEM((3, 2, ROWS, 2, 8, 128), f32),
-            pltpu.VMEM((4, 8, 2, 8, 128), f32),
-            pltpu.VMEM((4, 8, 2, 8, 128), f32),
-            pltpu.VMEM((4, 20, 8, 48, 128), bf16),
-            pltpu.VMEM((8, 8, 512, 128), bf16),
-            pltpu.VMEM((4, 16, 512, 128), bf16),
-            pltpu.VMEM((2, 1024, 1024), bf16),
-            pltpu.VMEM((8, 256, 128), f32),
-            pltpu.VMEM((512, 512), f32),
-            pltpu.VMEM((2, 384, 256), f32),
-            dma((3,)), dma((2,)), dma((4,)), dma((4,)), dma((2,)), dma((2,)),
-            dma((8, 7)), dma((8, 7)), dma((8,)), dma((8,)), dma((8,)),
-        ],
+        in_specs=[hbm, hbm] + [pl.BlockSpec(memory_space=pltpu.SMEM)] * 2 + [vmem] * 5 + [hbm],
+        out_specs=(hbm, vmem, vmem, vmem, vmem),
+        scratch_shapes=part_and_loss + first + second,
         compiler_params=pltpu.CompilerParams(
             collective_id=0, has_side_effects=True, vmem_limit_bytes=VMEM_ALL - (1 << 16)
         ),
     )(
-        init_field, conduct, nonlin.reshape(48, 1), counts.reshape(48, 1),
+        init_field, conduct, nonlin, counts,
         descriptors, time_code, w_in, bias_row, w_out, decoder.reshape(4096, 1024),
     )
-
-    new_w_in, new_bias, new_w_out, loss_sum = pl.pallas_call(
-        reduce_kernel,
-        name="reduce_grad",
-        out_shape=(
-            jax.ShapeDtypeStruct((256, 512), f32),
-            jax.ShapeDtypeStruct((1, 512), f32),
-            jax.ShapeDtypeStruct((512, 512), f32),
-            jax.ShapeDtypeStruct((8, 128), f32),
-        ),
-        in_specs=[vmem] * 7,
-        out_specs=(vmem,) * 4,
-        scratch_shapes=[
-            pltpu.VMEM((768, 256), bf16),
-            pltpu.VMEM((768, 512), bf16),
-            pltpu.VMEM((768, 512), f32),
-            pltpu.VMEM((768, 512), bf16),
-            pltpu.VMEM((768, 512), f32),
-            pltpu.VMEM((63, 24, 128), f32),
-            pltpu.VMEM((64, 8, 128), f32),
-            pltpu.VMEM((2, 8, 128), f32),
-            pltpu.VMEM((2, 64, 32, 128), bf16),
-            dma((63,)), dma((63,)), dma((63,)), dma((63,)), dma(()), dma((65,)), dma((63,)), dma((2,)), dma((2,)),
-        ],
-        compiler_params=pltpu.CompilerParams(collective_id=1, has_side_effects=True),
-    )(part, loss, descriptors, time_code.astype(f32).reshape(8, 1, 256), w_in, bias_row, w_out)
-    mean_loss = jnp.sum(loss_sum) / (768 * 512 * 1024)
+    mean_loss = loss_sum.reshape(())
     return final, new_w_in, new_bias.reshape(512), new_w_out, mean_loss
 
 

time: 137 us -> 129 us (0.942)
  Pallas kernels: 126 us -> 121 us
  local copies, waits for them, and re-layouts: 7.61 us -> 5.2 us
    pallas_call x2 -> x1, Pallas kernels: 126 us -> 121 us  [per_device(): pl.pallas_call(whole_kernel, name='solve_and_learn', out_shape=(jax.Shape...]
    reshape x3 -> x0, local copies, waits for them, and re-layouts: 3.99 us -> none  [the longest x1 1.35 us: per_device(): nonlin.reshape(48, 1)]
    unnamed x12 -> x10, local copies, waits for them, and re-layouts: 3.63 us -> 5.2 us
where the time goes in v7:
time: 129 us
  Pallas kernels  121 us (94%)
  local copies, waits for them, and re-layouts  5.2 us (4%)
  between operations  2.47 us (2%)
    pallas_call x1, Pallas kernels, per_device(): pl.pallas_call(whole_kernel, name='solve_and_learn', out_shape=(jax.Shape...  121 us
    unnamed x10, local copies, waits for them, and re-layouts  5.2 us

profile of v7, /device:TPU:1, one launch (start us, length us, event | category | flops | bytes accessed | tf_op | source)
XLA Modules:
  0.0 128.9 jit_solution(4625174374298616547)
XLA Ops:
  0.6 121.2 %solve_and_learn.1 = (f32[48,64,128]{2,1,0:T(8,128)}, f32[256,512]{1,0:T(8,128)}, f32[1,512]{1,0:T(1,128)}, f32[512,512]{1,0:T(8,128)}, f32[1,1]{1,0:T(1,128)}) custom-call(f32[48,64,128]{2,1,0:T(8,128)} %field.1, f32[64,128]{1,0:T(8,128)} %cond.1, f32[48]{0:T(128)} %nonlin.1, s32[48]{0:T(128)} %counts.1, bf16[96,256]{1,0:T(8,128)(2,1)} %desc.1, ...), custom_call_target="tpu_custom_call" | custom-call | tf_op jit(solution)/shard_map/solve_and_learn/pallas_call | solution.py:661
  121.9 0.0 copy-start.1
  121.9 0.0 copy-start.2
  121.9 0.0 copy-start
  121.9 2.8 %copy.20 = f32[48,64,128]{2,1,0:T(8,128)} copy(f32[48,64,128]{2,1,0:T(8,128)} %get-tuple-element.20) | data formatting | bytes 3145728
  124.7 0.0 copy-done.1
  124.7 0.8 copy.21
  125.5 0.0 copy-done.2
  125.5 0.6 copy.22
  126.1 0.0 copy-done
  126.1 1.0 copy.23
Async XLA Ops:
  121.9 2.9 %copy-start.1 = (f32[256,512]{1,0:T(8,128)S(1)}, f32[256,512]{1,0:T(8,128)}, u32[]{:S(2)}) copy-start(f32[256,512]{1,0:T(8,128)} %get-tuple-element.21) | copy-start | bytes 1572868
  121.9 3.7 %copy-start.2 = (f32[1,512]{1,0:T(1,128)S(1)}, f32[1,512]{1,0:T(1,128)}, u32[]{:S(2)}) copy-start(f32[1,512]{1,0:T(1,128)} %get-tuple-element.12) | copy-start | bytes 6148
  121.9 4.2 %copy-start = (f32[512,512]{1,0:T(8,128)S(1)}, f32[512,512]{1,0:T(8,128)}, u32[]{:S(2)}) copy-start(f32[512,512]{1,0:T(8,128)} %get-tuple-element.23) | copy-start | bytes 3145732

commit v8 on v7

--- a/solution.py
+++ b/solution.py
@@ -28,7 +28,7 @@
 
 
 def main_kernel(
-    field, conduct, nonlin, counts, desc, code, w_in, bias, w_out, decoder,
+    on_half, field, conduct, nonlin, counts, desc, code, w_in, bias, w_out, decoder,
     final, part, loss,
     nl, cnt, hid, fs, cd, u, cb, rs, rr, xs, xr, fx, ks, ac, snap, tr, dl, raw, tf, gram, acc,
     loc_sem, raw_sem, row_send, row_recv, col_send, col_recv, dec_send, dec_recv, own_sem, fwd_send, fwd_recv,
@@ -444,6 +444,7 @@
 
     squares = lax.fori_loop(0, 64, square, jnp.zeros((8, 128), f32))
 
+    total = squares
     for hh in range(2):
         for kk in range(4):
             fwd_copy(hh, kk).wait_recv()
@@ -465,14 +466,14 @@
             got = lax.dot_general(lhs, rhs, nt, preferred_element_type=f32)
             acc[hh] = got if kk == 0 else acc[hh] + got
 
-    total = squares
-    for hh in range(2):
         for half in range(2):
             at = slice(256 * half + 128 * hh, 256 * half + 128 * hh + 128)
             a = part[2 * half + hh]
             c = acc[hh, :, 128 * half : 128 * half + 128]
             part[2 * half + hh] = a - c
             total = total + jnp.sum((hid[:, at].astype(f32) * (a - 2.0 * c)).reshape(48, 8, 128), axis=0)
+        on_half(hh)
+
     loss[...] = total
 
     out_copy.wait()
@@ -486,8 +487,31 @@
             fwd_copy(hh, kk).wait_send()
 
 
+def piece_copies(part, r1, send1, recv1):
+    core, row, col = (lax.axis_index(n) for n in ("run", "row", "col"))
+    x, y, z = row % 4, col // 2, (col % 2) * 2 + row // 4
+
+    def chip(j):
+        x1, y1, z1 = (x + j % 4) % 4, (y + j // 4 % 4) % 4, (z + j // 16) % 4
+        return (z1 % 2) * 4 + x1, y1 * 2 + z1 // 2
+
+    offsets = list(range(1, 64))
+    offsets.sort(key=lambda j: -sum(min(d, 4 - d) for d in (j % 4, j // 4 % 4, j // 16)))
+    peers = [(core, *chip(j)) for j in offsets]
+
+    def piece(p):
+        return part.at[p // 16, pl.ds(pl.multiple_of(24 * (p % 16), 8), 24), :]
+
+    first, halves = [], []
+    for n, j in enumerate(offsets):
+        r, c = chip(j)
+        halves.append((r * 8 + c) // 16 % 2)
+        first.append(remote(piece(r * 8 + c), r1.at[n], send1.at[n], recv1.at[n], peers[n]))
+    return first, peers, halves
+
+
 def reduce_kernel(
-    part, loss_in, desc, code, w_in, bias, w_out,
+    pieces, part, loss_in, desc, code, w_in, bias, w_out,
     new_in, new_bias, new_out, loss_out,
     code_wide, rows, act, slope, grad, back, r1, l1, l2, got, send1, recv1, send2, recv2, lsend, lrecv, lsend2, xsend, xrecv,
 ):
@@ -496,29 +520,14 @@
     sibling = (1 - core, row, col)
     me = row * 8 + col
 
-    def chip(j):
-        x1, y1, z1 = (x + j % 4) % 4, (y + j // 4 % 4) % 4, (z + j // 16) % 4
-        return (z1 % 2) * 4 + x1, y1 * 2 + z1 // 2
-
-    offsets = list(range(1, 64))
-    offsets.sort(key=lambda j: -sum(min(d, 4 - d) for d in (j % 4, j // 4 % 4, j // 16)))
-    peers = [(core, *chip(j)) for j in offsets]
-
-    def piece(p):
-        return part.at[p // 16, pl.ds(pl.multiple_of(24 * (p % 16), 8), 24), :]
-
-    first = []
-    for n, j in enumerate(offsets):
-        r, c = chip(j)
-        first.append(remote(piece(r * 8 + c), r1.at[n], send1.at[n], recv1.at[n], peers[n]))
+    first, peers = pieces
+
     to_zero = remote(loss_in, l1.at[me], lsend, lrecv.at[me], (core, 0, 0))
 
     @pl.when(me > 0)
     def _():
         to_zero.start()
 
-    for c in first:
-        c.start()
 
     code_wide[...] = code[...].astype(f32)
 
@@ -575,20 +584,26 @@
                 ).astype(bf16)
                 grad[pl.ds(pl.multiple_of(384 * own + 48 * q, 48), 48), 128 * t : 128 * t + 128] = pair
 
+    tn = (((0,), (0,)), ((), ()))
+
+    def gradients(own):
+        at = pl.ds(pl.multiple_of(384 * own, 384), 384)
+        g = grad[at, :]
+        to_out = lax.dot_general(act[at, :], g, tn, preferred_element_type=f32)
+        to_pre = (
+            lax.dot_general(g, w_out[...], (((1,), (1,)), ((), ())), preferred_element_type=f32) * slope[at, :]
+        )
+        to_in = lax.dot_general(rows[at, :], to_pre.astype(bf16), tn, preferred_element_type=f32)
+        return to_in, jnp.sum(to_pre, axis=0, keepdims=True), to_out
+
     place(core)
+    new_in[...], new_bias[...], new_out[...] = gradients(core)
     cross.wait_recv()
     place(1 - core)
-    tn = (((0,), (0,)), ((), ()))
-    new_out[...] = w_out[...].astype(f32) - RATE * lax.dot_general(
-        act[...], grad[...], tn, preferred_element_type=f32
-    )
-    back[...] = (
-        lax.dot_general(grad[...], w_out[...], (((1,), (1,)), ((), ())), preferred_element_type=f32) * slope[...]
-    )
-    new_bias[...] = bias[...] - RATE * jnp.sum(back[...], axis=0, keepdims=True)
-    new_in[...] = w_in[...].astype(f32) - RATE * lax.dot_general(
-        rows[...], back[...].astype(bf16), tn, preferred_element_type=f32
-    )
+    to_in, to_bias, to_out = gradients(1 - core)
+    new_out[...] = w_out[...].astype(f32) - RATE * (new_out[...] + to_out)
+    new_bias[...] = bias[...] - RATE * (new_bias[...] + to_bias)
+    new_in[...] = w_in[...].astype(f32) - RATE * (new_in[...] + to_in)
     cross_loss.wait_recv()
     loss_out[...] = jnp.sum(l2[0] + l2[1], keepdims=True) * (1.0 / (768 * 512 * 1024))
 
@@ -653,9 +668,19 @@
     part_and_loss = [pltpu.VMEM((4, 384, 128), f32), pltpu.VMEM((8, 128), f32)]
 
     def whole_kernel(field, cond, nonlin, counts, desc, code, w_in, bias, w_out, dec, final, new_in, new_bias, new_out, total, part, loss, *rest):
-        main_kernel(field, cond, nonlin, counts, desc, code, w_in, bias, w_out, dec, final, part, loss, *rest[: len(first)])
+        later = rest[len(first) :]
+        copies, peers, halves = piece_copies(part, later[6], later[10], later[11])
+
+        def on_half(hh):
+            for c, half in zip(copies, halves):
+
+                @pl.when(half == hh)
+                def _():
+                    c.start()
+
+        main_kernel(on_half, field, cond, nonlin, counts, desc, code, w_in, bias, w_out, dec, final, part, loss, *rest[: len(first)])
         reduce_kernel(
-            part, loss, desc, code, w_in, bias, w_out, new_in, new_bias, new_out, total, *rest[len(first) :]
+            (copies, peers), part, loss, desc, code, w_in, bias, w_out, new_in, new_bias, new_out, total, *later
         )
 
     final, new_w_in, new_bias, new_w_out, loss_sum = pl.pallas_call(

time: 129 us -> 129 us (level)
  no operation moved by 1% of the time
where the time goes in v8:
time: 129 us
  Pallas kernels  121 us (94%)
  local copies, waits for them, and re-layouts  5.2 us (4%)
  between operations  2.47 us (2%)
    pallas_call x1, Pallas kernels, per_device(): pl.pallas_call(whole_kernel, name='solve_and_learn', out_shape=(jax.Shape...  121 us
    unnamed x10, local copies, waits for them, and re-layouts  5.2 us

profile of v8, /device:TPU:1, one launch (start us, length us, event | category | flops | bytes accessed | tf_op | source)
XLA Modules:
  0.0 129.1 jit_solution(8560770536097385088)
XLA Ops:
  0.6 121.5 %solve_and_learn.1 = (f32[48,64,128]{2,1,0:T(8,128)}, f32[256,512]{1,0:T(8,128)}, f32[1,512]{1,0:T(1,128)}, f32[512,512]{1,0:T(8,128)}, f32[1,1]{1,0:T(1,128)}) custom-call(f32[48,64,128]{2,1,0:T(8,128)} %field.1, f32[64,128]{1,0:T(8,128)} %cond.1, f32[48]{0:T(128)} %nonlin.1, s32[48]{0:T(128)} %counts.1, bf16[96,256]{1,0:T(8,128)(2,1)} %desc.1, ...), custom_call_target="tpu_custom_call" | custom-call | tf_op jit(solution)/shard_map/solve_and_learn/pallas_call | solution.py:686
  122.1 0.0 copy-start.1
  122.1 0.0 copy-start.2
  122.1 0.0 copy-start
  122.1 2.8 %copy.20 = f32[48,64,128]{2,1,0:T(8,128)} copy(f32[48,64,128]{2,1,0:T(8,128)} %get-tuple-element.20) | data formatting | bytes 3145728
  125.0 0.0 copy-done.1
  125.0 0.8 copy.21
  125.8 0.0 copy-done.2
  125.8 0.6 copy.22
  126.4 0.0 copy-done
  126.4 1.0 copy.23
Async XLA Ops:
  122.1 2.9 %copy-start.1 = (f32[256,512]{1,0:T(8,128)S(1)}, f32[256,512]{1,0:T(8,128)}, u32[]{:S(2)}) copy-start(f32[256,512]{1,0:T(8,128)} %get-tuple-element.21) | copy-start | bytes 1572868
  122.1 3.7 %copy-start.2 = (f32[1,512]{1,0:T(1,128)S(1)}, f32[1,512]{1,0:T(1,128)}, u32[]{:S(2)}) copy-start(f32[1,512]{1,0:T(1,128)} %get-tuple-element.12) | copy-start | bytes 6148
  122.1 4.2 %copy-start = (f32[512,512]{1,0:T(8,128)S(1)}, f32[512,512]{1,0:T(8,128)}, u32[]{:S(2)}) copy-start(f32[512,512]{1,0:T(8,128)} %get-tuple-element.23) | copy-start | bytes 3145732

commit v9 on v7

--- a/solution.py
+++ b/solution.py
@@ -237,10 +237,10 @@
     raw_copy(mine + 1, 1).wait()
     turn(mine + 1, 1)
     raw_copy(other + 1, 1).start()
+    for rnd in range(1, 8):
+        send_round(rnd // 4, rnd % 4)
     raw_copy(other, 0).wait()
     turn(other, 0)
-    for rnd in range(1, 8):
-        send_round(rnd // 4, rnd % 4)
     raw_copy(other + 1, 1).wait()
     turn(other + 1, 1)
 

time: 129 us -> 133 us (1.031)
  Pallas kernels: 121 us -> 125 us
    pallas_call x1, Pallas kernels: 121 us -> 125 us  [per_device(): pl.pallas_call(whole_kernel, name='solve_and_learn', out_shape=(jax.Shape...]
where the time goes in v9:
time: 133 us
  Pallas kernels  125 us (94%)
  local copies, waits for them, and re-layouts  5.2 us (4%)
  between operations  2.47 us (2%)
    pallas_call x1, Pallas kernels, per_device(): pl.pallas_call(whole_kernel, name='solve_and_learn', out_shape=(jax.Shape...  125 us
    unnamed x10, local copies, waits for them, and re-layouts  5.2 us

profile of v9, /device:TPU:1, one launch (start us, length us, event | category | flops | bytes accessed | tf_op | source)
XLA Modules:
  0.0 132.9 jit_solution(1051619057223520017)
XLA Ops:
  0.6 125.3 %solve_and_learn.1 = (f32[48,64,128]{2,1,0:T(8,128)}, f32[256,512]{1,0:T(8,128)}, f32[1,512]{1,0:T(1,128)}, f32[512,512]{1,0:T(8,128)}, f32[1,1]{1,0:T(1,128)}) custom-call(f32[48,64,128]{2,1,0:T(8,128)} %field.1, f32[64,128]{1,0:T(8,128)} %cond.1, f32[48]{0:T(128)} %nonlin.1, s32[48]{0:T(128)} %counts.1, bf16[96,256]{1,0:T(8,128)(2,1)} %desc.1, ...), custom_call_target="tpu_custom_call" | custom-call | tf_op jit(solution)/shard_map/solve_and_learn/pallas_call | solution.py:661
  125.9 0.0 copy-start.1
  125.9 0.0 copy-start.2
  125.9 0.0 copy-start
  125.9 2.8 %copy.20 = f32[48,64,128]{2,1,0:T(8,128)} copy(f32[48,64,128]{2,1,0:T(8,128)} %get-tuple-element.20) | data formatting | bytes 3145728
  128.8 0.0 copy-done.1
  128.8 0.8 copy.21
  129.6 0.0 copy-done.2
  129.6 0.6 copy.22
  130.2 0.0 copy-done
  130.2 1.0 copy.23
Async XLA Ops:
  125.9 2.9 %copy-start.1 = (f32[256,512]{1,0:T(8,128)S(1)}, f32[256,512]{1,0:T(8,128)}, u32[]{:S(2)}) copy-start(f32[256,512]{1,0:T(8,128)} %get-tuple-element.21) | copy-start | bytes 1572868
  125.9 3.7 %copy-start.2 = (f32[1,512]{1,0:T(1,128)S(1)}, f32[1,512]{1,0:T(1,128)}, u32[]{:S(2)}) copy-start(f32[1,512]{1,0:T(1,128)} %get-tuple-element.12) | copy-start | bytes 6148
  125.9 4.2 %copy-start = (f32[512,512]{1,0:T(8,128)S(1)}, f32[512,512]{1,0:T(8,128)}, u32[]{:S(2)}) copy-start(f32[512,512]{1,0:T(8,128)} %get-tuple-element.23) | copy-start | bytes 3145732
